TPU v7x, 32 devices: a whole 2x2x4 slice. The times are simulated.
32 devices in a mesh: tmpl: 4 (over x, core), row: 4 (over z), col: 2 (over y).
Axes of the slice: x: 2, y: 2, z: 4, core: 2. Of those that a mesh axis runs over, the one named last changes fastest.
Arguments:
- templ_pair: bfloat16 [4, 256, 256, 64], P('tmpl', 'row', 'col'), may hold values from -10 to 10
- main_pair: bfloat16 [256, 256, 128], P('row', 'col'), may hold values from -8 to 8
- coverage: int32 [4, 2], replicated, may hold values from 0 to 1
- pair_mask: int32 [2, 2], replicated, may hold values from 0 to 1
- tri_gain: float32 [64], replicated, may hold values from 0.1 to 1.9
- w_project: bfloat16 [64, 256], replicated, may hold values from -1 to 1
- w_bias: bfloat16 [64, 4], replicated, may hold values from -0.75 to 0.75
- w_tri_out: bfloat16 [64, 64], replicated, may hold values from -0.75 to 0.75
- merge_gain: float32 [64], replicated, may hold values from 0.1 to 1.9
- w_merge_q: bfloat16 [128, 64], replicated, may hold values from -1 to 1
- w_merge_kv: bfloat16 [64, 128], replicated, may hold values from -1 to 1
- w_merge_out: bfloat16 [64, 128], replicated, may hold values from -0.75 to 0.75
Outputs:
- templ_out: bfloat16 [4, 256, 256, 64], P('tmpl', 'row', 'col')
- embedding: bfloat16 [256, 256, 128], P('row', 'col')
All inputs are finite; a program needn't handle non-finite values.
Results may differ from a plain program's by a relative error of at most 0.015.
Values may be sent and summed in bfloat16 or wider, within the bound.
No kernel may reach another device: no remote copies, remote signals or barrier semaphores. Data moves between devices by JAX's collectives and lax.ppermute only.
A program may use at most 64 MiB of HBM per device.

v0:
```python
import jax
import jax.numpy as jnp
from jax import lax
from jax.sharding import PartitionSpec as P

BLOCK = 128


MASK_SHIFT = 10000.0
EPSILON = 1e-05
NEG_START = -1e30


def combined_all(part, axis, combine):
    gathered = jax.tree.map(lambda a: lax.all_gather(a, axis), part)

    def take(source):
        return jax.tree.map(lambda a: lax.dynamic_index_in_dim(a, source, 0, False), gathered)

    return lax.fori_loop(
        1, lax.axis_size(axis), lambda source, state: combine(state, take(source)), take(0)
    )


def layer_norm(values, scale_gain):
    values = values.astype(jnp.float32)
    center = values - jnp.mean(values, axis=-1, keepdims=True)
    spread = jnp.mean(center * center, axis=-1, keepdims=True)
    return center * lax.rsqrt(spread + EPSILON) * scale_gain


def row_group(rows_dev, cols_dev):
    chosen = 1
    for candidate in range(1, rows_dev + 1):
        if rows_dev % candidate == 0 and candidate * cols_dev <= 2048:
            chosen = candidate
    return chosen


def on_device(
    templ_pair,
    main_pair,
    coverage,
    pair_mask,
    tri_gain,
    w_project,
    w_bias,
    w_tri_out,
    merge_gain,
    w_merge_q,
    w_merge_kv,
    w_merge_out,
):
    pair_tile = templ_pair[0]
    rows_dev, cols_dev, channels = pair_tile.shape
    hidden = w_tri_out.shape[0]
    head_count = w_bias.shape[1]
    head_dim = hidden // head_count
    score_scale = head_dim ** (-0.5)
    row_start = lax.axis_index("row") * rows_dev
    col_start = lax.axis_index("col") * cols_dev
    templ_index = lax.axis_index("tmpl")
    cover_tok = jnp.repeat(coverage, BLOCK, axis=1)
    own_cover = lax.dynamic_index_in_dim(cover_tok, templ_index, 0, keepdims=False)
    mask_full = jnp.repeat(jnp.repeat(pair_mask, BLOCK, axis=0), BLOCK, axis=1)
    mask_rows = lax.dynamic_slice_in_dim(mask_full, row_start, rows_dev, 0)
    cover_rows = lax.dynamic_slice_in_dim(own_cover, row_start, rows_dev, 0)
    normed = layer_norm(pair_tile, tri_gain).astype(jnp.bfloat16)
    flat_norm = normed.reshape(-1, channels)
    w_query_gate = jnp.concatenate([w_project[:, :hidden], w_project[:, 3 * hidden :]], axis=1)
    query_gate = jnp.dot(flat_norm, w_query_gate, preferred_element_type=jnp.float32).reshape(
        rows_dev, cols_dev, 2 * hidden
    )
    queries = (
        (query_gate[..., :hidden] * score_scale)
        .astype(jnp.bfloat16)
        .reshape(rows_dev, cols_dev, head_count, head_dim)
    )
    gate_values = jax.nn.sigmoid(query_gate[..., hidden:])
    bias_tile = jnp.dot(flat_norm, w_bias, preferred_element_type=jnp.float32).astype(jnp.bfloat16)
    bias_tile = jnp.transpose(bias_tile.reshape(rows_dev, cols_dev, head_count), (2, 0, 1))
    bias_column = lax.all_gather(bias_tile, "row", axis=1, tiled=True)
    bias_slab = lax.all_to_all(bias_column, "col", split_axis=1, concat_axis=2, tiled=True)
    bias_rows = jnp.transpose(bias_slab, (1, 0, 2)).astype(jnp.float32)
    key_shift = MASK_SHIFT * (
        (cover_rows[:, None] * own_cover[None, :] * mask_rows).astype(jnp.float32) - 1.0
    )
    w_key_value = w_project[:, hidden : 3 * hidden]
    group = row_group(rows_dev, cols_dev)
    splits = rows_dev // group

    def grouped(array):
        return array.reshape((splits, group) + array.shape[1:])

    start_state = (
        jnp.full((rows_dev, cols_dev, head_count), NEG_START, jnp.float32),
        jnp.zeros((rows_dev, cols_dev, head_count), jnp.float32),
        jnp.zeros((rows_dev, cols_dev, head_count, head_dim), jnp.float32),
    )
    norm_piece = lax.all_gather(normed, "col", axis=1, tiled=True)
    piece_width = norm_piece.shape[1]

    def one_group(group_args):
        query_part, norm_part, shift_part, maxima, totals, weighted = group_args
        key_value = jnp.dot(
            norm_part.reshape(-1, channels), w_key_value, preferred_element_type=jnp.float32
        ).astype(jnp.bfloat16)
        key_value = key_value.reshape(group, piece_width, 2 * hidden)
        key_part = key_value[..., :hidden].reshape(group, piece_width, head_count, head_dim)
        value_part = key_value[..., hidden:].reshape(group, piece_width, head_count, head_dim)
        scores = jnp.einsum(
            "ijhd,ikhd->ijhk", query_part, key_part, preferred_element_type=jnp.float32
        )
        scores = scores + bias_rows[None] + shift_part[:, None, None, :]
        highest = jnp.maximum(maxima, jnp.max(scores, axis=-1))
        rescale = jnp.exp(maxima - highest)
        weights = jnp.exp(scores - highest[..., None])
        totals = totals * rescale + jnp.sum(weights, axis=-1)
        summed = jnp.einsum(
            "ijhk,ikhd->ijhd",
            weights.astype(jnp.bfloat16),
            value_part,
            preferred_element_type=jnp.float32,
        )
        weighted = weighted * rescale[..., None] + summed
        return (highest, totals, weighted)

    outcome = lax.map(
        one_group,
        (
            grouped(queries),
            grouped(norm_piece),
            grouped(key_shift),
            grouped(start_state[0]),
            grouped(start_state[1]),
            grouped(start_state[2]),
        ),
    )
    result = tuple((member.reshape((rows_dev,) + member.shape[2:]) for member in outcome))
    attended = result[2] / result[1][..., None]
    gated = (attended.reshape(rows_dev, cols_dev, hidden) * gate_values).astype(jnp.bfloat16)
    projected = jnp.dot(
        gated.reshape(-1, hidden), w_tri_out, preferred_element_type=jnp.float32
    ).reshape(rows_dev, cols_dev, channels)
    new_pair = (pair_tile.astype(jnp.float32) + projected).astype(jnp.bfloat16)
    merge_norm = layer_norm(new_pair, merge_gain).astype(jnp.bfloat16)
    merge_kv = jnp.dot(
        merge_norm.reshape(-1, channels), w_merge_kv, preferred_element_type=jnp.float32
    ).astype(jnp.bfloat16)
    merge_kv = merge_kv.reshape(rows_dev, cols_dev, 2 * hidden)
    pair_ch = main_pair.shape[-1]
    main_query = (
        jnp.dot(main_pair.reshape(-1, pair_ch), w_merge_q, preferred_element_type=jnp.float32)
        * score_scale
    )
    main_query = main_query.reshape(rows_dev, cols_dev, head_count, head_dim)
    mask_tile = lax.dynamic_slice_in_dim(mask_rows, col_start, cols_dev, 1)
    own_cols = lax.dynamic_slice_in_dim(own_cover, col_start, cols_dev, 0)
    own_valid = cover_rows[:, None] * own_cols[None, :] * mask_tile
    shift_bias = MASK_SHIFT * (own_valid.astype(jnp.float32) - 1.0)
    keys_own = (
        merge_kv[..., :hidden].astype(jnp.float32).reshape(rows_dev, cols_dev, head_count, head_dim)
    )
    values_own = (
        merge_kv[..., hidden:].astype(jnp.float32).reshape(rows_dev, cols_dev, head_count, head_dim)
    )
    scores = jnp.sum(main_query * keys_own, axis=-1) + shift_bias[..., None]

    def combine(earlier, later):
        highest = jnp.maximum(earlier[0], later[0])
        early_scale = jnp.exp(earlier[0] - highest)
        late_scale = jnp.exp(later[0] - highest)
        return (
            highest,
            earlier[1] * early_scale + later[1] * late_scale,
            earlier[2] * early_scale[..., None] + later[2] * late_scale[..., None],
        )

    merged_state = combined_all((scores, jnp.ones_like(scores), values_own), "tmpl", combine)
    merged = merged_state[2] / merged_state[1][..., None]
    merged = merged.reshape(-1, hidden).astype(jnp.bfloat16)
    embedding = jnp.dot(merged, w_merge_out, preferred_element_type=jnp.float32).astype(
        jnp.bfloat16
    )
    return (new_pair[None], embedding.reshape(rows_dev, cols_dev, pair_ch))


def solution(mesh):
    in_specs = (
        P("tmpl", "row", "col", None),
        P("row", "col", None),
        P(),
        P(),
        P(),
        P(),
        P(),
        P(),
        P(),
        P(),
        P(),
        P(),
    )
    out_specs = (P("tmpl", "row", "col", None), P("row", "col", None))
    return jax.shard_map(
        on_device, mesh=mesh, in_specs=in_specs, out_specs=out_specs, check_vma=False
    )
```

profile of v0, /device:TPU:0, one launch (start us, length us, event | category | flops | bytes accessed | tf_op | source)
XLA Modules:
  0.0 242.9 jit_solution(12087617554621203379)
XLA Ops:
  7.2 1.6 convert_reduce_fusion.1
  8.9 1.7 multiply_reduce_fusion
  10.6 1.5 multiply_convert_fusion
  12.8 1.2 fusion.42
  14.0 16.3 %all_gather.15 = bf16[4,256,128]{2,0,1:T(4,128)(2,1)} all-gather(bf16[4,64,128]{2,0,1:T(4,128)(2,1)S(1)} %fusion.42), channel_id=1, replica_groups=mesh['tmpl'=4,'row'=4,'col'=2] {'row'}, dimensions={1}, use_global_device_ids=true | all-gather | bytes 327680 | tf_op jit(solution)/shard_map/all_gather | solution.py:82
  30.4 3.4 %all-to-all-start = ((bf16[4,256,128]{2,0,1:T(4,128)(2,1)}), bf16[4,256,128]{2,0,1:T(4,128)(2,1)S(1)}, u32[]{:S(2)}, u32[]{:S(2)}) async-start(bf16[4,256,128]{2,0,1:T(4,128)(2,1)} %all_gather.15), calls=%async_computation | async-start | bytes 524288 | tf_op jit(solution)/shard_map/all_to_all | solution.py:83
  36.2 2.0 copy-done.5
  38.2 1.3 fusion.37
  39.5 0.9 add_multiply_fusion
  40.4 1.9 all-to-all-done
  42.3 1.1 copy.84
  43.4 7.5 %all-gather.3.cloned.1.call-done = bf16[64,256,64]{1,2,0:T(8,128)(2,1)} async-done(((bf16[64,128,64]{1,2,0:T(8,128)(2,1)}), bf16[64,256,64]{1,2,0:T(8,128)(2,1)}) %all-gather.3.cloned.1.call-update) | async-done | bytes 2097168 | tf_op jit(solution)/shard_map/all_gather | solution.py:100
  50.9 90.5 %while.32 = (s32[]{:T(128)}, f32[4,16,128,4]{2,3,1,0:T(4,128)}, f32[4,16,128,4,16]{2,4,3,1,0:T(8,128)}, bf16[4,16,256,64]{2,3,1,0:T(8,128)(2,1)}, bf16[64,128]{1...) while((s32[]{:T(128)}, f32[4,16,128,4]{2,3,1,0:T(4,128)}, ...), condition=%wide.region_5.6_spmd, body=%wide.region_2.5_spmd.sunk | while | flops 225091584 | bytes 72548528 | solution.py:128
  50.9 1.9 constant_dynamic-slice_fusion.5
  52.8 1.5 copy.135
  54.7 1.4 fusion.92
  56.1 2.3 copy.136
  58.4 3.8 %fusion.93 = (f32[16,128,4]{1,2,0:T(4,128)S(1)}, f32[16,4,256,128]{3,2,1,0:T(8,128)S(1)}) fusion(f32[16,256]{1,0:T(8,128)S(1)} %dynamic-slice_bitcast_fusion.4, f32[128,4,256]{0,2,1:T(8,128)} %get-tuple-element.486, bf16[16,256,4,16]{1,3,2,0:T(8,128)(2,1)} %bitcast.211, bf16[4,16,128,4,16]{2,4,3,1,0:T(8,128)(2,1)} %get-tuple-element.485, s32[]{:T(128)S(6)} %copy.143), kind=kOutput, calls=%fused_computation.5.clone.1 | convolution fusion | flops 73392128 | bytes 9748484 | tf_op jit(solution)/shard_map/while/body/eval_jaxpr/ijhd,ikhd->ijhk/dot_general | solution.py:111
  62.3 2.5 %fusion.94 = f32[16,128,4]{1,2,0:T(4,128)S(1)} fusion(f32[16,4,256,128]{3,2,1,0:T(8,128)S(1)} %get-tuple-element.447, f32[16,128,4]{1,2,0:T(4,128)S(1)} %get-tuple-element.449, f32[16,256]{1,0:T(8,128)S(1)} %dynamic-slice_bitcast_fusion.4, f32[128,4,256]{0,2,1:T(8,128)S(1)} %copy-done.2), kind=kLoop, calls=%fused_computation.4.clone.1 | loop fusion | flops 8380416 | bytes 8994816 | tf_op jit(solution)/shard_map/while/body/eval_jaxpr/reduce_sum | solution.py:118
  66.1 1.1 copy.137
  67.3 6.2 %fusion.95 = f32[4,16,128,4,16]{2,4,3,1,0:T(8,128)} fusion(f32[4,16,128,4,16]{2,4,3,1,0:T(8,128)} %get-tuple-element.473, s32[]{:T(128)S(6)} %copy.143, bf16[16,256,4,16]{1,3,2,0:T(8,128)(2,1)} %bitcast.212, f32[16,4,256,128]{3,2,1,0:T(8,128)} %copy-done.1, f32[16,128,4]{1,2,0:T(4,128)S(1)} %get-tuple-element.449, ...), kind=kOutput, calls=%fused_computation.11.clone.1 | convolution fusion | flops 75628544 | bytes 10043396 | tf_op jit(solution)/shard_map/while/body/eval_jaxpr/ijhk,ikhd->ijhd/dot_general | solution.py:119
  73.5 1.9 constant_dynamic-slice_fusion.5
  75.4 1.5 copy.135
  77.3 1.4 fusion.92
  78.7 2.3 copy.136
  81.1 3.8 %fusion.93 = (f32[16,128,4]{1,2,0:T(4,128)S(1)}, f32[16,4,256,128]{3,2,1,0:T(8,128)S(1)}) fusion(f32[16,256]{1,0:T(8,128)S(1)} %dynamic-slice_bitcast_fusion.4, f32[128,4,256]{0,2,1:T(8,128)} %get-tuple-element.486, bf16[16,256,4,16]{1,3,2,0:T(8,128)(2,1)} %bitcast.211, bf16[4,16,128,4,16]{2,4,3,1,0:T(8,128)(2,1)} %get-tuple-element.485, s32[]{:T(128)S(6)} %copy.143), kind=kOutput, calls=%fused_computation.5.clone.1 | convolution fusion | flops 73392128 | bytes 9748484 | tf_op jit(solution)/shard_map/while/body/eval_jaxpr/ijhd,ikhd->ijhk/dot_general | solution.py:111
  85.0 2.5 %fusion.94 = f32[16,128,4]{1,2,0:T(4,128)S(1)} fusion(f32[16,4,256,128]{3,2,1,0:T(8,128)S(1)} %get-tuple-element.447, f32[16,128,4]{1,2,0:T(4,128)S(1)} %get-tuple-element.449, f32[16,256]{1,0:T(8,128)S(1)} %dynamic-slice_bitcast_fusion.4, f32[128,4,256]{0,2,1:T(8,128)S(1)} %copy-done.2), kind=kLoop, calls=%fused_computation.4.clone.1 | loop fusion | flops 8380416 | bytes 8994816 | tf_op jit(solution)/shard_map/while/body/eval_jaxpr/reduce_sum | solution.py:118
  88.8 1.1 copy.137
  89.9 6.2 %fusion.95 = f32[4,16,128,4,16]{2,4,3,1,0:T(8,128)} fusion(f32[4,16,128,4,16]{2,4,3,1,0:T(8,128)} %get-tuple-element.473, s32[]{:T(128)S(6)} %copy.143, bf16[16,256,4,16]{1,3,2,0:T(8,128)(2,1)} %bitcast.212, f32[16,4,256,128]{3,2,1,0:T(8,128)} %copy-done.1, f32[16,128,4]{1,2,0:T(4,128)S(1)} %get-tuple-element.449, ...), kind=kOutput, calls=%fused_computation.11.clone.1 | convolution fusion | flops 75628544 | bytes 10043396 | tf_op jit(solution)/shard_map/while/body/eval_jaxpr/ijhk,ikhd->ijhd/dot_general | solution.py:119
  96.1 1.9 constant_dynamic-slice_fusion.5
  98.0 1.5 copy.135
  99.9 1.4 fusion.92
  101.3 2.3 copy.136
  103.7 3.8 %fusion.93 = (f32[16,128,4]{1,2,0:T(4,128)S(1)}, f32[16,4,256,128]{3,2,1,0:T(8,128)S(1)}) fusion(f32[16,256]{1,0:T(8,128)S(1)} %dynamic-slice_bitcast_fusion.4, f32[128,4,256]{0,2,1:T(8,128)} %get-tuple-element.486, bf16[16,256,4,16]{1,3,2,0:T(8,128)(2,1)} %bitcast.211, bf16[4,16,128,4,16]{2,4,3,1,0:T(8,128)(2,1)} %get-tuple-element.485, s32[]{:T(128)S(6)} %copy.143), kind=kOutput, calls=%fused_computation.5.clone.1 | convolution fusion | flops 73392128 | bytes 9748484 | tf_op jit(solution)/shard_map/while/body/eval_jaxpr/ijhd,ikhd->ijhk/dot_general | solution.py:111
  107.6 2.5 %fusion.94 = f32[16,128,4]{1,2,0:T(4,128)S(1)} fusion(f32[16,4,256,128]{3,2,1,0:T(8,128)S(1)} %get-tuple-element.447, f32[16,128,4]{1,2,0:T(4,128)S(1)} %get-tuple-element.449, f32[16,256]{1,0:T(8,128)S(1)} %dynamic-slice_bitcast_fusion.4, f32[128,4,256]{0,2,1:T(8,128)S(1)} %copy-done.2), kind=kLoop, calls=%fused_computation.4.clone.1 | loop fusion | flops 8380416 | bytes 8994816 | tf_op jit(solution)/shard_map/while/body/eval_jaxpr/reduce_sum | solution.py:118
  111.4 1.1 copy.137
  112.5 6.2 %fusion.95 = f32[4,16,128,4,16]{2,4,3,1,0:T(8,128)} fusion(f32[4,16,128,4,16]{2,4,3,1,0:T(8,128)} %get-tuple-element.473, s32[]{:T(128)S(6)} %copy.143, bf16[16,256,4,16]{1,3,2,0:T(8,128)(2,1)} %bitcast.212, f32[16,4,256,128]{3,2,1,0:T(8,128)} %copy-done.1, f32[16,128,4]{1,2,0:T(4,128)S(1)} %get-tuple-element.449, ...), kind=kOutput, calls=%fused_computation.11.clone.1 | convolution fusion | flops 75628544 | bytes 10043396 | tf_op jit(solution)/shard_map/while/body/eval_jaxpr/ijhk,ikhd->ijhd/dot_general | solution.py:119
  118.7 1.9 constant_dynamic-slice_fusion.5
  120.6 1.5 copy.135
  122.6 1.4 fusion.92
  124.0 2.3 copy.136
  126.3 3.8 %fusion.93 = (f32[16,128,4]{1,2,0:T(4,128)S(1)}, f32[16,4,256,128]{3,2,1,0:T(8,128)S(1)}) fusion(f32[16,256]{1,0:T(8,128)S(1)} %dynamic-slice_bitcast_fusion.4, f32[128,4,256]{0,2,1:T(8,128)} %get-tuple-element.486, bf16[16,256,4,16]{1,3,2,0:T(8,128)(2,1)} %bitcast.211, bf16[4,16,128,4,16]{2,4,3,1,0:T(8,128)(2,1)} %get-tuple-element.485, s32[]{:T(128)S(6)} %copy.143), kind=kOutput, calls=%fused_computation.5.clone.1 | convolution fusion | flops 73392128 | bytes 9748484 | tf_op jit(solution)/shard_map/while/body/eval_jaxpr/ijhd,ikhd->ijhk/dot_general | solution.py:111
  130.2 2.5 %fusion.94 = f32[16,128,4]{1,2,0:T(4,128)S(1)} fusion(f32[16,4,256,128]{3,2,1,0:T(8,128)S(1)} %get-tuple-element.447, f32[16,128,4]{1,2,0:T(4,128)S(1)} %get-tuple-element.449, f32[16,256]{1,0:T(8,128)S(1)} %dynamic-slice_bitcast_fusion.4, f32[128,4,256]{0,2,1:T(8,128)S(1)} %copy-done.2), kind=kLoop, calls=%fused_computation.4.clone.1 | loop fusion | flops 8380416 | bytes 8994816 | tf_op jit(solution)/shard_map/while/body/eval_jaxpr/reduce_sum | solution.py:118
  134.0 1.1 copy.137
  135.1 6.2 %fusion.95 = f32[4,16,128,4,16]{2,4,3,1,0:T(8,128)} fusion(f32[4,16,128,4,16]{2,4,3,1,0:T(8,128)} %get-tuple-element.473, s32[]{:T(128)S(6)} %copy.143, bf16[16,256,4,16]{1,3,2,0:T(8,128)(2,1)} %bitcast.212, f32[16,4,256,128]{3,2,1,0:T(8,128)} %copy-done.1, f32[16,128,4]{1,2,0:T(4,128)S(1)} %get-tuple-element.449, ...), kind=kOutput, calls=%fused_computation.11.clone.1 | convolution fusion | flops 75628544 | bytes 10043396 | tf_op jit(solution)/shard_map/while/body/eval_jaxpr/ijhk,ikhd->ijhd/dot_general | solution.py:119
  141.4 3.0 %fusion.40 = bf16[64,128,64]{1,2,0:T(8,128)(2,1)S(1)} fusion(f32[64,128,128]{1,2,0:T(8,128)} %copy-done.5, f32[64,128,64]{1,2,0:T(8,128)} %bitcast.222, f32[64,128,4]{1,2,0:T(4,128)} %bitcast.229), kind=kLoop, calls=%fused_computation.62 | loop fusion | flops 3145728 | bytes 5373952 | tf_op jit(solution)/shard_map/convert_element_type | solution.py:141
  145.5 0.8 convolution_convert_fusion.2
  146.4 3.2 %fusion.61 = (bf16[64,128,64]{2,1,0:T(8,128)(2,1)}, bf16[64,128,64]{2,1,0:T(8,128)(2,1)}) fusion(bf16[64,128,128]{2,1,0:T(8,128)(2,1)S(1)} %bitcast.214), kind=kLoop, calls=%fused_computation.99 | loop fusion | bytes 4194304 | tf_op jit(solution)/shard_map/slice | solution.py:165
  149.5 2.0 copy.101
  151.6 1.6 convert.9
  154.0 1.7 copy.106
  155.8 1.0 add_multiply_fusion.1
  156.8 2.2 copy.100
  159.3 1.6 copy-done.7
  160.9 1.2 fusion.39
  162.1 10.4 %all_gather.16 = f32[4,64,128,4]{2,1,3,0:T(8,128)S(1)} all-gather(f32[1,64,128,4]{2,1,3,0:T(8,128)S(1)} %bitcast_add_fusion.2), channel_id=1, replica_groups=mesh['tmpl'=4,'row'=4,'col'=2] {'tmpl'}, dimensions={0}, use_global_device_ids=true | all-gather | bytes 655360 | tf_op jit(solution)/shard_map/all_gather | solution.py:15
  172.6 41.8 %all-gather.5.cloned.1.call-done = f32[4,64,128,4,16]{2,4,3,1,0:T(8,128)} async-done(((f32[1,64,128,4,16]{2,4,3,1,0:T(8,128)}), f32[4,64,128,4,16]{2,4,3,1,0:T(8,128)}) %all-gather.5.cloned.1.call-update) | async-done | bytes 8388624 | tf_op jit(solution)/shard_map/all_gather | solution.py:15
  214.4 3.2 %slice_bitcast_fusion = f32[64,128,4,16]{1,3,2,0:T(8,128)} fusion(f32[4,64,128,4,16]{2,4,3,1,0:T(8,128)} %all-gather.5.cloned.1.call-done), kind=kLoop, calls=%fused_computation.45 | loop fusion | bytes 4194304 | tf_op jit(solution)/shard_map/jit(dynamic_index_in_dim)/squeeze | solution.py:18
  217.6 13.6 %while.33 = (s32[]{:T(128)}, f32[64,128,4]{1,2,0:T(4,128)S(1)}, f32[64,128,4]{1,2,0:T(4,128)S(1)}, f32[64,128,4,16]{1,3,2,0:T(8,128)}, f32[4,64,128,4]{2,1,3,0:T...) while((s32[]{:T(128)}, f32[64,128,4]{1,2,0:T(4,128)S(1)}, ...), condition=%wide.region_10.11_spmd.clone, body=%wide.region_9.10_spmd.clone.sunk | while | flops 1769478 | bytes 7733401 | solution.py:20
  217.8 4.3 %fusion.97 = f32[64,128,4,16]{1,3,2,0:T(8,128)} fusion(f32[4,64,128,4,16]{2,4,3,1,0:T(8,128)} %get-tuple-element.512, s32[]{:T(128)S(6)} %select_n.43, f32[64,128,4,16]{1,3,2,0:T(8,128)} %get-tuple-element.501, f32[64,128,4]{1,2,0:T(4,128)S(1)} %get-tuple-element.460, f32[64,128,4]{1,2,0:T(4,128)S(1)} %get-tuple-element.461), kind=kLoop, calls=%fused_computation.22.clone.1 | loop fusion | flops 1572864 | bytes 6553604 | tf_op jit(solution)/shard_map/while/body/eval_jaxpr/add | solution.py:176
  222.3 4.3 %fusion.97 = f32[64,128,4,16]{1,3,2,0:T(8,128)} fusion(f32[4,64,128,4,16]{2,4,3,1,0:T(8,128)} %get-tuple-element.512, s32[]{:T(128)S(6)} %select_n.43, f32[64,128,4,16]{1,3,2,0:T(8,128)} %get-tuple-element.501, f32[64,128,4]{1,2,0:T(4,128)S(1)} %get-tuple-element.460, f32[64,128,4]{1,2,0:T(4,128)S(1)} %get-tuple-element.461), kind=kLoop, calls=%fused_computation.22.clone.1 | loop fusion | flops 1572864 | bytes 6553604 | tf_op jit(solution)/shard_map/while/body/eval_jaxpr/add | solution.py:176
  226.8 4.3 %fusion.97 = f32[64,128,4,16]{1,3,2,0:T(8,128)} fusion(f32[4,64,128,4,16]{2,4,3,1,0:T(8,128)} %get-tuple-element.512, s32[]{:T(128)S(6)} %select_n.43, f32[64,128,4,16]{1,3,2,0:T(8,128)} %get-tuple-element.501, f32[64,128,4]{1,2,0:T(4,128)S(1)} %get-tuple-element.460, f32[64,128,4]{1,2,0:T(4,128)S(1)} %get-tuple-element.461), kind=kLoop, calls=%fused_computation.22.clone.1 | loop fusion | flops 1572864 | bytes 6553604 | tf_op jit(solution)/shard_map/while/body/eval_jaxpr/add | solution.py:176
  231.1 1.9 divide_convert_fusion
  233.8 2.3 convolution_convert_fusion.1
  (103 shorter events, 13.8 us)
Async XLA Ops:
  7.2 146.0 %copy-start = (bf16[64,128,128]{2,1,0:T(8,128)(2,1)S(1)}, bf16[64,128,128]{2,1,0:T(8,128)(2,1)}, u32[]{:S(2)}) copy-start(bf16[64,128,128]{2,1,0:T(8,128)(2,1)} %param.17) | copy-start | bytes 6291460
  7.2 3.4 %copy-start.3 = (bf16[1,64,128,64]{2,3,1,0:T(8,128)(2,1)S(1)}, bf16[1,64,128,64]{2,3,1,0:T(8,128)(2,1)}, u32[]{:S(2)}) copy-start(bf16[1,64,128,64]{2,3,1,0:T(8,128)(2,1)} %param.16) | copy-start | bytes 3145732
  7.2 3.4 %copy-start.15 = (f32[64]{0:T(128)S(1)}, f32[64]{0:T(128)}, u32[]{:S(2)}) copy-start(f32[64]{0:T(128)} %param.20) | copy-start | bytes 772
  7.2 43.7 %all-gather.3.cloned.1.call-start = ((), (), s32[]{:S(2)}) async-start(), calls=%async_computation.1 | async-start | bytes 3145728 | tf_op jit(solution)/shard_map/all_gather | solution.py:100
  12.1 0.7 copy-start.17
  12.7 21.2 %copy-start.9 = (bf16[64,256]{1,0:T(8,128)(2,1)S(1)}, bf16[64,256]{1,0:T(8,128)(2,1)}, u32[]{:S(2)}) copy-start(bf16[64,256]{1,0:T(8,128)(2,1)} %param.21) | copy-start | bytes 98308
  12.8 21.2 %copy-start.13 = (s32[2,2]{1,0:T(2,128)S(1)}, s32[2,2]{1,0:T(2,128)}, u32[]{:S(2)}) copy-start(s32[2,2]{1,0:T(2,128)} %param.19) | copy-start | bytes 52
  12.8 22.3 %copy-start.14 = (s32[4,2]{0,1:T(2,128)S(1)}, s32[4,2]{0,1:T(2,128)}, u32[]{:S(2)}) copy-start(s32[4,2]{0,1:T(2,128)} %param.18) | copy-start | bytes 100
  12.8 22.6 %copy-start.6 = (bf16[64,128,64]{1,2,0:T(8,128)(2,1)S(1)}, bf16[64,128,64]{1,2,0:T(8,128)(2,1)}, u32[]{:S(2)}) copy-start(bf16[64,128,64]{1,2,0:T(8,128)(2,1)} %multiply_convert_fusion) | copy-start | bytes 3145732
  30.4 11.9 %all-to-all-start = ((bf16[4,256,128]{2,0,1:T(4,128)(2,1)}), bf16[4,256,128]{2,0,1:T(4,128)(2,1)S(1)}, u32[]{:S(2)}, u32[]{:S(2)}) async-start(bf16[4,256,128]{2,0,1:T(4,128)(2,1)} %all_gather.15), calls=%async_computation | async-start | bytes 524288 | tf_op jit(solution)/shard_map/all_to_all | solution.py:83
  33.8 180.6 %all-gather.5.cloned.1.call-start = ((), (), s32[]{:S(2)}) async-start(), calls=%async_computation.2 | async-start | bytes 10485760 | tf_op jit(solution)/shard_map/all_gather | solution.py:15
  36.2 2.0 copy-start.5
  58.4 3.9 %copy-start.2 = (f32[128,4,256]{0,2,1:T(8,128)S(1)}, f32[128,4,256]{0,2,1:T(8,128)}, u32[]{:S(2)}) copy-start(f32[128,4,256]{0,2,1:T(8,128)} %get-tuple-element.486) | copy-start | bytes 1572868 | tf_op jit(solution)/shard_map/while
  62.3 3.2 %copy-start.1 = (f32[16,4,256,128]{3,2,1,0:T(8,128)}, f32[16,4,256,128]{3,2,1,0:T(8,128)S(1)}, u32[]{:S(2)}) copy-start(f32[16,4,256,128]{3,2,1,0:T(8,128)S(1)} %get-tuple-element.447) | copy-start | bytes 25165828 | tf_op jit(solution)/shard_map/while
  81.1 3.9 %copy-start.2 = (f32[128,4,256]{0,2,1:T(8,128)S(1)}, f32[128,4,256]{0,2,1:T(8,128)}, u32[]{:S(2)}) copy-start(f32[128,4,256]{0,2,1:T(8,128)} %get-tuple-element.486) | copy-start | bytes 1572868 | tf_op jit(solution)/shard_map/while
  84.9 3.2 %copy-start.1 = (f32[16,4,256,128]{3,2,1,0:T(8,128)}, f32[16,4,256,128]{3,2,1,0:T(8,128)S(1)}, u32[]{:S(2)}) copy-start(f32[16,4,256,128]{3,2,1,0:T(8,128)S(1)} %get-tuple-element.447) | copy-start | bytes 25165828 | tf_op jit(solution)/shard_map/while
  103.7 3.9 %copy-start.2 = (f32[128,4,256]{0,2,1:T(8,128)S(1)}, f32[128,4,256]{0,2,1:T(8,128)}, u32[]{:S(2)}) copy-start(f32[128,4,256]{0,2,1:T(8,128)} %get-tuple-element.486) | copy-start | bytes 1572868 | tf_op jit(solution)/shard_map/while
  107.5 3.2 %copy-start.1 = (f32[16,4,256,128]{3,2,1,0:T(8,128)}, f32[16,4,256,128]{3,2,1,0:T(8,128)S(1)}, u32[]{:S(2)}) copy-start(f32[16,4,256,128]{3,2,1,0:T(8,128)S(1)} %get-tuple-element.447) | copy-start | bytes 25165828 | tf_op jit(solution)/shard_map/while
  126.3 3.9 %copy-start.2 = (f32[128,4,256]{0,2,1:T(8,128)S(1)}, f32[128,4,256]{0,2,1:T(8,128)}, u32[]{:S(2)}) copy-start(f32[128,4,256]{0,2,1:T(8,128)} %get-tuple-element.486) | copy-start | bytes 1572868 | tf_op jit(solution)/shard_map/while
  130.1 3.2 %copy-start.1 = (f32[16,4,256,128]{3,2,1,0:T(8,128)}, f32[16,4,256,128]{3,2,1,0:T(8,128)S(1)}, u32[]{:S(2)}) copy-start(f32[16,4,256,128]{3,2,1,0:T(8,128)S(1)} %get-tuple-element.447) | copy-start | bytes 25165828 | tf_op jit(solution)/shard_map/while
  141.4 3.0 %copy-start.4 = (bf16[1,64,128,64]{2,3,1,0:T(8,128)(2,1)S(1)}, bf16[1,64,128,64]{2,3,1,0:T(8,128)(2,1)}, u32[]{:S(2)}) copy-start(bf16[1,64,128,64]{2,3,1,0:T(8,128)(2,1)} %param.16) | copy-start | bytes 3145732
  141.4 3.0 %copy-start.10 = (bf16[64,64]{1,0:T(8,128)(2,1)S(1)}, bf16[64,64]{1,0:T(8,128)(2,1)}, u32[]{:S(2)}) copy-start(bf16[64,64]{1,0:T(8,128)(2,1)} %param.23) | copy-start | bytes 24580
  144.4 1.1 copy-start.16
  144.4 1.1 copy-start.18
  145.0 1.4 copy-start.8
  151.5 1.7 copy-start.11
  159.0 1.9 copy-start.7
  231.1 2.6 %copy-start.12 = (bf16[64,128]{1,0:T(8,128)(2,1)S(1)}, bf16[64,128]{1,0:T(8,128)(2,1)}, u32[]{:S(2)}) copy-start(bf16[64,128]{1,0:T(8,128)(2,1)} %param.27) | copy-start | bytes 49156
Sparse Core Ops, SparseCore 0:
  12.2 38.5 all-gather.2
  153.3 61.0 all-gather.4
where the time goes:
time: 244 us; the launch traced here: 243 us
  local copies, waits for them, and re-layouts  55.8 us (23%)
  waiting for transfers between devices  51.2 us (21%)
  matrix products  48.5 us (20%)
  other arithmetic  42.5 us (17%)
  blocking collectives  26.7 us (11%)
  between operations  14.4 us (6%)
  starting transfers between devices  3.52 us (1%)
    all_gather x1, waiting for transfers between devices, combined_all(): gathered = jax.tree.map(lambda a: lax.all_gather(a, axis), part)  41.8 us
    dot_general x4, matrix products, one_group(): jnp.einsum('ijhk,ikhd->ijhd', weights.astype(jnp.bfloat16), value_part, p...  24.9 us
    all_gather x1, blocking collectives, on_device(): bias_column = lax.all_gather(bias_tile, 'row', axis=1, tiled=True)  16.3 us
    dot_general x4, matrix products, one_group(): jnp.einsum('ijhd,ikhd->ijhk', query_part, key_part, preferred_element_typ...  15.3 us
    dynamic_slice x8, local copies, waits for them, and re-layouts, on_device(): lax.map(one_group, (grouped(queries), grouped(norm_piece), grouped(key_sh...  13.6 us
    add x3, other arithmetic, combine(): earlier[2] * early_scale[..., None] + later[2] * late_scale[..., None]  12.9 us
    unnamed x42, local copies, waits for them, and re-layouts  10.6 us
    all_gather x1, blocking collectives, combined_all(): gathered = jax.tree.map(lambda a: lax.all_gather(a, axis), part)  10.4 us
  transfers between devices with their start and end apart: 3, of which 3 were waited for; matrix products, arithmetic and copies ran while one was open for 6% of the time, Pallas kernels for 0%

commit v1 on v0

--- a/solution.py
+++ b/solution.py
@@ -1,6 +1,10 @@
+import functools
+
 import jax
 import jax.numpy as jnp
 from jax import lax
+from jax.experimental import pallas as pl
+from jax.experimental.pallas import tpu as pltpu
 from jax.sharding import PartitionSpec as P
 
 BLOCK = 128
@@ -37,7 +41,7 @@
     return chosen
 
 
-def on_device(
+def plain_on_device(
     templ_pair,
     main_pair,
     coverage,
@@ -185,6 +189,445 @@
     return (new_pair[None], embedding.reshape(rows_dev, cols_dev, pair_ch))
 
 
+LOG2E = 1.4426950408889634
+
+
+def normed_rows(values, gain):
+    center = values - jnp.mean(values, axis=0, keepdims=True)
+    spread = jnp.mean(center * center, axis=0, keepdims=True)
+    return (center * lax.rsqrt(spread + EPSILON) * gain).astype(jnp.bfloat16)
+
+
+def piece_block(idx_ref, piece, pieces):
+    half = idx_ref[0]
+    side = half if piece % 2 else 1 - half
+    return side * (pieces // 2) + piece // 2
+
+
+def mask_shift(cover_ref, mask_ref, templ, row_block, col_block):
+    valid = (
+        cover_ref[templ, row_block] * cover_ref[templ, col_block] * mask_ref[row_block, col_block]
+    )
+    return MASK_SHIFT * (valid.astype(jnp.float32) - 1.0)
+
+
+def matmul(lhs, rhs, lhs_dim=1, rhs_dim=0):
+    return lax.dot_general(
+        lhs, rhs, (((lhs_dim,), (rhs_dim,)), ((), ())), preferred_element_type=jnp.float32
+    )
+
+
+def norm_kernel(
+    heads, idx_ref, x_ref, gain_ref, bias_w_ref, *refs
+):
+    piece = pl.program_id(0)
+    *norm_refs, bias_ref, held = refs
+    for chunk, norm_ref in enumerate(norm_refs):
+
+        @pl.when(piece // 2 == chunk)
+        def _():
+            for i in range(x_ref.shape[0]):
+                normed = normed_rows(x_ref[i].astype(jnp.float32), gain_ref[...])
+                norm_ref[i] = normed
+                row_bias = matmul(bias_w_ref[...], normed)
+                for head in range(heads):
+                    held[head, i : i + 1, :] = row_bias[head : head + 1, :]
+
+    bias_ref[...] = held[...].astype(jnp.bfloat16)
+
+
+def weight_kernel(heads, project_ref, tri_out_ref, kv_ref, pack_ref):
+    channels = project_ref.shape[0]
+    hidden = tri_out_ref.shape[0]
+    dim = hidden // heads
+    scale = dim ** (-0.5) * LOG2E
+    project = project_ref[...]
+    for head in range(heads):
+        query = project[:, head * dim : (head + 1) * dim]
+        key = project[:, hidden + head * dim : hidden + (head + 1) * dim]
+        pack_ref[head * channels : (head + 1) * channels, :] = (
+            matmul(key, query, 1, 1) * scale
+        ).astype(jnp.bfloat16)
+    row = heads * channels
+    rest = (
+        project[:, 3 * hidden :],
+        project[:, 2 * hidden : 3 * hidden],
+        tri_out_ref[...],
+        kv_ref[...],
+    )
+    for part in rest:
+        flipped = part.astype(jnp.float32).T.astype(jnp.bfloat16)
+        pack_ref[row : row + flipped.shape[0], :] = flipped
+        row += flipped.shape[0]
+
+
+def bias_kernel(tiles_per_col, row_devs, idx_ref, cover_ref, mask_ref, *refs):
+    *tile_refs, out_ref = refs
+    heads, tile_rows, cols = tile_refs[0].shape
+    templ, row_dev, col_dev, row_block = idx_ref[1], idx_ref[2], idx_ref[3], idx_ref[4]
+    col_devs = row_devs // tiles_per_col
+    best = jnp.float32(-MASK_SHIFT)
+    for block in range(col_devs):
+        best = jnp.maximum(best, mask_shift(cover_ref, mask_ref, templ, row_block, block))
+    for turn, tile_ref in enumerate(tile_refs):
+        source = lax.rem(row_dev - turn + row_devs, row_devs)
+        for place in range(row_devs):
+            part, block = place // col_devs, place % col_devs
+
+            @pl.when(source == place)
+            def _():
+                slot = lax.rem(block - col_dev + col_devs, col_devs)
+                shift = mask_shift(cover_ref, mask_ref, templ, row_block, block) - best
+                for head in range(heads):
+                    flipped = tile_ref[head].astype(jnp.float32).T
+                    out_ref[
+                        head,
+                        pl.ds(slot * cols, cols),
+                        part * tile_rows : (part + 1) * tile_rows,
+                    ] = (flipped + shift) * LOG2E
+
+
+def attend_kernel(
+    heads, idx_ref, x_ref, own_ref, far_ref, main_ref, bias_ref, pack_ref, query_ref, gain_ref, *refs
+):
+    out_ref, state_ref = refs[-2:]
+    channels = x_ref.shape[1]
+    cols = x_ref.shape[2]
+    hidden = query_ref.shape[0]
+    dim = hidden // heads
+    row = heads * channels + hidden
+    first_w = pack_ref[:row, :]
+    value_w = pack_ref[row : row + hidden, :]
+    tri_w = pack_ref[row + hidden : row + hidden + channels, :]
+    kv_w = pack_ref[row + hidden + channels :, :]
+    ones = jnp.ones((dim, 2 * cols), jnp.bfloat16)
+    for i in range(x_ref.shape[0]):
+        own = own_ref[i]
+        both = jnp.concatenate([own, far_ref[i]], axis=1)
+        first = matmul(first_w, own)
+        gates = jax.nn.sigmoid(first[heads * channels :, :])
+        probe = first.astype(jnp.bfloat16)
+        probe = jnp.concatenate(
+            [probe[h * channels : (h + 1) * channels, :] for h in range(heads)], axis=1
+        )
+        scores = matmul(both, probe, 0, 0)
+        values = matmul(value_w, both).astype(jnp.bfloat16)
+        gated = []
+        for pair in range(heads // 2):
+            weights = []
+            for head in (2 * pair, 2 * pair + 1):
+                part = scores[:, head * cols : (head + 1) * cols] + bias_ref[head]
+                highest = jnp.max(part, axis=0, keepdims=True)
+                weights.append(jnp.exp2(part - highest).astype(jnp.bfloat16))
+            summed = matmul(
+                jnp.concatenate([values[2 * pair * dim : 2 * (pair + 1) * dim, :], ones], axis=0),
+                jnp.concatenate(weights, axis=1),
+            )
+            for side in range(2):
+                head = 2 * pair + side
+                lanes = slice(side * cols, (side + 1) * cols)
+                total = summed[2 * dim : 2 * dim + 1, lanes]
+                gated.append(
+                    summed[side * dim : (side + 1) * dim, lanes]
+                    * (1.0 / total)
+                    * gates[head * dim : (head + 1) * dim, :]
+                )
+        gated = jnp.concatenate(gated, axis=0).astype(jnp.bfloat16)
+        fresh = (x_ref[i].astype(jnp.float32) + matmul(tri_w, gated)).astype(jnp.bfloat16)
+        out_ref[i] = fresh
+        merge_norm = normed_rows(fresh.astype(jnp.float32), gain_ref[...])
+        merge_kv = matmul(kv_w, merge_norm).astype(jnp.bfloat16)
+        main_query = matmul(query_ref[...], main_ref[i], 1, 1) * dim ** (-0.5)
+        product = main_query * merge_kv[:hidden, :].astype(jnp.float32)
+        score = jnp.concatenate(
+            [
+                jnp.sum(product[h * dim : (h + 1) * dim, :], axis=0, keepdims=True)
+                for h in range(heads)
+            ],
+            axis=0,
+        )
+        store_state(state_ref, i, merge_kv[hidden:, :], score)
+
+
+def store_state(state_ref, i, values, score):
+    hidden = values.shape[0]
+    high = score.astype(jnp.bfloat16)
+    low = (score - high.astype(jnp.float32)).astype(jnp.bfloat16)
+    state_ref[i, :hidden, :] = values
+    state_ref[i, hidden:, :] = jnp.concatenate([high, low], axis=0)
+
+
+def spread_heads(per_head, dim):
+    heads, cols = per_head.shape
+    return jnp.concatenate(
+        [jnp.broadcast_to(per_head[h : h + 1, :], (dim, cols)) for h in range(heads)], axis=0
+    )
+
+
+def joined(heads, first_ref, second_ref, i, first_shift, second_shift):
+    hidden = first_ref.shape[1] - 2 * heads
+
+    def parts(ref, shift):
+        extra = ref[i, hidden:, :].astype(jnp.float32)
+        return ref[i, :hidden, :].astype(jnp.float32), extra[:heads] + extra[heads:] + shift
+
+    first_values, first_score = parts(first_ref, first_shift)
+    second_values, second_score = parts(second_ref, second_shift)
+    highest = jnp.maximum(first_score, second_score)
+    first_weight = jnp.exp(first_score - highest)
+    second_weight = jnp.exp(second_score - highest)
+    total = first_weight + second_weight
+    inverse = 1.0 / total
+    dim = hidden // heads
+    values = first_values * spread_heads(first_weight * inverse, dim)
+    values = values + second_values * spread_heads(second_weight * inverse, dim)
+    return values, highest + jnp.log(total)
+
+
+def pair_shifts(idx_ref, cover_ref, mask_ref):
+    templ, col_dev, row_block = idx_ref[1], idx_ref[3], idx_ref[4]
+    even = templ - lax.rem(templ, 2)
+    own = mask_shift(cover_ref, mask_ref, templ, row_block, col_dev)
+    other = mask_shift(cover_ref, mask_ref, 2 * even + 1 - templ, row_block, col_dev)
+    far = 2 - even
+    far_best = jnp.maximum(
+        mask_shift(cover_ref, mask_ref, far, row_block, col_dev),
+        mask_shift(cover_ref, mask_ref, far + 1, row_block, col_dev),
+    )
+    best = jnp.maximum(own, other)
+    return own - best, other - best, best, far_best
+
+
+def core_join_kernel(heads, idx_ref, cover_ref, mask_ref, own_ref, other_ref, state_ref):
+    own_shift, other_shift, _, _ = pair_shifts(idx_ref, cover_ref, mask_ref)
+    for i in range(own_ref.shape[0]):
+        values, score = joined(heads, own_ref, other_ref, i, own_shift, other_shift)
+        store_state(state_ref, i, values.astype(jnp.bfloat16), score)
+
+
+def chip_join_kernel(
+    heads, idx_ref, cover_ref, mask_ref, own_ref, other_ref, w_ref, *refs
+):
+    merged_ref, out_ref = refs[-2:]
+    _, _, best, far_best = pair_shifts(idx_ref, cover_ref, mask_ref)
+    top = jnp.maximum(best, far_best)
+    for i in range(own_ref.shape[0]):
+        values, _ = joined(heads, own_ref, other_ref, i, best - top, far_best - top)
+        merged = values.astype(jnp.bfloat16)
+        merged_ref[i] = merged
+        out_ref[i] = matmul(merged, w_ref[...], 0, 0).astype(jnp.bfloat16)
+
+
+def embed_kernel(idx_ref, merged_ref, w_ref, prior_ref, out_ref):
+    for i in range(merged_ref.shape[0]):
+        out_ref[i] = matmul(merged_ref[i], w_ref[...], 0, 0).astype(jnp.bfloat16)
+
+
+def fused_on_device(
+    templ_pair, main_pair, coverage, pair_mask, tri_gain, w_project, w_bias, w_tri_out,
+    merge_gain, w_merge_q, w_merge_kv, w_merge_out,
+):
+    rows, cols, channels = templ_pair.shape[1:]
+    hidden = w_tri_out.shape[0]
+    heads = w_bias.shape[1]
+    pair_ch = main_pair.shape[-1]
+    row_devs, col_devs = lax.axis_size("row"), lax.axis_size("col")
+    tiles_per_col = row_devs // col_devs
+    templ, row_dev, col_dev = (lax.axis_index(a) for a in ("tmpl", "row", "col"))
+    idx = jnp.stack([templ % 2, templ, row_dev, col_dev, (row_dev * rows) // BLOCK]).astype(jnp.int32)
+    pieces = PIECES
+    piece_rows = rows // pieces
+    step_rows = STEP_ROWS
+    steps = piece_rows // step_rows
+    stored = jnp.swapaxes(templ_pair[0], 1, 2)
+    bf16, f32 = jnp.bfloat16, jnp.float32
+    tri_gain_wide = jnp.broadcast_to(tri_gain[:, None], (channels, cols))
+    merge_gain_wide = jnp.broadcast_to(merge_gain[:, None], (channels, cols))
+
+    def whole(array):
+        return pl.BlockSpec(array.shape, lambda *_: (0,) * array.ndim)
+
+    smem = pl.BlockSpec(memory_space=pltpu.SMEM)
+
+    def call(kernel, grid, in_specs, out_specs, out_shape, scratch=(), aliases=None, cost=1e6):
+        return pl.pallas_call(
+            kernel,
+            grid_spec=pltpu.PrefetchScalarGridSpec(
+                num_scalar_prefetch=1, grid=grid, in_specs=in_specs, out_specs=out_specs,
+                scratch_shapes=list(scratch),
+            ),
+            out_shape=out_shape,
+            input_output_aliases=aliases or {},
+            cost_estimate=pl.CostEstimate(
+                flops=int(cost), bytes_accessed=1 << 20, transcendentals=0
+            ),
+        )
+
+    chunks = pieces // 2
+
+    def piece_of(p, idx_ref):
+        half = idx_ref[0]
+        side = jnp.where(p % 2 == 1, half, 1 - half)
+        return side * (pieces // 2) + p // 2
+
+    norm_specs = [
+        pl.BlockSpec(
+            (piece_rows, channels, cols),
+            functools.partial(lambda c, p, s: (jnp.clip(p - 2 * c, 0, 1), 0, 0), chunk),
+        )
+        for chunk in range(chunks)
+    ]
+    *norms, bias_tile = call(
+        functools.partial(norm_kernel, heads),
+        (pieces,),
+        [
+            pl.BlockSpec((piece_rows, channels, cols), lambda p, s: (piece_of(p, s), 0, 0)),
+            whole(tri_gain_wide),
+            pl.BlockSpec((heads, channels), lambda *_: (0, 0)),
+        ],
+        norm_specs + [pl.BlockSpec((heads, piece_rows, cols), lambda p, s: (0, piece_of(p, s), 0))],
+        [jax.ShapeDtypeStruct((2 * piece_rows, channels, cols), bf16)] * chunks
+        + [jax.ShapeDtypeStruct((heads, rows, cols), bf16)],
+        [pltpu.VMEM((heads, piece_rows, cols), f32)],
+    )(idx, stored, tri_gain_wide, w_bias.T)
+
+    tiles = []
+    for turn in range(row_devs):
+        perm = []
+        for source_row in range(row_devs):
+            for source_col in range(col_devs):
+                place = (source_row % tiles_per_col) * col_devs + source_col
+                target = ((place + turn) % row_devs) * col_devs + source_row // tiles_per_col
+                perm.append((source_row * col_devs + source_col, target))
+        tiles.append(lax.ppermute(bias_tile, ("row", "col"), perm))
+    swap = [(c, col_devs - 1 - c) for c in range(col_devs)]
+    fars = [lax.ppermute(norm, "col", swap) for norm in norms]
+
+    pack_shape = ((heads + 1) * channels * 0 + heads * channels + 2 * hidden + channels + 2 * hidden, channels)
+    pack = pl.pallas_call(
+        functools.partial(weight_kernel, heads),
+        out_shape=jax.ShapeDtypeStruct(pack_shape, bf16),
+    )(w_project, w_tri_out, w_merge_kv)
+    bias = call(
+        functools.partial(bias_kernel, tiles_per_col, row_devs),
+        (1,),
+        [smem, smem] + [whole(t) for t in tiles],
+        pl.BlockSpec((heads, col_devs * cols, cols), lambda *_: (0, 0, 0)),
+        jax.ShapeDtypeStruct((heads, col_devs * cols, cols), f32),
+    )(idx, coverage, pair_mask, *tiles)
+
+    query_w = w_merge_q.T
+    out = None
+    states = []
+    for piece in range(pieces):
+        chunk, side = piece // 2, piece % 2
+
+        def at_rows(g, s, piece=piece):
+            return (piece_block(s, piece, pieces) * steps + g, 0, 0)
+
+        def at_norm(g, s, side=side):
+            return (side * steps + g, 0, 0)
+
+        prior = [] if out is None else [out]
+        operands = [
+            stored, norms[chunk], fars[chunk], main_pair, bias, pack, query_w, merge_gain_wide
+        ] + prior
+        specs = [
+            pl.BlockSpec((step_rows, channels, cols), at_rows),
+            pl.BlockSpec((step_rows, channels, cols), at_norm),
+            pl.BlockSpec((step_rows, channels, cols), at_norm),
+            pl.BlockSpec((step_rows, cols, pair_ch), at_rows),
+            whole(bias), whole(pack), whole(query_w), whole(merge_gain_wide),
+        ] + [pl.BlockSpec(memory_space=pl.ANY)] * len(prior)
+        out, state = call(
+            functools.partial(attend_kernel, heads),
+            (steps,),
+            specs,
+            [
+                pl.BlockSpec((step_rows, channels, cols), at_rows),
+                pl.BlockSpec((step_rows, hidden + 2 * heads, cols), lambda g, s: (g, 0, 0)),
+            ],
+            [
+                jax.ShapeDtypeStruct(stored.shape, bf16),
+                jax.ShapeDtypeStruct((piece_rows, hidden + 2 * heads, cols), bf16),
+            ],
+            aliases={len(operands): 0} if prior else None,
+            cost=6e9,
+        )(idx, *operands)
+        states.append(state)
+
+    cores = [(t, t + 1 - 2 * (t % 2)) for t in range(lax.axis_size("tmpl"))]
+    chips = [(t, (t + 2) % 4) for t in range(lax.axis_size("tmpl"))]
+    emb = None
+    emb_shape = jax.ShapeDtypeStruct(main_pair.shape, bf16)
+    for chunk in range(chunks):
+        sent, kept = states[2 * chunk], states[2 * chunk + 1]
+        other = lax.ppermute(sent, "tmpl", cores)
+        pair_state = call(
+            functools.partial(core_join_kernel, heads),
+            (1,),
+            [smem, smem, whole(kept), whole(other)],
+            whole(kept),
+            jax.ShapeDtypeStruct(kept.shape, bf16),
+        )(idx, coverage, pair_mask, kept, other)
+        far_state = lax.ppermute(pair_state, "tmpl", chips)
+
+        def at_own(g, s, piece=2 * chunk + 1):
+            return (piece_block(s, piece, pieces), 0, 0)
+
+        def at_other(g, s, piece=2 * chunk):
+            return (piece_block(s, piece, pieces), 0, 0)
+
+        prior = [] if emb is None else [emb]
+        operands = [coverage, pair_mask, pair_state, far_state, w_merge_out] + prior
+        merged, emb = call(
+            functools.partial(chip_join_kernel, heads),
+            (1,),
+            [smem, smem, whole(pair_state), whole(far_state), whole(w_merge_out)]
+            + [pl.BlockSpec(memory_space=pl.ANY)] * len(prior),
+            [
+                pl.BlockSpec((piece_rows, hidden, cols), lambda *_: (0, 0, 0)),
+                pl.BlockSpec((piece_rows, cols, pair_ch), at_own),
+            ],
+            [jax.ShapeDtypeStruct((piece_rows, hidden, cols), bf16), emb_shape],
+            aliases={len(operands): 1} if prior else None,
+        )(idx, *operands)
+        merged_other = lax.ppermute(merged, "tmpl", cores)
+        emb = call(
+            embed_kernel,
+            (1,),
+            [whole(merged_other), whole(w_merge_out), pl.BlockSpec(memory_space=pl.ANY)],
+            pl.BlockSpec((piece_rows, cols, pair_ch), at_other),
+            emb_shape,
+            aliases={3: 0},
+        )(idx, merged_other, w_merge_out, emb)
+    return (jnp.swapaxes(out, 1, 2)[None], emb)
+
+
+PIECES = 4
+STEP_ROWS = 4
+
+
+def takes_fused(templ_pair, main_pair):
+    rows, cols = templ_pair.shape[1:3]
+    row_devs, col_devs = lax.axis_size("row"), lax.axis_size("col")
+    return (
+        lax.axis_size("tmpl") == 4
+        and col_devs == 2
+        and cols == BLOCK
+        and BLOCK % rows == 0
+        and row_devs % col_devs == 0
+        and rows * (row_devs // col_devs) == cols
+        and rows % (PIECES * STEP_ROWS) == 0
+    )
+
+
+def on_device(*operands):
+    if takes_fused(*operands[:2]):
+        return fused_on_device(*operands)
+    return plain_on_device(*operands)
+
+
 def solution(mesh):
     in_specs = (
         P("tmpl", "row", "col", None),

time: 244 us -> 122 us (0.50)
  Pallas kernels: 0 us -> 87.6 us
  matrix products: 48.5 us -> 0 us
  waiting for transfers between devices: 51.2 us -> 4.33 us
  local copies, waits for them, and re-layouts: 55.8 us -> 10.3 us
  other arithmetic: 42.5 us -> 0 us
  blocking collectives: 26.7 us -> 0 us
  starting transfers between devices: 3.52 us -> 17.8 us
  between operations: 14.4 us -> 0.76 us
    pallas_call x0 -> x13, Pallas kernels: none -> 87.6 us  [the longest x4 61.4 us: fused_on_device(): call(functools.partial(attend_kernel, heads), (steps,), specs, [pl.BlockS...]
    all_gather x2 -> x0, waiting for transfers between devices: 49.3 us -> none  [the longest x1 41.8 us: combined_all(): gathered = jax.tree.map(lambda a: lax.all_gather(a, axis), part)]
    dot_general x18 -> x0, matrix products: 48.5 us -> none  [the longest x4 24.9 us: one_group(): jnp.einsum('ijhk,ikhd->ijhd', weights.astype(jnp.bfloat16), value_part, p...]
    all_gather x2 -> x0, blocking collectives: 26.7 us -> none  [the longest x1 16.3 us: on_device(): bias_column = lax.all_gather(bias_tile, 'row', axis=1, tiled=True)]
    slice x15 -> x0, local copies, waits for them, and re-layouts: 22.8 us -> none  [the longest x8 10.2 us: one_group(): key_value[..., hidden:].reshape(group, piece_width, head_count, head_dim)]
    ppermute x0 -> x12, starting transfers between devices: none -> 17.8 us  [the longest x4 11 us: fused_on_device(): tiles.append(lax.ppermute(bias_tile, ('row', 'col'), perm))]
    reduce_sum x8 -> x0, other arithmetic: 14.9 us -> none  [the longest x4 9.94 us: one_group(): totals = totals * rescale + jnp.sum(weights, axis=-1)]
    dynamic_slice x12 -> x0, local copies, waits for them, and re-layouts: 13.6 us -> none  [the longest x8 13.6 us: on_device(): lax.map(one_group, (grouped(queries), grouped(norm_piece), grouped(key_sh...]
  transfers between devices with their start and end apart: 3 -> 12, of which waited for: 3 -> 3; matrix products, arithmetic and copies ran while one was open for 6% -> 2% of each run, Pallas kernels for 0% -> 64%
where the time goes in v1:
time: 122 us; the launch traced here: 121 us
  Pallas kernels  87.6 us (72%)
  starting transfers between devices  17.8 us (15%)
  local copies, waits for them, and re-layouts  10.3 us (8%)
  waiting for transfers between devices  4.33 us (4%)
    pallas_call x4, Pallas kernels, fused_on_device(): call(functools.partial(attend_kernel, heads), (steps,), specs, [pl.BlockS...  61.4 us
    ppermute x4, starting transfers between devices, fused_on_device(): tiles.append(lax.ppermute(bias_tile, ('row', 'col'), perm))  11 us
    unnamed x27, local copies, waits for them, and re-layouts  7.62 us
    pallas_call x2, Pallas kernels, fused_on_device(): call(functools.partial(chip_join_kernel, heads), (1,), [smem, smem, whole...  5.84 us
    pallas_call x2, Pallas kernels, fused_on_device(): call(embed_kernel, (1,), [whole(merged_other), whole(w_merge_out), pl.Blo...  5.49 us
    pallas_call x2, Pallas kernels, fused_on_device(): call(functools.partial(core_join_kernel, heads), (1,), [smem, smem, whole...  5.26 us
    pallas_call x1, Pallas kernels, fused_on_device(): call(functools.partial(norm_kernel, heads), (pieces,), [pl.BlockSpec((pie...  4.77 us
    ppermute x2, starting transfers between devices, fused_on_device(): fars = [lax.ppermute(norm, 'col', swap) for norm in norms]  4.14 us
  transfers between devices with their start and end apart: 12, of which 3 were waited for; matrix products, arithmetic and copies ran while one was open for 2% of the time, Pallas kernels for 64%

profile of v1, /device:TPU:0, one launch (start us, length us, event | category | flops | bytes accessed | tf_op | source)
XLA Modules:
  0.0 120.9 jit_solution(2960259933063955731)
XLA Ops:
  0.6 0.0 copy-start.10
  0.7 0.6 stack.23.idx_ref
  1.3 1.3 %broadcast_in_dim.6.gain_ref = f32[64,128]{1,0:T(8,128)} broadcast(f32[64]{0:T(128)} %param.16), dimensions={0} | broadcast | bytes 33024 | tf_op jit(solution)/shard_map/broadcast_in_dim | solution.py:444
  2.6 4.8 %shard_map.131 = (bf16[32,64,128]{2,1,0:T(8,128)(2,1)}, bf16[32,64,128]{2,1,0:T(8,128)(2,1)}, bf16[4,64,128]{2,1,0:T(8,128)(2,1)}) custom-call(s32[5]{0:T(128)} %stack.23.idx_ref, bf16[64,64,128]{2,1,0:T(8,128)(2,1)} %bitcast.13, f32[64,128]{1,0:T(8,128)} %broadcast_in_dim.6.gain_ref, bf16[4,64]{1,0:T(4,128)(2,1)} %bitcast.18), custom_call_target="tpu_custom_call" | custom-call | flops 1000000 | bytes 1048576 | tf_op jit(solution)/shard_map/pallas_call | solution.py:480
  7.4 3.0 %collective-permute-start.5 = (bf16[32,64,128]{2,1,0:T(8,128)(2,1)}, bf16[32,64,128]{2,1,0:T(8,128)(2,1)S(1)}, u32[]{:S(2)}, u32[]{:S(2)}) collective-permute-start(bf16[32,64,128]{2,1,0:T(8,128)(2,1)} %get-tuple-element.19.own_ref), channel_id=1, source_target_pairs={{0,1},{1,0},{2,3},{3,2},{4,5},{5,4},{6,7},{7,6},{8,9},{9,8},{10,11... | collective-permute-start | bytes 1572872 | tf_op jit(solution)/shard_map/ppermute | solution.py:504
  10.4 5.5 %collective-permute-start.4 = (bf16[4,64,128]{2,1,0:T(8,128)(2,1)}, bf16[4,64,128]{2,1,0:T(8,128)(2,1)S(1)}, u32[]{:S(2)}, u32[]{:S(2)}) collective-permute-start(bf16[4,64,128]{2,1,0:T(8,128)(2,1)} %get-tuple-element.18), channel_id=1, source_target_pairs={{0,6},{1,0},{2,2},{3,4},{4,7},{5,1},{6,3},{7,5},{8,14},{9,8},{10,1... | collective-permute-start | bytes 196616 | tf_op jit(solution)/shard_map/ppermute | solution.py:502
  15.9 0.6 collective-permute-start.3
  16.4 3.4 %collective-permute-start.2 = (bf16[4,64,128]{2,1,0:T(8,128)(2,1)}, bf16[4,64,128]{2,1,0:T(8,128)(2,1)S(1)}, u32[]{:S(2)}, u32[]{:S(2)}) collective-permute-start(bf16[4,64,128]{2,1,0:T(8,128)(2,1)} %get-tuple-element.18), channel_id=1, source_target_pairs={{0,2},{1,4},{2,6},{3,0},{4,3},{5,5},{6,7},{7,1},{8,10},{9,12},{10,... | collective-permute-start | bytes 196616 | tf_op jit(solution)/shard_map/ppermute | solution.py:502
  19.8 1.5 %collective-permute-start.1 = (bf16[4,64,128]{2,1,0:T(8,128)(2,1)}, bf16[4,64,128]{2,1,0:T(8,128)(2,1)S(1)}, u32[]{:S(2)}, u32[]{:S(2)}) collective-permute-start(bf16[4,64,128]{2,1,0:T(8,128)(2,1)} %get-tuple-element.18), channel_id=1, source_target_pairs={{0,0},{1,2},{2,4},{3,6},{4,1},{5,3},{6,5},{7,7},{8,8},{9,10},{10,1... | collective-permute-start | bytes 196616 | tf_op jit(solution)/shard_map/ppermute | solution.py:502
  21.3 1.3 %copy.20.cover_ref = s32[4,2]{1,0:T(4,128)} copy(s32[4,2]{0,1:T(2,128)} %param.14) | data formatting | bytes 64 | tf_op args[2]
  22.7 1.7 %shard_map.133.pack_ref = bf16[576,64]{1,0:T(8,128)(2,1)} custom-call(bf16[64,256]{1,0:T(8,128)(2,1)} %project_ref.1, bf16[64,64]{1,0:T(8,128)(2,1)} %tri_out_ref.1, bf16[64,128]{1,0:T(8,128)(2,1)} %kv_ref.1), custom_call_target="tpu_custom_call" | custom-call | tf_op jit(solution)/shard_map/pallas_call | solution.py:507
  24.3 1.0 collective-permute-done.4.refs_3_
  25.3 0.0 copy-start.6
  25.3 1.1 collective-permute-start
  26.4 0.0 collective-permute-done.3.refs_2_
  26.4 0.0 copy-start.7
  26.4 0.0 collective-permute-done.2.refs_1_
  26.5 0.0 copy-start.8
  26.5 0.0 collective-permute-done.1.refs_0_
  26.5 0.0 copy-done.6
  26.5 0.6 copy-done.7
  27.1 0.0 copy-done.8
  27.1 0.0 copy-start.9
  27.1 0.6 copy-done.9
  27.7 3.2 %shard_map.132.bias_ref = f32[4,256,128]{2,1,0:T(8,128)} custom-call(s32[5]{0:T(128)} %stack.23.idx_ref, s32[4,2]{1,0:T(4,128)} %copy.20.cover_ref, s32[2,2]{1,0:T(2,128)} %mask_ref.9, bf16[4,64,128]{2,1,0:T(8,128)(2,1)} %copy-done.9, bf16[4,64,128]{2,1,0:T(8,128)(2,1)} %copy-done.8, bf16[4,64,128]{2,1,0:T(8,128)(2,1)} %copy-done.7, ...), custom_call_target="tpu_custom_call" | custom-call | flops 1000000 | bytes 1048576 | tf_op jit(solution)/shard_map/pallas_call | solution.py:511
  30.9 0.0 collective-permute-done.5.far_ref
  30.9 0.0 copy-start.12
  30.9 0.0 copy-done.10
  30.9 0.8 broadcast_in_dim.7.gain_ref
  31.7 0.0 copy-done.12
  31.8 15.3 %shard_map.134 = (bf16[64,64,128]{2,1,0:T(8,128)(2,1)}, bf16[16,72,128]{2,1,0:T(8,128)(2,1)}) custom-call(s32[5]{0:T(128)} %stack.23.idx_ref, bf16[64,64,128]{2,1,0:T(8,128)(2,1)} %bitcast.14, bf16[32,64,128]{2,1,0:T(8,128)(2,1)} %get-tuple-element.19.own_ref, bf16[32,64,128]{2,1,0:T(8,128)(2,1)} %copy-done.12, bf16[64,128,128]{2,1,0:T(8,128)(2,1)} %main_ref.7, ...), custom_call_target="tpu_custom_call" | custom-call | flops 6000000000 | bytes 1048576 | tf_op jit(solution)/shard_map/pallas_call | solution.py:542
  47.1 0.0 collective-permute-start.8
  47.1 15.4 %shard_map.135 = (bf16[64,64,128]{2,1,0:T(8,128)(2,1)}, bf16[16,72,128]{2,1,0:T(8,128)(2,1)}) custom-call(s32[5]{0:T(128)} %stack.23.idx_ref, bf16[64,64,128]{2,1,0:T(8,128)(2,1)} %bitcast.15, bf16[32,64,128]{2,1,0:T(8,128)(2,1)} %get-tuple-element.19.own_ref, bf16[32,64,128]{2,1,0:T(8,128)(2,1)} %copy-done.12, ...), custom_call_target="tpu_custom_call", output_to_operand_aliasing={{0}: (9, {})} | custom-call | flops 6000000000 | bytes 1048576 | tf_op jit(solution)/shard_map/pallas_call | solution.py:542
  62.5 0.0 collective-permute-done.far_ref
  62.5 0.0 copy-start.11
  62.5 0.8 copy-done.11
  63.3 15.3 %shard_map.136 = (bf16[64,64,128]{2,1,0:T(8,128)(2,1)}, bf16[16,72,128]{2,1,0:T(8,128)(2,1)}) custom-call(s32[5]{0:T(128)} %stack.23.idx_ref, bf16[64,64,128]{2,1,0:T(8,128)(2,1)} %bitcast.16, bf16[32,64,128]{2,1,0:T(8,128)(2,1)} %get-tuple-element.17.own_ref, bf16[32,64,128]{2,1,0:T(8,128)(2,1)} %copy-done.11, ...), custom_call_target="tpu_custom_call", output_to_operand_aliasing={{0}: (9, {})} | custom-call | flops 6000000000 | bytes 1048576 | tf_op jit(solution)/shard_map/pallas_call | solution.py:542
  78.6 0.5 collective-permute-start.6
  79.1 0.0 collective-permute-done.8.other_ref
  79.1 0.0 copy-start.3
  79.1 0.7 copy-done.3
  79.8 2.6 %shard_map.139.own_ref = bf16[16,72,128]{2,1,0:T(8,128)(2,1)} custom-call(s32[5]{0:T(128)} %stack.23.idx_ref, s32[4,2]{1,0:T(4,128)} %copy.20.cover_ref, s32[2,2]{1,0:T(2,128)} %mask_ref.9, bf16[16,72,128]{2,1,0:T(8,128)(2,1)} %get-tuple-element.26.own_ref, bf16[16,72,128]{2,1,0:T(8,128)(2,1)} %copy-done.3), custom_call_target="tpu_custom_call" | custom-call | flops 1000000 | bytes 1048576 | tf_op jit(solution)/shard_map/pallas_call | solution.py:566
  82.5 1.5 %collective-permute-start.9 = (bf16[16,72,128]{2,1,0:T(8,128)(2,1)}, bf16[16,72,128]{2,1,0:T(8,128)(2,1)S(1)}, u32[]{:S(2)}, u32[]{:S(2)}) collective-permute-start(bf16[16,72,128]{2,1,0:T(8,128)(2,1)} %shard_map.139.own_ref), channel_id=1, source_target_pairs={{0,16},{8,24},{16,0},{24,8},{1,17},{9,25},{17,1},{25,9},{2,18},{10... | collective-permute-start | bytes 884744 | tf_op jit(solution)/shard_map/ppermute | solution.py:573
  84.0 15.4 %shard_map.137 = (bf16[64,64,128]{2,1,0:T(8,128)(2,1)}, bf16[16,72,128]{2,1,0:T(8,128)(2,1)}) custom-call(s32[5]{0:T(128)} %stack.23.idx_ref, bf16[64,64,128]{2,1,0:T(8,128)(2,1)} %bitcast.17, bf16[32,64,128]{2,1,0:T(8,128)(2,1)} %get-tuple-element.17.own_ref, bf16[32,64,128]{2,1,0:T(8,128)(2,1)} %copy-done.11, ...), custom_call_target="tpu_custom_call", output_to_operand_aliasing={{0}: (9, {})} | custom-call | flops 6000000000 | bytes 1048576 | tf_op jit(solution)/shard_map/pallas_call | solution.py:542
  99.3 0.0 collective-permute-done.6.other_ref
  99.3 0.0 copy-start.2
  99.3 0.7 copy-done.2
  100.0 2.6 %shard_map.138.own_ref = bf16[16,72,128]{2,1,0:T(8,128)(2,1)} custom-call(s32[5]{0:T(128)} %stack.23.idx_ref, s32[4,2]{1,0:T(4,128)} %copy.20.cover_ref, s32[2,2]{1,0:T(2,128)} %mask_ref.9, bf16[16,72,128]{2,1,0:T(8,128)(2,1)} %get-tuple-element.24.own_ref, bf16[16,72,128]{2,1,0:T(8,128)(2,1)} %copy-done.2), custom_call_target="tpu_custom_call" | custom-call | flops 1000000 | bytes 1048576 | tf_op jit(solution)/shard_map/pallas_call | solution.py:566
  102.7 0.5 collective-permute-start.7
  103.2 0.0 collective-permute-done.9.other_ref
  103.2 0.0 copy-start.1
  103.2 0.7 copy-done.1
  103.9 2.9 %shard_map.140 = (bf16[16,64,128]{2,1,0:T(8,128)(2,1)}, bf16[64,128,128]{2,1,0:T(8,128)(2,1)}) custom-call(s32[5]{0:T(128)} %stack.23.idx_ref, s32[4,2]{1,0:T(4,128)} %copy.20.cover_ref, s32[2,2]{1,0:T(2,128)} %mask_ref.9, bf16[16,72,128]{2,1,0:T(8,128)(2,1)} %shard_map.139.own_ref, bf16[16,72,128]{2,1,0:T(8,128)(2,1)} %copy-done.1, bf16[64,128]{1,0:T(8,128)(2,1)} %w_ref.7), custom_call_target="tpu_custom_call" | custom-call | flops 1000000 | bytes 1048576 | tf_op jit(solution)/shard_map/pallas_call | solution.py:583
  106.8 0.0 collective-permute-start.10
  106.8 1.7 %collective-permute-done.10.merged_ref = bf16[16,64,128]{2,1,0:T(8,128)(2,1)S(1)} collective-permute-done((bf16[16,64,128]{2,1,0:T(8,128)(2,1)}, bf16[16,64,128]{2,1,0:T(8,128)(2,1)S(1)}, u32[]{:S(2)}, u32[]{:S(2)}) %collective-permute-start.10) | collective-permute-done | bytes 262176 | tf_op jit(solution)/shard_map/ppermute | solution.py:595
  108.6 0.7 copy-done.5
  109.3 2.7 %shard_map.141.refs_0_ = bf16[64,128,128]{2,1,0:T(8,128)(2,1)} custom-call(s32[5]{0:T(128)} %stack.23.idx_ref, bf16[16,64,128]{2,1,0:T(8,128)(2,1)} %copy-done.5, bf16[64,128]{1,0:T(8,128)(2,1)} %w_ref.7, bf16[64,128,128]{2,1,0:T(8,128)(2,1)} %get-tuple-element.29.prior_ref), custom_call_target="tpu_custom_call", output_to_operand_aliasing={{}: (3, {})} | custom-call | flops 1000000 | bytes 1048576 | tf_op jit(solution)/shard_map/pallas_call | solution.py:596
  112.0 0.0 collective-permute-done.7.other_ref
  112.0 0.7 copy-done
  112.7 2.9 %shard_map.142 = (bf16[16,64,128]{2,1,0:T(8,128)(2,1)}, bf16[64,128,128]{2,1,0:T(8,128)(2,1)}) custom-call(s32[5]{0:T(128)} %stack.23.idx_ref, s32[4,2]{1,0:T(4,128)} %copy.20.cover_ref, s32[2,2]{1,0:T(2,128)} %mask_ref.9, bf16[16,72,128]{2,1,0:T(8,128)(2,1)} %shard_map.138.own_ref, bf16[16,72,128]{2,1,0:T(8,128)(2,1)} %copy-done, ...), custom_call_target="tpu_custom_call", output_to_operand_aliasing={{1}: (6, {})} | custom-call | flops 1000000 | bytes 1048576 | tf_op jit(solution)/shard_map/pallas_call | solution.py:583
  115.7 0.1 collective-permute-start.11
  115.8 1.6 %collective-permute-done.11.merged_ref = bf16[16,64,128]{2,1,0:T(8,128)(2,1)S(1)} collective-permute-done((bf16[16,64,128]{2,1,0:T(8,128)(2,1)}, bf16[16,64,128]{2,1,0:T(8,128)(2,1)S(1)}, u32[]{:S(2)}, u32[]{:S(2)}) %collective-permute-start.11) | collective-permute-done | bytes 262176 | tf_op jit(solution)/shard_map/ppermute | solution.py:595
  117.4 0.7 copy-done.4
  118.1 2.7 %shard_map.143 = bf16[64,128,128]{2,1,0:T(8,128)(2,1)} custom-call(s32[5]{0:T(128)} %stack.23.idx_ref, bf16[16,64,128]{2,1,0:T(8,128)(2,1)} %copy-done.4, bf16[64,128]{1,0:T(8,128)(2,1)} %w_ref.7, bf16[64,128,128]{2,1,0:T(8,128)(2,1)} %get-tuple-element.31.prior_ref), custom_call_target="tpu_custom_call", output_to_operand_aliasing={{}: (3, {})} | custom-call | flops 1000000 | bytes 1048576 | tf_op jit(solution)/shard_map/pallas_call | solution.py:596
  (3 shorter events, 0.0 us)
Async XLA Ops:
  0.6 30.3 %copy-start.10 = (f32[64]{0:T(128)S(1)}, f32[64]{0:T(128)}, u32[]{:S(2)}) copy-start(f32[64]{0:T(128)} %param.20) | copy-start | bytes 772
  7.4 23.6 %collective-permute-start.5 = (bf16[32,64,128]{2,1,0:T(8,128)(2,1)}, bf16[32,64,128]{2,1,0:T(8,128)(2,1)S(1)}, u32[]{:S(2)}, u32[]{:S(2)}) collective-permute-start(bf16[32,64,128]{2,1,0:T(8,128)(2,1)} %get-tuple-element.19.own_ref), channel_id=1, source_target_pairs={{0,1},{1,0},{2,3},{3,2},{4,5},{5,4},{6,7},{7,6},{8,9},{9,8},{10,11... | collective-permute-start | bytes 1572872 | tf_op jit(solution)/shard_map/ppermute | solution.py:504
  10.4 14.9 %collective-permute-start.4 = (bf16[4,64,128]{2,1,0:T(8,128)(2,1)}, bf16[4,64,128]{2,1,0:T(8,128)(2,1)S(1)}, u32[]{:S(2)}, u32[]{:S(2)}) collective-permute-start(bf16[4,64,128]{2,1,0:T(8,128)(2,1)} %get-tuple-element.18), channel_id=1, source_target_pairs={{0,6},{1,0},{2,2},{3,4},{4,7},{5,1},{6,3},{7,5},{8,14},{9,8},{10,1... | collective-permute-start | bytes 196616 | tf_op jit(solution)/shard_map/ppermute | solution.py:502
  15.9 10.6 %collective-permute-start.3 = (bf16[4,64,128]{2,1,0:T(8,128)(2,1)}, bf16[4,64,128]{2,1,0:T(8,128)(2,1)S(1)}, u32[]{:S(2)}, u32[]{:S(2)}) collective-permute-start(bf16[4,64,128]{2,1,0:T(8,128)(2,1)} %get-tuple-element.18), channel_id=1, source_target_pairs={{0,4},{1,6},{2,0},{3,2},{4,5},{5,7},{6,1},{7,3},{8,12},{9,14},{10,... | collective-permute-start | bytes 196616 | tf_op jit(solution)/shard_map/ppermute | solution.py:502
  16.4 10.0 %collective-permute-start.2 = (bf16[4,64,128]{2,1,0:T(8,128)(2,1)}, bf16[4,64,128]{2,1,0:T(8,128)(2,1)S(1)}, u32[]{:S(2)}, u32[]{:S(2)}) collective-permute-start(bf16[4,64,128]{2,1,0:T(8,128)(2,1)} %get-tuple-element.18), channel_id=1, source_target_pairs={{0,2},{1,4},{2,6},{3,0},{4,3},{5,5},{6,7},{7,1},{8,10},{9,12},{10,... | collective-permute-start | bytes 196616 | tf_op jit(solution)/shard_map/ppermute | solution.py:502
  19.8 6.6 %collective-permute-start.1 = (bf16[4,64,128]{2,1,0:T(8,128)(2,1)}, bf16[4,64,128]{2,1,0:T(8,128)(2,1)S(1)}, u32[]{:S(2)}, u32[]{:S(2)}) collective-permute-start(bf16[4,64,128]{2,1,0:T(8,128)(2,1)} %get-tuple-element.18), channel_id=1, source_target_pairs={{0,0},{1,2},{2,4},{3,6},{4,1},{5,3},{6,5},{7,7},{8,8},{9,10},{10,1... | collective-permute-start | bytes 196616 | tf_op jit(solution)/shard_map/ppermute | solution.py:502
  25.3 1.2 copy-start.6
  25.3 37.2 %collective-permute-start = (bf16[32,64,128]{2,1,0:T(8,128)(2,1)}, bf16[32,64,128]{2,1,0:T(8,128)(2,1)S(1)}, u32[]{:S(2)}, u32[]{:S(2)}) collective-permute-start(bf16[32,64,128]{2,1,0:T(8,128)(2,1)} %get-tuple-element.17.own_ref), channel_id=1, source_target_pairs={{0,1},{1,0},{2,3},{3,2},{4,5},{5,4},{6,7},{7,6},{8,9},{9,8},{10,11... | collective-permute-start | bytes 1572872 | tf_op jit(solution)/shard_map/ppermute | solution.py:504
  26.4 0.6 copy-start.7
  26.5 0.6 copy-start.8
  27.1 0.6 copy-start.9
  30.9 0.8 copy-start.12
  47.1 32.0 %collective-permute-start.8 = (bf16[16,72,128]{2,1,0:T(8,128)(2,1)}, bf16[16,72,128]{2,1,0:T(8,128)(2,1)S(1)}, u32[]{:S(2)}, u32[]{:S(2)}) collective-permute-start(bf16[16,72,128]{2,1,0:T(8,128)(2,1)} %get-tuple-element.27), channel_id=1, source_target_pairs={{0,8},{8,0},{16,24},{24,16},{1,9},{9,1},{17,25},{25,17},{2,10},{10... | collective-permute-start | bytes 884744 | tf_op jit(solution)/shard_map/ppermute | solution.py:565
  62.5 0.8 copy-start.11
  78.6 20.7 %collective-permute-start.6 = (bf16[16,72,128]{2,1,0:T(8,128)(2,1)}, bf16[16,72,128]{2,1,0:T(8,128)(2,1)S(1)}, u32[]{:S(2)}, u32[]{:S(2)}) collective-permute-start(bf16[16,72,128]{2,1,0:T(8,128)(2,1)} %get-tuple-element.25), channel_id=1, source_target_pairs={{0,8},{8,0},{16,24},{24,16},{1,9},{9,1},{17,25},{25,17},{2,10},{10... | collective-permute-start | bytes 884744 | tf_op jit(solution)/shard_map/ppermute | solution.py:565
  79.1 0.7 copy-start.3
  82.5 20.7 %collective-permute-start.9 = (bf16[16,72,128]{2,1,0:T(8,128)(2,1)}, bf16[16,72,128]{2,1,0:T(8,128)(2,1)S(1)}, u32[]{:S(2)}, u32[]{:S(2)}) collective-permute-start(bf16[16,72,128]{2,1,0:T(8,128)(2,1)} %shard_map.139.own_ref), channel_id=1, source_target_pairs={{0,16},{8,24},{16,0},{24,8},{1,17},{9,25},{17,1},{25,9},{2,18},{10... | collective-permute-start | bytes 884744 | tf_op jit(solution)/shard_map/ppermute | solution.py:573
  99.3 0.7 copy-start.2
  102.7 9.4 %collective-permute-start.7 = (bf16[16,72,128]{2,1,0:T(8,128)(2,1)}, bf16[16,72,128]{2,1,0:T(8,128)(2,1)S(1)}, u32[]{:S(2)}, u32[]{:S(2)}) collective-permute-start(bf16[16,72,128]{2,1,0:T(8,128)(2,1)} %shard_map.138.own_ref), channel_id=1, source_target_pairs={{0,16},{8,24},{16,0},{24,8},{1,17},{9,25},{17,1},{25,9},{2,18},{10... | collective-permute-start | bytes 884744 | tf_op jit(solution)/shard_map/ppermute | solution.py:573
  103.2 0.7 copy-start.1
  106.8 1.7 %collective-permute-start.10 = (bf16[16,64,128]{2,1,0:T(8,128)(2,1)}, bf16[16,64,128]{2,1,0:T(8,128)(2,1)S(1)}, u32[]{:S(2)}, u32[]{:S(2)}) collective-permute-start(bf16[16,64,128]{2,1,0:T(8,128)(2,1)} %get-tuple-element.28), channel_id=1, source_target_pairs={{0,8},{8,0},{16,24},{24,16},{1,9},{9,1},{17,25},{25,17},{2,10},{10... | collective-permute-start | bytes 786440 | tf_op jit(solution)/shard_map/ppermute | solution.py:595
  108.6 0.7 copy-start.5
  112.0 0.7 copy-start
  115.7 1.7 %collective-permute-start.11 = (bf16[16,64,128]{2,1,0:T(8,128)(2,1)}, bf16[16,64,128]{2,1,0:T(8,128)(2,1)S(1)}, u32[]{:S(2)}, u32[]{:S(2)}) collective-permute-start(bf16[16,64,128]{2,1,0:T(8,128)(2,1)} %get-tuple-element.30), channel_id=1, source_target_pairs={{0,8},{8,0},{16,24},{24,16},{1,9},{9,1},{17,25},{25,17},{2,10},{10... | collective-permute-start | bytes 786440 | tf_op jit(solution)/shard_map/ppermute | solution.py:595
  117.4 0.7 copy-start.4

commit v2 on v1

--- a/solution.py
+++ b/solution.py
@@ -290,9 +290,8 @@
 def attend_kernel(
     heads, idx_ref, x_ref, own_ref, far_ref, main_ref, bias_ref, pack_ref, query_ref, gain_ref, *refs
 ):
-    out_ref, state_ref = refs[-2:]
-    channels = x_ref.shape[1]
-    cols = x_ref.shape[2]
+    out_ref, state_ref, turned, probes, gates, mixers, held, tops, gated = refs[-9:]
+    step_rows, channels, cols = x_ref.shape
     hidden = query_ref.shape[0]
     dim = hidden // heads
     row = heads * channels + hidden
@@ -300,42 +299,48 @@
     value_w = pack_ref[row : row + hidden, :]
     tri_w = pack_ref[row + hidden : row + hidden + channels, :]
     kv_w = pack_ref[row + hidden + channels :, :]
-    ones = jnp.ones((dim, 2 * cols), jnp.bfloat16)
-    for i in range(x_ref.shape[0]):
+    for i in range(step_rows):
         own = own_ref[i]
         both = jnp.concatenate([own, far_ref[i]], axis=1)
         first = matmul(first_w, own)
-        gates = jax.nn.sigmoid(first[heads * channels :, :])
-        probe = first.astype(jnp.bfloat16)
-        probe = jnp.concatenate(
-            [probe[h * channels : (h + 1) * channels, :] for h in range(heads)], axis=1
-        )
-        scores = matmul(both, probe, 0, 0)
+        for h in range(heads):
+            probes[i, h] = first[h * channels : (h + 1) * channels, :].astype(jnp.bfloat16)
+        gates[i] = jax.nn.sigmoid(first[heads * channels :, :])
         values = matmul(value_w, both).astype(jnp.bfloat16)
-        gated = []
-        for pair in range(heads // 2):
-            weights = []
-            for head in (2 * pair, 2 * pair + 1):
-                part = scores[:, head * cols : (head + 1) * cols] + bias_ref[head]
-                highest = jnp.max(part, axis=0, keepdims=True)
-                weights.append(jnp.exp2(part - highest).astype(jnp.bfloat16))
-            summed = matmul(
-                jnp.concatenate([values[2 * pair * dim : 2 * (pair + 1) * dim, :], ones], axis=0),
-                jnp.concatenate(weights, axis=1),
+        for h in range(heads):
+            mixers[i, h, :dim, :] = values[h * dim : (h + 1) * dim, :]
+            mixers[i, h, dim:, :] = jnp.ones((mixers.shape[2] - dim, both.shape[1]), jnp.bfloat16)
+        turned[i] = both.T
+
+    slots = held.shape[0]
+
+    def score_row(i):
+        for h in range(heads):
+            scores = matmul(turned[i], probes[i, h]) + bias_ref[h]
+            held[i % slots, h] = scores
+            tops[i % slots, h] = jnp.broadcast_to(
+                jnp.max(scores, axis=0, keepdims=True), tops.shape[2:]
             )
-            for side in range(2):
-                head = 2 * pair + side
-                lanes = slice(side * cols, (side + 1) * cols)
-                total = summed[2 * dim : 2 * dim + 1, lanes]
-                gated.append(
-                    summed[side * dim : (side + 1) * dim, lanes]
-                    * (1.0 / total)
-                    * gates[head * dim : (head + 1) * dim, :]
-                )
-        gated = jnp.concatenate(gated, axis=0).astype(jnp.bfloat16)
-        fresh = (x_ref[i].astype(jnp.float32) + matmul(tri_w, gated)).astype(jnp.bfloat16)
-        out_ref[i] = fresh
-        merge_norm = normed_rows(fresh.astype(jnp.float32), gain_ref[...])
+
+    def mix_row(i):
+        for h in range(heads):
+            weights = jnp.exp2(held[i % slots, h] - tops[i % slots, h][:1])
+            mixed = matmul(mixers[i, h], weights.astype(jnp.bfloat16))
+            span = slice(h * dim, (h + 1) * dim)
+            gated[i, span, :] = (
+                mixed[:dim] * (1.0 / mixed[dim : dim + 1]) * gates[i, span, :]
+            ).astype(jnp.bfloat16)
+
+    score_row(0)
+    for i in range(step_rows):
+        if i + 1 < step_rows:
+            score_row(i + 1)
+        mix_row(i)
+    for i in range(step_rows):
+        fresh = x_ref[i].astype(jnp.float32) + matmul(tri_w, gated[i])
+        out_ref[i] = fresh.astype(jnp.bfloat16)
+    for i in range(step_rows):
+        merge_norm = normed_rows(out_ref[i].astype(jnp.float32), gain_ref[...])
         merge_kv = matmul(kv_w, merge_norm).astype(jnp.bfloat16)
         main_query = matmul(query_ref[...], main_ref[i], 1, 1) * dim ** (-0.5)
         product = main_query * merge_kv[:hidden, :].astype(jnp.float32)
@@ -430,6 +435,7 @@
     rows, cols, channels = templ_pair.shape[1:]
     hidden = w_tri_out.shape[0]
     heads = w_bias.shape[1]
+    dim = hidden // heads
     pair_ch = main_pair.shape[-1]
     row_devs, col_devs = lax.axis_size("row"), lax.axis_size("col")
     tiles_per_col = row_devs // col_devs
@@ -503,7 +509,7 @@
     swap = [(c, col_devs - 1 - c) for c in range(col_devs)]
     fars = [lax.ppermute(norm, "col", swap) for norm in norms]
 
-    pack_shape = ((heads + 1) * channels * 0 + heads * channels + 2 * hidden + channels + 2 * hidden, channels)
+    pack_shape = (heads * channels + 2 * hidden + channels + 2 * hidden, channels)
     pack = pl.pallas_call(
         functools.partial(weight_kernel, heads),
         out_shape=jax.ShapeDtypeStruct(pack_shape, bf16),
@@ -550,6 +556,15 @@
             [
                 jax.ShapeDtypeStruct(stored.shape, bf16),
                 jax.ShapeDtypeStruct((piece_rows, hidden + 2 * heads, cols), bf16),
+            ],
+            [
+                pltpu.VMEM((step_rows, col_devs * cols, channels), bf16),
+                pltpu.VMEM((step_rows, heads, channels, cols), bf16),
+                pltpu.VMEM((step_rows, hidden, cols), f32),
+                pltpu.VMEM((step_rows, heads, 2 * dim, col_devs * cols), bf16),
+                pltpu.VMEM((2, heads, col_devs * cols, cols), f32),
+                pltpu.VMEM((2, heads, 8, cols), f32),
+                pltpu.VMEM((step_rows, hidden, cols), bf16),
             ],
             aliases={len(operands): 0} if prior else None,
             cost=6e9,
@@ -605,7 +620,7 @@
 
 
 PIECES = 4
-STEP_ROWS = 4
+STEP_ROWS = 8
 
 
 def takes_fused(templ_pair, main_pair):

time: 122 us -> 87.5 us (0.72)
  Pallas kernels: 87.6 us -> 53.5 us
    pallas_call x4, Pallas kernels: 61.4 us -> 27.1 us  [fused_on_device(): call(functools.partial(attend_kernel, heads), (steps,), specs, [pl.BlockS...]
  transfers between devices with their start and end apart: 12 -> 12, of which waited for: 3 -> 3; matrix products, arithmetic and copies ran while one was open for 2% -> 2% of each run, Pallas kernels for 64% -> 50%
where the time goes in v2:
time: 87.5 us; the launch traced here: 86.7 us
  Pallas kernels  53.5 us (61%)
  starting transfers between devices  17.8 us (20%)
  local copies, waits for them, and re-layouts  10.3 us (12%)
  waiting for transfers between devices  4.34 us (5%)
    pallas_call x4, Pallas kernels, fused_on_device(): call(functools.partial(attend_kernel, heads), (steps,), specs, [pl.BlockS...  27.1 us
    ppermute x4, starting transfers between devices, fused_on_device(): tiles.append(lax.ppermute(bias_tile, ('row', 'col'), perm))  11 us
    unnamed x27, local copies, waits for them, and re-layouts  7.62 us
    pallas_call x2, Pallas kernels, fused_on_device(): call(functools.partial(chip_join_kernel, heads), (1,), [smem, smem, whole...  5.84 us
    pallas_call x2, Pallas kernels, fused_on_device(): call(embed_kernel, (1,), [whole(merged_other), whole(w_merge_out), pl.Blo...  5.49 us
    pallas_call x2, Pallas kernels, fused_on_device(): call(functools.partial(core_join_kernel, heads), (1,), [smem, smem, whole...  5.26 us
    pallas_call x1, Pallas kernels, fused_on_device(): call(functools.partial(norm_kernel, heads), (pieces,), [pl.BlockSpec((pie...  4.77 us
    ppermute x2, starting transfers between devices, fused_on_device(): fars = [lax.ppermute(norm, 'col', swap) for norm in norms]  4.14 us
  transfers between devices with their start and end apart: 12, of which 3 were waited for; matrix products, arithmetic and copies ran while one was open for 2% of the time, Pallas kernels for 50%

profile of v2, /device:TPU:0, one launch (start us, length us, event | category | flops | bytes accessed | tf_op | source)
XLA Modules:
  0.0 86.7 jit_solution(12003860237240889717)
XLA Ops:
  0.6 0.0 copy-start.10
  0.7 0.6 stack.23.idx_ref
  1.3 1.3 %broadcast_in_dim.6.gain_ref = f32[64,128]{1,0:T(8,128)} broadcast(f32[64]{0:T(128)} %param.16), dimensions={0} | broadcast | bytes 33024 | tf_op jit(solution)/shard_map/broadcast_in_dim | solution.py:450
  2.6 4.8 %shard_map.131 = (bf16[32,64,128]{2,1,0:T(8,128)(2,1)}, bf16[32,64,128]{2,1,0:T(8,128)(2,1)}, bf16[4,64,128]{2,1,0:T(8,128)(2,1)}) custom-call(s32[5]{0:T(128)} %stack.23.idx_ref, bf16[64,64,128]{2,1,0:T(8,128)(2,1)} %bitcast.13, f32[64,128]{1,0:T(8,128)} %broadcast_in_dim.6.gain_ref, bf16[4,64]{1,0:T(4,128)(2,1)} %bitcast.18), custom_call_target="tpu_custom_call" | custom-call | flops 1000000 | bytes 1048576 | tf_op jit(solution)/shard_map/pallas_call | solution.py:486
  7.4 3.0 %collective-permute-start.5 = (bf16[32,64,128]{2,1,0:T(8,128)(2,1)}, bf16[32,64,128]{2,1,0:T(8,128)(2,1)S(1)}, u32[]{:S(2)}, u32[]{:S(2)}) collective-permute-start(bf16[32,64,128]{2,1,0:T(8,128)(2,1)} %get-tuple-element.19.own_ref), channel_id=1, source_target_pairs={{0,1},{1,0},{2,3},{3,2},{4,5},{5,4},{6,7},{7,6},{8,9},{9,8},{10,11... | collective-permute-start | bytes 1572872 | tf_op jit(solution)/shard_map/ppermute | solution.py:510
  10.4 5.5 %collective-permute-start.4 = (bf16[4,64,128]{2,1,0:T(8,128)(2,1)}, bf16[4,64,128]{2,1,0:T(8,128)(2,1)S(1)}, u32[]{:S(2)}, u32[]{:S(2)}) collective-permute-start(bf16[4,64,128]{2,1,0:T(8,128)(2,1)} %get-tuple-element.18), channel_id=1, source_target_pairs={{0,6},{1,0},{2,2},{3,4},{4,7},{5,1},{6,3},{7,5},{8,14},{9,8},{10,1... | collective-permute-start | bytes 196616 | tf_op jit(solution)/shard_map/ppermute | solution.py:508
  15.9 0.6 collective-permute-start.3
  16.4 3.4 %collective-permute-start.2 = (bf16[4,64,128]{2,1,0:T(8,128)(2,1)}, bf16[4,64,128]{2,1,0:T(8,128)(2,1)S(1)}, u32[]{:S(2)}, u32[]{:S(2)}) collective-permute-start(bf16[4,64,128]{2,1,0:T(8,128)(2,1)} %get-tuple-element.18), channel_id=1, source_target_pairs={{0,2},{1,4},{2,6},{3,0},{4,3},{5,5},{6,7},{7,1},{8,10},{9,12},{10,... | collective-permute-start | bytes 196616 | tf_op jit(solution)/shard_map/ppermute | solution.py:508
  19.8 1.5 %collective-permute-start.1 = (bf16[4,64,128]{2,1,0:T(8,128)(2,1)}, bf16[4,64,128]{2,1,0:T(8,128)(2,1)S(1)}, u32[]{:S(2)}, u32[]{:S(2)}) collective-permute-start(bf16[4,64,128]{2,1,0:T(8,128)(2,1)} %get-tuple-element.18), channel_id=1, source_target_pairs={{0,0},{1,2},{2,4},{3,6},{4,1},{5,3},{6,5},{7,7},{8,8},{9,10},{10,1... | collective-permute-start | bytes 196616 | tf_op jit(solution)/shard_map/ppermute | solution.py:508
  21.3 1.3 %copy.20.cover_ref = s32[4,2]{1,0:T(4,128)} copy(s32[4,2]{0,1:T(2,128)} %param.14) | data formatting | bytes 64 | tf_op args[2]
  22.7 1.7 %shard_map.133.pack_ref = bf16[576,64]{1,0:T(8,128)(2,1)} custom-call(bf16[64,256]{1,0:T(8,128)(2,1)} %project_ref.1, bf16[64,64]{1,0:T(8,128)(2,1)} %tri_out_ref.1, bf16[64,128]{1,0:T(8,128)(2,1)} %kv_ref.1), custom_call_target="tpu_custom_call" | custom-call | tf_op jit(solution)/shard_map/pallas_call | solution.py:513
  24.3 1.0 %collective-permute-done.4.refs_3_ = bf16[4,64,128]{2,1,0:T(8,128)(2,1)S(1)} collective-permute-done((bf16[4,64,128]{2,1,0:T(8,128)(2,1)}, bf16[4,64,128]{2,1,0:T(8,128)(2,1)S(1)}, u32[]{:S(2)}, u32[]{:S(2)}) %collective-permute-start.4) | collective-permute-done | bytes 65568 | tf_op jit(solution)/shard_map/ppermute | solution.py:508
  25.3 0.0 copy-start.6
  25.3 1.1 %collective-permute-start = (bf16[32,64,128]{2,1,0:T(8,128)(2,1)}, bf16[32,64,128]{2,1,0:T(8,128)(2,1)S(1)}, u32[]{:S(2)}, u32[]{:S(2)}) collective-permute-start(bf16[32,64,128]{2,1,0:T(8,128)(2,1)} %get-tuple-element.17.own_ref), channel_id=1, source_target_pairs={{0,1},{1,0},{2,3},{3,2},{4,5},{5,4},{6,7},{7,6},{8,9},{9,8},{10,11... | collective-permute-start | bytes 1572872 | tf_op jit(solution)/shard_map/ppermute | solution.py:510
  26.4 0.0 collective-permute-done.3.refs_2_
  26.4 0.0 copy-start.7
  26.4 0.0 collective-permute-done.2.refs_1_
  26.5 0.0 copy-start.8
  26.5 0.0 collective-permute-done.1.refs_0_
  26.5 0.0 copy-done.6
  26.5 0.6 copy-done.7
  27.1 0.0 copy-done.8
  27.1 0.0 copy-start.9
  27.1 0.6 copy-done.9
  27.7 3.4 %shard_map.132.bias_ref = f32[4,256,128]{2,1,0:T(8,128)} custom-call(s32[5]{0:T(128)} %stack.23.idx_ref, s32[4,2]{1,0:T(4,128)} %copy.20.cover_ref, s32[2,2]{1,0:T(2,128)} %mask_ref.9, bf16[4,64,128]{2,1,0:T(8,128)(2,1)} %copy-done.9, bf16[4,64,128]{2,1,0:T(8,128)(2,1)} %copy-done.8, bf16[4,64,128]{2,1,0:T(8,128)(2,1)} %copy-done.7, ...), custom_call_target="tpu_custom_call" | custom-call | flops 1000000 | bytes 1048576 | tf_op jit(solution)/shard_map/pallas_call | solution.py:517
  31.1 0.0 collective-permute-done.5.far_ref
  31.1 0.0 copy-start.12
  31.1 0.0 copy-done.10
  31.1 0.8 broadcast_in_dim.7.gain_ref
  31.9 0.0 copy-done.12
  31.9 6.8 %shard_map.134 = (bf16[64,64,128]{2,1,0:T(8,128)(2,1)}, bf16[16,72,128]{2,1,0:T(8,128)(2,1)}) custom-call(s32[5]{0:T(128)} %stack.23.idx_ref, bf16[64,64,128]{2,1,0:T(8,128)(2,1)} %bitcast.14, bf16[32,64,128]{2,1,0:T(8,128)(2,1)} %get-tuple-element.19.own_ref, bf16[32,64,128]{2,1,0:T(8,128)(2,1)} %copy-done.12, bf16[64,128,128]{2,1,0:T(8,128)(2,1)} %main_ref.7, ...), custom_call_target="tpu_custom_call" | custom-call | flops 6000000000 | bytes 1048576 | tf_op jit(solution)/shard_map/pallas_call | solution.py:548
  38.7 0.0 collective-permute-start.8
  38.7 6.8 %shard_map.135 = (bf16[64,64,128]{2,1,0:T(8,128)(2,1)}, bf16[16,72,128]{2,1,0:T(8,128)(2,1)}) custom-call(s32[5]{0:T(128)} %stack.23.idx_ref, bf16[64,64,128]{2,1,0:T(8,128)(2,1)} %bitcast.15, bf16[32,64,128]{2,1,0:T(8,128)(2,1)} %get-tuple-element.19.own_ref, bf16[32,64,128]{2,1,0:T(8,128)(2,1)} %copy-done.12, ...), custom_call_target="tpu_custom_call", output_to_operand_aliasing={{0}: (9, {})} | custom-call | flops 6000000000 | bytes 1048576 | tf_op jit(solution)/shard_map/pallas_call | solution.py:548
  45.5 0.0 collective-permute-done.far_ref
  45.5 0.0 copy-start.11
  45.5 0.8 copy-done.11
  46.3 6.8 %shard_map.136 = (bf16[64,64,128]{2,1,0:T(8,128)(2,1)}, bf16[16,72,128]{2,1,0:T(8,128)(2,1)}) custom-call(s32[5]{0:T(128)} %stack.23.idx_ref, bf16[64,64,128]{2,1,0:T(8,128)(2,1)} %bitcast.16, bf16[32,64,128]{2,1,0:T(8,128)(2,1)} %get-tuple-element.17.own_ref, bf16[32,64,128]{2,1,0:T(8,128)(2,1)} %copy-done.11, ...), custom_call_target="tpu_custom_call", output_to_operand_aliasing={{0}: (9, {})} | custom-call | flops 6000000000 | bytes 1048576 | tf_op jit(solution)/shard_map/pallas_call | solution.py:548
  53.1 0.5 collective-permute-start.6
  53.6 0.0 collective-permute-done.8.other_ref
  53.6 0.0 copy-start.3
  53.6 0.7 copy-done.3
  54.3 2.6 %shard_map.139.own_ref = bf16[16,72,128]{2,1,0:T(8,128)(2,1)} custom-call(s32[5]{0:T(128)} %stack.23.idx_ref, s32[4,2]{1,0:T(4,128)} %copy.20.cover_ref, s32[2,2]{1,0:T(2,128)} %mask_ref.9, bf16[16,72,128]{2,1,0:T(8,128)(2,1)} %get-tuple-element.26.own_ref, bf16[16,72,128]{2,1,0:T(8,128)(2,1)} %copy-done.3), custom_call_target="tpu_custom_call" | custom-call | flops 1000000 | bytes 1048576 | tf_op jit(solution)/shard_map/pallas_call | solution.py:581
  56.9 1.5 %collective-permute-start.9 = (bf16[16,72,128]{2,1,0:T(8,128)(2,1)}, bf16[16,72,128]{2,1,0:T(8,128)(2,1)S(1)}, u32[]{:S(2)}, u32[]{:S(2)}) collective-permute-start(bf16[16,72,128]{2,1,0:T(8,128)(2,1)} %shard_map.139.own_ref), channel_id=1, source_target_pairs={{0,16},{8,24},{16,0},{24,8},{1,17},{9,25},{17,1},{25,9},{2,18},{10... | collective-permute-start | bytes 884744 | tf_op jit(solution)/shard_map/ppermute | solution.py:588
  58.4 6.8 %shard_map.137 = (bf16[64,64,128]{2,1,0:T(8,128)(2,1)}, bf16[16,72,128]{2,1,0:T(8,128)(2,1)}) custom-call(s32[5]{0:T(128)} %stack.23.idx_ref, bf16[64,64,128]{2,1,0:T(8,128)(2,1)} %bitcast.17, bf16[32,64,128]{2,1,0:T(8,128)(2,1)} %get-tuple-element.17.own_ref, bf16[32,64,128]{2,1,0:T(8,128)(2,1)} %copy-done.11, ...), custom_call_target="tpu_custom_call", output_to_operand_aliasing={{0}: (9, {})} | custom-call | flops 6000000000 | bytes 1048576 | tf_op jit(solution)/shard_map/pallas_call | solution.py:548
  65.2 0.0 collective-permute-done.6.other_ref
  65.2 0.0 copy-start.2
  65.2 0.7 copy-done.2
  65.9 2.6 %shard_map.138.own_ref = bf16[16,72,128]{2,1,0:T(8,128)(2,1)} custom-call(s32[5]{0:T(128)} %stack.23.idx_ref, s32[4,2]{1,0:T(4,128)} %copy.20.cover_ref, s32[2,2]{1,0:T(2,128)} %mask_ref.9, bf16[16,72,128]{2,1,0:T(8,128)(2,1)} %get-tuple-element.24.own_ref, bf16[16,72,128]{2,1,0:T(8,128)(2,1)} %copy-done.2), custom_call_target="tpu_custom_call" | custom-call | flops 1000000 | bytes 1048576 | tf_op jit(solution)/shard_map/pallas_call | solution.py:581
  68.5 0.5 collective-permute-start.7
  69.1 0.0 collective-permute-done.9.other_ref
  69.1 0.0 copy-start.1
  69.1 0.7 copy-done.1
  69.8 2.9 %shard_map.140 = (bf16[16,64,128]{2,1,0:T(8,128)(2,1)}, bf16[64,128,128]{2,1,0:T(8,128)(2,1)}) custom-call(s32[5]{0:T(128)} %stack.23.idx_ref, s32[4,2]{1,0:T(4,128)} %copy.20.cover_ref, s32[2,2]{1,0:T(2,128)} %mask_ref.9, bf16[16,72,128]{2,1,0:T(8,128)(2,1)} %shard_map.139.own_ref, bf16[16,72,128]{2,1,0:T(8,128)(2,1)} %copy-done.1, bf16[64,128]{1,0:T(8,128)(2,1)} %w_ref.7), custom_call_target="tpu_custom_call" | custom-call | flops 1000000 | bytes 1048576 | tf_op jit(solution)/shard_map/pallas_call | solution.py:598
  72.7 0.0 collective-permute-start.10
  72.7 1.7 %collective-permute-done.10.merged_ref = bf16[16,64,128]{2,1,0:T(8,128)(2,1)S(1)} collective-permute-done((bf16[16,64,128]{2,1,0:T(8,128)(2,1)}, bf16[16,64,128]{2,1,0:T(8,128)(2,1)S(1)}, u32[]{:S(2)}, u32[]{:S(2)}) %collective-permute-start.10) | collective-permute-done | bytes 262176 | tf_op jit(solution)/shard_map/ppermute | solution.py:610
  74.5 0.7 copy-done.5
  75.2 2.8 %shard_map.141.refs_0_ = bf16[64,128,128]{2,1,0:T(8,128)(2,1)} custom-call(s32[5]{0:T(128)} %stack.23.idx_ref, bf16[16,64,128]{2,1,0:T(8,128)(2,1)} %copy-done.5, bf16[64,128]{1,0:T(8,128)(2,1)} %w_ref.7, bf16[64,128,128]{2,1,0:T(8,128)(2,1)} %get-tuple-element.29.prior_ref), custom_call_target="tpu_custom_call", output_to_operand_aliasing={{}: (3, {})} | custom-call | flops 1000000 | bytes 1048576 | tf_op jit(solution)/shard_map/pallas_call | solution.py:611
  77.9 0.0 collective-permute-done.7.other_ref
  77.9 0.7 copy-done
  78.6 2.9 %shard_map.142 = (bf16[16,64,128]{2,1,0:T(8,128)(2,1)}, bf16[64,128,128]{2,1,0:T(8,128)(2,1)}) custom-call(s32[5]{0:T(128)} %stack.23.idx_ref, s32[4,2]{1,0:T(4,128)} %copy.20.cover_ref, s32[2,2]{1,0:T(2,128)} %mask_ref.9, bf16[16,72,128]{2,1,0:T(8,128)(2,1)} %shard_map.138.own_ref, bf16[16,72,128]{2,1,0:T(8,128)(2,1)} %copy-done, ...), custom_call_target="tpu_custom_call", output_to_operand_aliasing={{1}: (6, {})} | custom-call | flops 1000000 | bytes 1048576 | tf_op jit(solution)/shard_map/pallas_call | solution.py:598
  81.5 0.1 collective-permute-start.11
  81.7 1.6 %collective-permute-done.11.merged_ref = bf16[16,64,128]{2,1,0:T(8,128)(2,1)S(1)} collective-permute-done((bf16[16,64,128]{2,1,0:T(8,128)(2,1)}, bf16[16,64,128]{2,1,0:T(8,128)(2,1)S(1)}, u32[]{:S(2)}, u32[]{:S(2)}) %collective-permute-start.11) | collective-permute-done | bytes 262176 | tf_op jit(solution)/shard_map/ppermute | solution.py:610
  83.3 0.7 copy-done.4
  84.0 2.7 %shard_map.143 = bf16[64,128,128]{2,1,0:T(8,128)(2,1)} custom-call(s32[5]{0:T(128)} %stack.23.idx_ref, bf16[16,64,128]{2,1,0:T(8,128)(2,1)} %copy-done.4, bf16[64,128]{1,0:T(8,128)(2,1)} %w_ref.7, bf16[64,128,128]{2,1,0:T(8,128)(2,1)} %get-tuple-element.31.prior_ref), custom_call_target="tpu_custom_call", output_to_operand_aliasing={{}: (3, {})} | custom-call | flops 1000000 | bytes 1048576 | tf_op jit(solution)/shard_map/pallas_call | solution.py:611
  (3 shorter events, 0.0 us)
Async XLA Ops:
  0.6 30.5 %copy-start.10 = (f32[64]{0:T(128)S(1)}, f32[64]{0:T(128)}, u32[]{:S(2)}) copy-start(f32[64]{0:T(128)} %param.20) | copy-start | bytes 772
  7.4 23.8 %collective-permute-start.5 = (bf16[32,64,128]{2,1,0:T(8,128)(2,1)}, bf16[32,64,128]{2,1,0:T(8,128)(2,1)S(1)}, u32[]{:S(2)}, u32[]{:S(2)}) collective-permute-start(bf16[32,64,128]{2,1,0:T(8,128)(2,1)} %get-tuple-element.19.own_ref), channel_id=1, source_target_pairs={{0,1},{1,0},{2,3},{3,2},{4,5},{5,4},{6,7},{7,6},{8,9},{9,8},{10,11... | collective-permute-start | bytes 1572872 | tf_op jit(solution)/shard_map/ppermute | solution.py:510
  10.4 14.9 %collective-permute-start.4 = (bf16[4,64,128]{2,1,0:T(8,128)(2,1)}, bf16[4,64,128]{2,1,0:T(8,128)(2,1)S(1)}, u32[]{:S(2)}, u32[]{:S(2)}) collective-permute-start(bf16[4,64,128]{2,1,0:T(8,128)(2,1)} %get-tuple-element.18), channel_id=1, source_target_pairs={{0,6},{1,0},{2,2},{3,4},{4,7},{5,1},{6,3},{7,5},{8,14},{9,8},{10,1... | collective-permute-start | bytes 196616 | tf_op jit(solution)/shard_map/ppermute | solution.py:508
  15.9 10.6 %collective-permute-start.3 = (bf16[4,64,128]{2,1,0:T(8,128)(2,1)}, bf16[4,64,128]{2,1,0:T(8,128)(2,1)S(1)}, u32[]{:S(2)}, u32[]{:S(2)}) collective-permute-start(bf16[4,64,128]{2,1,0:T(8,128)(2,1)} %get-tuple-element.18), channel_id=1, source_target_pairs={{0,4},{1,6},{2,0},{3,2},{4,5},{5,7},{6,1},{7,3},{8,12},{9,14},{10,... | collective-permute-start | bytes 196616 | tf_op jit(solution)/shard_map/ppermute | solution.py:508
  16.4 10.0 %collective-permute-start.2 = (bf16[4,64,128]{2,1,0:T(8,128)(2,1)}, bf16[4,64,128]{2,1,0:T(8,128)(2,1)S(1)}, u32[]{:S(2)}, u32[]{:S(2)}) collective-permute-start(bf16[4,64,128]{2,1,0:T(8,128)(2,1)} %get-tuple-element.18), channel_id=1, source_target_pairs={{0,2},{1,4},{2,6},{3,0},{4,3},{5,5},{6,7},{7,1},{8,10},{9,12},{10,... | collective-permute-start | bytes 196616 | tf_op jit(solution)/shard_map/ppermute | solution.py:508
  19.8 6.6 %collective-permute-start.1 = (bf16[4,64,128]{2,1,0:T(8,128)(2,1)}, bf16[4,64,128]{2,1,0:T(8,128)(2,1)S(1)}, u32[]{:S(2)}, u32[]{:S(2)}) collective-permute-start(bf16[4,64,128]{2,1,0:T(8,128)(2,1)} %get-tuple-element.18), channel_id=1, source_target_pairs={{0,0},{1,2},{2,4},{3,6},{4,1},{5,3},{6,5},{7,7},{8,8},{9,10},{10,1... | collective-permute-start | bytes 196616 | tf_op jit(solution)/shard_map/ppermute | solution.py:508
  25.3 1.2 %copy-start.6 = (bf16[4,64,128]{2,1,0:T(8,128)(2,1)}, bf16[4,64,128]{2,1,0:T(8,128)(2,1)S(1)}, u32[]{:S(2)}) copy-start(bf16[4,64,128]{2,1,0:T(8,128)(2,1)S(1)} %collective-permute-done.4.refs_3_) | copy-start | bytes 196612
  25.3 20.2 %collective-permute-start = (bf16[32,64,128]{2,1,0:T(8,128)(2,1)}, bf16[32,64,128]{2,1,0:T(8,128)(2,1)S(1)}, u32[]{:S(2)}, u32[]{:S(2)}) collective-permute-start(bf16[32,64,128]{2,1,0:T(8,128)(2,1)} %get-tuple-element.17.own_ref), channel_id=1, source_target_pairs={{0,1},{1,0},{2,3},{3,2},{4,5},{5,4},{6,7},{7,6},{8,9},{9,8},{10,11... | collective-permute-start | bytes 1572872 | tf_op jit(solution)/shard_map/ppermute | solution.py:510
  26.4 0.6 copy-start.7
  26.5 0.6 copy-start.8
  27.1 0.6 copy-start.9
  31.1 0.8 copy-start.12
  38.7 14.9 %collective-permute-start.8 = (bf16[16,72,128]{2,1,0:T(8,128)(2,1)}, bf16[16,72,128]{2,1,0:T(8,128)(2,1)S(1)}, u32[]{:S(2)}, u32[]{:S(2)}) collective-permute-start(bf16[16,72,128]{2,1,0:T(8,128)(2,1)} %get-tuple-element.27), channel_id=1, source_target_pairs={{0,8},{8,0},{16,24},{24,16},{1,9},{9,1},{17,25},{25,17},{2,10},{10... | collective-permute-start | bytes 884744 | tf_op jit(solution)/shard_map/ppermute | solution.py:580
  45.5 0.8 copy-start.11
  53.1 12.1 %collective-permute-start.6 = (bf16[16,72,128]{2,1,0:T(8,128)(2,1)}, bf16[16,72,128]{2,1,0:T(8,128)(2,1)S(1)}, u32[]{:S(2)}, u32[]{:S(2)}) collective-permute-start(bf16[16,72,128]{2,1,0:T(8,128)(2,1)} %get-tuple-element.25), channel_id=1, source_target_pairs={{0,8},{8,0},{16,24},{24,16},{1,9},{9,1},{17,25},{25,17},{2,10},{10... | collective-permute-start | bytes 884744 | tf_op jit(solution)/shard_map/ppermute | solution.py:580
  53.6 0.7 copy-start.3
  56.9 12.2 %collective-permute-start.9 = (bf16[16,72,128]{2,1,0:T(8,128)(2,1)}, bf16[16,72,128]{2,1,0:T(8,128)(2,1)S(1)}, u32[]{:S(2)}, u32[]{:S(2)}) collective-permute-start(bf16[16,72,128]{2,1,0:T(8,128)(2,1)} %shard_map.139.own_ref), channel_id=1, source_target_pairs={{0,16},{8,24},{16,0},{24,8},{1,17},{9,25},{17,1},{25,9},{2,18},{10... | collective-permute-start | bytes 884744 | tf_op jit(solution)/shard_map/ppermute | solution.py:588
  65.2 0.7 copy-start.2
  68.5 9.4 %collective-permute-start.7 = (bf16[16,72,128]{2,1,0:T(8,128)(2,1)}, bf16[16,72,128]{2,1,0:T(8,128)(2,1)S(1)}, u32[]{:S(2)}, u32[]{:S(2)}) collective-permute-start(bf16[16,72,128]{2,1,0:T(8,128)(2,1)} %shard_map.138.own_ref), channel_id=1, source_target_pairs={{0,16},{8,24},{16,0},{24,8},{1,17},{9,25},{17,1},{25,9},{2,18},{10... | collective-permute-start | bytes 884744 | tf_op jit(solution)/shard_map/ppermute | solution.py:588
  69.1 0.7 copy-start.1
  72.7 1.7 %collective-permute-start.10 = (bf16[16,64,128]{2,1,0:T(8,128)(2,1)}, bf16[16,64,128]{2,1,0:T(8,128)(2,1)S(1)}, u32[]{:S(2)}, u32[]{:S(2)}) collective-permute-start(bf16[16,64,128]{2,1,0:T(8,128)(2,1)} %get-tuple-element.28), channel_id=1, source_target_pairs={{0,8},{8,0},{16,24},{24,16},{1,9},{9,1},{17,25},{25,17},{2,10},{10... | collective-permute-start | bytes 786440 | tf_op jit(solution)/shard_map/ppermute | solution.py:610
  74.5 0.7 copy-start.5
  77.9 0.7 copy-start
  81.5 1.7 %collective-permute-start.11 = (bf16[16,64,128]{2,1,0:T(8,128)(2,1)}, bf16[16,64,128]{2,1,0:T(8,128)(2,1)S(1)}, u32[]{:S(2)}, u32[]{:S(2)}) collective-permute-start(bf16[16,64,128]{2,1,0:T(8,128)(2,1)} %get-tuple-element.30), channel_id=1, source_target_pairs={{0,8},{8,0},{16,24},{24,16},{1,9},{9,1},{17,25},{25,17},{2,10},{10... | collective-permute-start | bytes 786440 | tf_op jit(solution)/shard_map/ppermute | solution.py:610
  83.3 0.7 copy-start.4

commit v3 on v2

--- a/solution.py
+++ b/solution.py
@@ -198,15 +198,16 @@
     return (center * lax.rsqrt(spread + EPSILON) * gain).astype(jnp.bfloat16)
 
 
-def piece_block(idx_ref, piece, pieces):
+def piece_of(piece, idx_ref, pieces):
     half = idx_ref[0]
-    side = half if piece % 2 else 1 - half
+    odd = lax.rem(piece, 2)
+    side = odd * half + (1 - odd) * (1 - half)
     return side * (pieces // 2) + piece // 2
 
 
 def mask_shift(cover_ref, mask_ref, templ, row_block, col_block):
     valid = (
-        cover_ref[templ, row_block] * cover_ref[templ, col_block] * mask_ref[row_block, col_block]
+        cover_ref[row_block, templ] * cover_ref[col_block, templ] * mask_ref[row_block, col_block]
     )
     return MASK_SHIFT * (valid.astype(jnp.float32) - 1.0)
 
@@ -217,26 +218,41 @@
     )
 
 
-def norm_kernel(
-    heads, idx_ref, x_ref, gain_ref, bias_w_ref, *refs
-):
+def widened(row_ref, cols):
+    return jnp.broadcast_to(row_ref[...], (cols, row_ref.shape[1])).T
+
+
+def norm_kernel(heads, idx_ref, x_ref, gain_ref, bias_w_ref, *refs):
     piece = pl.program_id(0)
-    *norm_refs, bias_ref, held = refs
-    for chunk, norm_ref in enumerate(norm_refs):
+    *kept_refs, bias_ref, held, wide = refs
+    norm_refs, raw_refs = kept_refs[::2], kept_refs[1::2]
+
+    @pl.when(piece == 0)
+    def _():
+        wide[...] = widened(gain_ref, wide.shape[1])
+
+    step_rows = x_ref.shape[0]
+    for chunk, (norm_ref, raw_ref) in enumerate(zip(norm_refs, raw_refs)):
 
         @pl.when(piece // 2 == chunk)
         def _():
-            for i in range(x_ref.shape[0]):
-                normed = normed_rows(x_ref[i].astype(jnp.float32), gain_ref[...])
-                norm_ref[i] = normed
-                row_bias = matmul(bias_w_ref[...], normed)
+            base = (piece - 2 * chunk) * step_rows
+            for i in range(step_rows):
+                raw_ref[base + i] = x_ref[i]
+                norm_ref[base + i] = normed_rows(x_ref[i].astype(jnp.float32), wide[...])
+            cols = x_ref.shape[2]
+            wide_norm = jnp.concatenate([norm_ref[base + i] for i in range(step_rows)], axis=1)
+            wide_bias = matmul(bias_w_ref[...], wide_norm)
+            for i in range(step_rows):
                 for head in range(heads):
-                    held[head, i : i + 1, :] = row_bias[head : head + 1, :]
-
-    bias_ref[...] = held[...].astype(jnp.bfloat16)
-
-
-def weight_kernel(heads, project_ref, tri_out_ref, kv_ref, pack_ref):
+                    held[head, i : i + 1, :] = wide_bias[head : head + 1, i * cols : (i + 1) * cols]
+
+    first = pl.multiple_of(piece_of(piece, idx_ref, pl.num_programs(0)) * step_rows, step_rows)
+    bias_ref[:, pl.ds(first, step_rows), :] = held[...].astype(jnp.bfloat16)
+
+
+def weight_kernel(heads, idx_ref, project_ref, tri_out_ref, kv_ref, gain_ref, pack_ref, wide_ref):
+    wide_ref[...] = widened(gain_ref, wide_ref.shape[1])
     channels = project_ref.shape[0]
     hidden = tri_out_ref.shape[0]
     dim = hidden // heads
@@ -261,38 +277,88 @@
         row += flipped.shape[0]
 
 
-def bias_kernel(tiles_per_col, row_devs, idx_ref, cover_ref, mask_ref, *refs):
+def when_held(idx_ref, column, part, tile_refs, tiles_per_col, act):
+    wanted = idx_ref[2] ^ (tiles_per_col * column + part)
+    for turn, tile_ref in enumerate(tile_refs):
+
+        @pl.when(wanted == turn)
+        def _():
+            act(tile_ref)
+
+
+def pick_kernel(idx_ref, *refs):
+    *tile_refs, _, _, out_ref = refs
+    for part in range(out_ref.shape[0]):
+
+        def act(tile_ref, part=part):
+            out_ref[part] = tile_ref[...]
+
+        when_held(idx_ref, 1 - idx_ref[3], part, tile_refs, out_ref.shape[0], act)
+
+
+def relative_shift(idx_ref, cover_ref, mask_ref, block):
+    shifts = [mask_shift(cover_ref, mask_ref, idx_ref[1], idx_ref[4], b) for b in (block, 1 - block)]
+    return shifts[0] - jnp.maximum(*shifts)
+
+
+def place_bias(out_ref, part, tile, shift):
+    heads, tile_rows, _ = tile.shape
+    for head in range(heads):
+        flipped = tile[head].astype(jnp.float32).T
+        out_ref[head, :, part * tile_rows : (part + 1) * tile_rows] = (flipped + shift) * LOG2E
+
+
+def own_bias_kernel(idx_ref, cover_ref, mask_ref, *refs):
     *tile_refs, out_ref = refs
-    heads, tile_rows, cols = tile_refs[0].shape
-    templ, row_dev, col_dev, row_block = idx_ref[1], idx_ref[2], idx_ref[3], idx_ref[4]
-    col_devs = row_devs // tiles_per_col
-    best = jnp.float32(-MASK_SHIFT)
-    for block in range(col_devs):
-        best = jnp.maximum(best, mask_shift(cover_ref, mask_ref, templ, row_block, block))
-    for turn, tile_ref in enumerate(tile_refs):
-        source = lax.rem(row_dev - turn + row_devs, row_devs)
-        for place in range(row_devs):
-            part, block = place // col_devs, place % col_devs
-
-            @pl.when(source == place)
-            def _():
-                slot = lax.rem(block - col_dev + col_devs, col_devs)
-                shift = mask_shift(cover_ref, mask_ref, templ, row_block, block) - best
-                for head in range(heads):
-                    flipped = tile_ref[head].astype(jnp.float32).T
-                    out_ref[
-                        head,
-                        pl.ds(slot * cols, cols),
-                        part * tile_rows : (part + 1) * tile_rows,
-                    ] = (flipped + shift) * LOG2E
+    tiles_per_col = out_ref.shape[2] // tile_refs[0].shape[1]
+    shift = relative_shift(idx_ref, cover_ref, mask_ref, idx_ref[3])
+    for part in range(tiles_per_col):
+
+        def act(tile_ref, part=part):
+            place_bias(out_ref, part, tile_ref[...], shift)
+
+        when_held(idx_ref, idx_ref[3], part, tile_refs, tiles_per_col, act)
+
+
+def far_bias_kernel(idx_ref, cover_ref, mask_ref, tiles_ref, out_ref):
+    shift = relative_shift(idx_ref, cover_ref, mask_ref, 1 - idx_ref[3])
+    for part in range(tiles_ref.shape[0]):
+        place_bias(out_ref, part, tiles_ref[part], shift)
+
+
+def query_kernel(scale, idx_ref, main_ref, w_ref, out_ref):
+    step_rows, cols, pair_ch = main_ref.shape
+    base = pl.program_id(0) * step_rows
+    wide = matmul(w_ref[...], main_ref[...].reshape(step_rows * cols, pair_ch), 1, 1) * scale
+    for i in range(step_rows):
+        out_ref[base + i] = wide[:, i * cols : (i + 1) * cols]
 
 
 def attend_kernel(
-    heads, idx_ref, x_ref, own_ref, far_ref, main_ref, bias_ref, pack_ref, query_ref, gain_ref, *refs
+    heads,
+    skip,
+    query_skip,
+    x_ref,
+    own_ref,
+    far_ref,
+    main_query,
+    own_bias_ref,
+    far_bias_ref,
+    pack_ref,
+    gain_ref,
+    after_ref,
+    out_ref,
+    state_ref,
+    turned,
+    probes,
+    gates,
+    mixers,
+    held,
+    tops,
+    gated,
 ):
-    out_ref, state_ref, turned, probes, gates, mixers, held, tops, gated = refs[-9:]
-    step_rows, channels, cols = x_ref.shape
-    hidden = query_ref.shape[0]
+    step_rows, channels, cols = out_ref.shape
+    hidden = main_query.shape[1]
     dim = hidden // heads
     row = heads * channels + hidden
     first_w = pack_ref[:row, :]
@@ -300,8 +366,8 @@
     tri_w = pack_ref[row + hidden : row + hidden + channels, :]
     kv_w = pack_ref[row + hidden + channels :, :]
     for i in range(step_rows):
-        own = own_ref[i]
-        both = jnp.concatenate([own, far_ref[i]], axis=1)
+        own = own_ref[skip + i]
+        both = jnp.concatenate([own, far_ref[skip + i]], axis=1)
         first = matmul(first_w, own)
         for h in range(heads):
             probes[i, h] = first[h * channels : (h + 1) * channels, :].astype(jnp.bfloat16)
@@ -316,11 +382,13 @@
 
     def score_row(i):
         for h in range(heads):
-            scores = matmul(turned[i], probes[i, h]) + bias_ref[h]
-            held[i % slots, h] = scores
-            tops[i % slots, h] = jnp.broadcast_to(
-                jnp.max(scores, axis=0, keepdims=True), tops.shape[2:]
-            )
+            scores = matmul(turned[i], probes[i, h])
+            near = scores[:cols] + own_bias_ref[h]
+            other = scores[cols:] + far_bias_ref[h]
+            held[i % slots, h, :cols] = near
+            held[i % slots, h, cols:] = other
+            highest = jnp.max(jnp.maximum(near, other), axis=0, keepdims=True)
+            tops[i % slots, h] = jnp.broadcast_to(highest, tops.shape[2:])
 
     def mix_row(i):
         for h in range(heads):
@@ -337,13 +405,12 @@
             score_row(i + 1)
         mix_row(i)
     for i in range(step_rows):
-        fresh = x_ref[i].astype(jnp.float32) + matmul(tri_w, gated[i])
+        fresh = x_ref[skip + i].astype(jnp.float32) + matmul(tri_w, gated[i])
         out_ref[i] = fresh.astype(jnp.bfloat16)
     for i in range(step_rows):
         merge_norm = normed_rows(out_ref[i].astype(jnp.float32), gain_ref[...])
         merge_kv = matmul(kv_w, merge_norm).astype(jnp.bfloat16)
-        main_query = matmul(query_ref[...], main_ref[i], 1, 1) * dim ** (-0.5)
-        product = main_query * merge_kv[:hidden, :].astype(jnp.float32)
+        product = main_query[query_skip + i] * merge_kv[:hidden, :].astype(jnp.float32)
         score = jnp.concatenate(
             [
                 jnp.sum(product[h * dim : (h + 1) * dim, :], axis=0, keepdims=True)
@@ -410,22 +477,33 @@
         store_state(state_ref, i, values.astype(jnp.bfloat16), score)
 
 
-def chip_join_kernel(
-    heads, idx_ref, cover_ref, mask_ref, own_ref, other_ref, w_ref, *refs
-):
-    merged_ref, out_ref = refs[-2:]
+def chip_join_kernel(heads, idx_ref, cover_ref, mask_ref, own_ref, other_ref, _, merged_ref):
     _, _, best, far_best = pair_shifts(idx_ref, cover_ref, mask_ref)
     top = jnp.maximum(best, far_best)
     for i in range(own_ref.shape[0]):
         values, _ = joined(heads, own_ref, other_ref, i, best - top, far_best - top)
-        merged = values.astype(jnp.bfloat16)
-        merged_ref[i] = merged
-        out_ref[i] = matmul(merged, w_ref[...], 0, 0).astype(jnp.bfloat16)
-
-
-def embed_kernel(idx_ref, merged_ref, w_ref, prior_ref, out_ref):
+        merged_ref[i] = values.astype(jnp.bfloat16)
+
+
+def embed_rows(merged_ref, w_ref, out_ref):
     for i in range(merged_ref.shape[0]):
         out_ref[i] = matmul(merged_ref[i], w_ref[...], 0, 0).astype(jnp.bfloat16)
+
+
+def embed_kernel(idx_ref, merged_ref, w_ref, prior_ref, out_ref):
+    embed_rows(merged_ref, w_ref, out_ref)
+
+
+def finish_kernel(idx_ref, *refs):
+    *row_refs, other_ref, own_ref, w_ref, fresh_ref, out_ref, token_ref = refs
+    token_ref[...] = jnp.zeros_like(token_ref)
+    for piece, row_ref in enumerate(row_refs):
+
+        @pl.when(pl.program_id(0) == piece)
+        def _():
+            fresh_ref[...] = row_ref[...]
+            if piece < 2:
+                embed_rows((other_ref, own_ref)[piece], w_ref, out_ref)
 
 
 def fused_on_device(
@@ -447,13 +525,19 @@
     steps = piece_rows // step_rows
     stored = jnp.swapaxes(templ_pair[0], 1, 2)
     bf16, f32 = jnp.bfloat16, jnp.float32
-    tri_gain_wide = jnp.broadcast_to(tri_gain[:, None], (channels, cols))
-    merge_gain_wide = jnp.broadcast_to(merge_gain[:, None], (channels, cols))
+    def in_hbm(array):
+        return pltpu.with_memory_space_constraint(array, pltpu.HBM)
+
+    gain_row = in_hbm(tri_gain[None, :])
+    cover = coverage.T
+    stored, main_pair = in_hbm(stored), in_hbm(main_pair)
 
     def whole(array):
         return pl.BlockSpec(array.shape, lambda *_: (0,) * array.ndim)
 
     smem = pl.BlockSpec(memory_space=pltpu.SMEM)
+    vmem = pl.BlockSpec(memory_space=pltpu.VMEM)
+    anywhere = pl.BlockSpec(memory_space=pl.ANY)
 
     def call(kernel, grid, in_specs, out_specs, out_shape, scratch=(), aliases=None, cost=1e6):
         return pl.pallas_call(
@@ -467,159 +551,187 @@
             cost_estimate=pl.CostEstimate(
                 flops=int(cost), bytes_accessed=1 << 20, transcendentals=0
             ),
+            compiler_params=pltpu.CompilerParams(vmem_limit_bytes=VMEM_GRANT),
         )
 
     chunks = pieces // 2
 
-    def piece_of(p, idx_ref):
-        half = idx_ref[0]
-        side = jnp.where(p % 2 == 1, half, 1 - half)
-        return side * (pieces // 2) + p // 2
-
-    norm_specs = [
-        pl.BlockSpec(
-            (piece_rows, channels, cols),
-            functools.partial(lambda c, p, s: (jnp.clip(p - 2 * c, 0, 1), 0, 0), chunk),
-        )
-        for chunk in range(chunks)
-    ]
-    *norms, bias_tile = call(
+    *kept_rows, bias_tile = call(
         functools.partial(norm_kernel, heads),
         (pieces,),
         [
-            pl.BlockSpec((piece_rows, channels, cols), lambda p, s: (piece_of(p, s), 0, 0)),
-            whole(tri_gain_wide),
+            pl.BlockSpec((piece_rows, channels, cols), lambda p, s: (piece_of(p, s, pieces), 0, 0)),
+            whole(gain_row),
             pl.BlockSpec((heads, channels), lambda *_: (0, 0)),
         ],
-        norm_specs + [pl.BlockSpec((heads, piece_rows, cols), lambda p, s: (0, piece_of(p, s), 0))],
-        [jax.ShapeDtypeStruct((2 * piece_rows, channels, cols), bf16)] * chunks
+        [vmem] * (2 * chunks + 1),
+        [jax.ShapeDtypeStruct((2 * piece_rows, channels, cols), bf16)] * (2 * chunks)
         + [jax.ShapeDtypeStruct((heads, rows, cols), bf16)],
-        [pltpu.VMEM((heads, piece_rows, cols), f32)],
-    )(idx, stored, tri_gain_wide, w_bias.T)
-
-    tiles = []
-    for turn in range(row_devs):
-        perm = []
-        for source_row in range(row_devs):
-            for source_col in range(col_devs):
-                place = (source_row % tiles_per_col) * col_devs + source_col
-                target = ((place + turn) % row_devs) * col_devs + source_row // tiles_per_col
-                perm.append((source_row * col_devs + source_col, target))
-        tiles.append(lax.ppermute(bias_tile, ("row", "col"), perm))
+        [pltpu.VMEM((heads, piece_rows, cols), f32), pltpu.VMEM((channels, cols), f32)],
+    )(idx, stored, gain_row, in_hbm(w_bias.T))
+    norms, raws = kept_rows[::2], kept_rows[1::2]
+
+
+    def plain_call(kernel, in_specs, out_shape, scratch=(), cost=1e6):
+        return pl.pallas_call(
+            kernel,
+            in_specs=in_specs,
+            out_specs=jax.tree.map(lambda _: vmem, out_shape),
+            out_shape=out_shape,
+            scratch_shapes=list(scratch),
+            cost_estimate=pl.CostEstimate(
+                flops=int(cost), bytes_accessed=1 << 20, transcendentals=0
+            ),
+            compiler_params=pltpu.CompilerParams(vmem_limit_bytes=VMEM_GRANT),
+        )
+
+    tiles = [bias_tile]
+    for turn in range(1, row_devs):
+        perm = [(z, z ^ turn) for z in range(row_devs)]
+        tiles.append(lax.ppermute(bias_tile, "row", perm))
     swap = [(c, col_devs - 1 - c) for c in range(col_devs)]
-    fars = [lax.ppermute(norm, "col", swap) for norm in norms]
-
+    fars = [lax.ppermute(norms[0], "col", swap)]
     pack_shape = (heads * channels + 2 * hidden + channels + 2 * hidden, channels)
-    pack = pl.pallas_call(
-        functools.partial(weight_kernel, heads),
-        out_shape=jax.ShapeDtypeStruct(pack_shape, bf16),
-    )(w_project, w_tri_out, w_merge_kv)
-    bias = call(
-        functools.partial(bias_kernel, tiles_per_col, row_devs),
-        (1,),
-        [smem, smem] + [whole(t) for t in tiles],
-        pl.BlockSpec((heads, col_devs * cols, cols), lambda *_: (0, 0, 0)),
-        jax.ShapeDtypeStruct((heads, col_devs * cols, cols), f32),
-    )(idx, coverage, pair_mask, *tiles)
-
-    query_w = w_merge_q.T
-    out = None
-    states = []
+    raw_weights = [in_hbm(w) for w in (w_project, w_tri_out, w_merge_kv, merge_gain[None, :])]
+    packed_shapes = [
+        jax.ShapeDtypeStruct(pack_shape, bf16),
+        jax.ShapeDtypeStruct((channels, cols), f32),
+    ]
+    with jax.named_scope("pack"):
+        pack, merge_gain_wide = call(
+            functools.partial(weight_kernel, heads),
+            (1,),
+            [whole(w) for w in raw_weights],
+            [vmem] * len(packed_shapes),
+            packed_shapes,
+        )(idx, *raw_weights)
+    query_w = in_hbm(w_merge_q.T)
+    query_w = in_hbm(w_merge_q.T)
+    with jax.named_scope("query"):
+        main_query = call(
+            functools.partial(query_kernel, dim ** (-0.5)),
+            (pieces,),
+            [
+                pl.BlockSpec(
+                    (piece_rows, cols, pair_ch),
+                    lambda g, s: (piece_of(g, s, pieces), 0, 0),
+                ),
+                whole(query_w),
+            ],
+            vmem,
+            jax.ShapeDtypeStruct((rows, hidden, cols), f32),
+        )(idx, main_pair, query_w)
+    picked = plain_call(
+        pick_kernel,
+        [smem] + [vmem] * row_devs + [anywhere] * 2,
+        jax.ShapeDtypeStruct((tiles_per_col,) + bias_tile.shape, bf16),
+    )(idx, *tiles, pack, main_query)
+    far_tiles = lax.ppermute(picked, "col", swap)
+    half_shape = jax.ShapeDtypeStruct((heads, cols, cols), f32)
+    own_bias = plain_call(own_bias_kernel, [smem] * 3 + [vmem] * row_devs, half_shape)(
+        idx, cover, pair_mask, *tiles
+    )
+    far_bias = plain_call(far_bias_kernel, [smem] * 3 + [vmem], half_shape)(
+        idx, cover, pair_mask, far_tiles
+    )
+    fars += [lax.ppermute(norm, "col", swap) for norm in norms[1:]]
+
+    fresh, states, pair_states = [], [], []
+    after = far_bias
+    cores = [(t, t + 1 - 2 * (t % 2)) for t in range(lax.axis_size("tmpl"))]
+    chips = [(t, (t + 2) % 4) for t in range(lax.axis_size("tmpl"))]
+    state_shape = jax.ShapeDtypeStruct((piece_rows, hidden + 2 * heads, cols), bf16)
     for piece in range(pieces):
         chunk, side = piece // 2, piece % 2
-
-        def at_rows(g, s, piece=piece):
-            return (piece_block(s, piece, pieces) * steps + g, 0, 0)
-
-        def at_norm(g, s, side=side):
-            return (side * steps + g, 0, 0)
-
-        prior = [] if out is None else [out]
-        operands = [
-            stored, norms[chunk], fars[chunk], main_pair, bias, pack, query_w, merge_gain_wide
-        ] + prior
-        specs = [
-            pl.BlockSpec((step_rows, channels, cols), at_rows),
-            pl.BlockSpec((step_rows, channels, cols), at_norm),
-            pl.BlockSpec((step_rows, channels, cols), at_norm),
-            pl.BlockSpec((step_rows, cols, pair_ch), at_rows),
-            whole(bias), whole(pack), whole(query_w), whole(merge_gain_wide),
-        ] + [pl.BlockSpec(memory_space=pl.ANY)] * len(prior)
-        out, state = call(
-            functools.partial(attend_kernel, heads),
-            (steps,),
-            specs,
-            [
-                pl.BlockSpec((step_rows, channels, cols), at_rows),
-                pl.BlockSpec((step_rows, hidden + 2 * heads, cols), lambda g, s: (g, 0, 0)),
-            ],
-            [
-                jax.ShapeDtypeStruct(stored.shape, bf16),
-                jax.ShapeDtypeStruct((piece_rows, hidden + 2 * heads, cols), bf16),
-            ],
-            [
-                pltpu.VMEM((step_rows, col_devs * cols, channels), bf16),
-                pltpu.VMEM((step_rows, heads, channels, cols), bf16),
-                pltpu.VMEM((step_rows, hidden, cols), f32),
-                pltpu.VMEM((step_rows, heads, 2 * dim, col_devs * cols), bf16),
-                pltpu.VMEM((2, heads, col_devs * cols, cols), f32),
-                pltpu.VMEM((2, heads, 8, cols), f32),
-                pltpu.VMEM((step_rows, hidden, cols), bf16),
-            ],
-            aliases={len(operands): 0} if prior else None,
-            cost=6e9,
-        )(idx, *operands)
+        with jax.named_scope("attend%d" % piece):
+            rows_out, state = plain_call(
+                functools.partial(attend_kernel, heads, side * piece_rows, piece * piece_rows),
+                [vmem] * 8 + [anywhere],
+                [jax.ShapeDtypeStruct((piece_rows, channels, cols), bf16), state_shape],
+                [
+                    pltpu.VMEM((piece_rows, col_devs * cols, channels), bf16),
+                    pltpu.VMEM((piece_rows, heads, channels, cols), bf16),
+                    pltpu.VMEM((piece_rows, hidden, cols), f32),
+                    pltpu.VMEM((piece_rows, heads, 2 * dim, col_devs * cols), bf16),
+                    pltpu.VMEM((2, heads, col_devs * cols, cols), f32),
+                    pltpu.VMEM((2, heads, 8, cols), f32),
+                    pltpu.VMEM((piece_rows, hidden, cols), bf16),
+                ],
+                6e9,
+            )(
+                raws[chunk], norms[chunk], fars[chunk], main_query, own_bias, far_bias, pack,
+                merge_gain_wide, after,
+            )
+        fresh.append(rows_out)
         states.append(state)
-
-    cores = [(t, t + 1 - 2 * (t % 2)) for t in range(lax.axis_size("tmpl"))]
-    chips = [(t, (t + 2) % 4) for t in range(lax.axis_size("tmpl"))]
-    emb = None
+        after = state
+        if side:
+            with jax.named_scope("corejoin%d" % chunk):
+                after = plain_call(
+                    functools.partial(core_join_kernel, heads),
+                    [smem] * 3 + [vmem] * 2,
+                    state_shape,
+                )(idx, cover, pair_mask, state, swapped)
+            pair_states.append(after)
+        else:
+            with jax.named_scope("coreswap%d" % chunk):
+                swapped = lax.ppermute(state, "tmpl", cores)
+
     emb_shape = jax.ShapeDtypeStruct(main_pair.shape, bf16)
+    token = pair_states[-1]
+    token_shape = jax.ShapeDtypeStruct((8, cols), f32)
+    merged_shape = jax.ShapeDtypeStruct((piece_rows, hidden, cols), bf16)
     for chunk in range(chunks):
-        sent, kept = states[2 * chunk], states[2 * chunk + 1]
-        other = lax.ppermute(sent, "tmpl", cores)
-        pair_state = call(
-            functools.partial(core_join_kernel, heads),
-            (1,),
-            [smem, smem, whole(kept), whole(other)],
-            whole(kept),
-            jax.ShapeDtypeStruct(kept.shape, bf16),
-        )(idx, coverage, pair_mask, kept, other)
-        far_state = lax.ppermute(pair_state, "tmpl", chips)
-
-        def at_own(g, s, piece=2 * chunk + 1):
-            return (piece_block(s, piece, pieces), 0, 0)
-
-        def at_other(g, s, piece=2 * chunk):
-            return (piece_block(s, piece, pieces), 0, 0)
-
-        prior = [] if emb is None else [emb]
-        operands = [coverage, pair_mask, pair_state, far_state, w_merge_out] + prior
-        merged, emb = call(
-            functools.partial(chip_join_kernel, heads),
-            (1,),
-            [smem, smem, whole(pair_state), whole(far_state), whole(w_merge_out)]
-            + [pl.BlockSpec(memory_space=pl.ANY)] * len(prior),
-            [
-                pl.BlockSpec((piece_rows, hidden, cols), lambda *_: (0, 0, 0)),
-                pl.BlockSpec((piece_rows, cols, pair_ch), at_own),
-            ],
-            [jax.ShapeDtypeStruct((piece_rows, hidden, cols), bf16), emb_shape],
-            aliases={len(operands): 1} if prior else None,
-        )(idx, *operands)
-        merged_other = lax.ppermute(merged, "tmpl", cores)
-        emb = call(
-            embed_kernel,
-            (1,),
-            [whole(merged_other), whole(w_merge_out), pl.BlockSpec(memory_space=pl.ANY)],
-            pl.BlockSpec((piece_rows, cols, pair_ch), at_other),
-            emb_shape,
-            aliases={3: 0},
-        )(idx, merged_other, w_merge_out, emb)
+        pair_state = pair_states[chunk]
+        with jax.named_scope("chipswap%d" % chunk):
+            far_state = lax.ppermute(pair_state, "tmpl", chips)
+        with jax.named_scope("chipjoin%d" % chunk):
+            merged = plain_call(
+                functools.partial(chip_join_kernel, heads),
+                [smem] * 3 + [vmem] * 2 + [anywhere],
+                merged_shape,
+            )(idx, cover, pair_mask, pair_state, far_state, token)
+        with jax.named_scope("lastswap%d" % chunk):
+            merged_other = lax.ppermute(merged, "tmpl", cores)
+
+        def at_piece(piece):
+            return lambda g, s: (piece_of(piece, s, pieces), 0, 0)
+
+        if chunk == 0:
+            with jax.named_scope("finish"):
+                out, emb, token = call(
+                    finish_kernel,
+                    (pieces,),
+                    [vmem] * (pieces + 3),
+                    [
+                        pl.BlockSpec(
+                            (piece_rows, channels, cols),
+                            lambda g, s: (piece_of(g, s, pieces), 0, 0),
+                        ),
+                        pl.BlockSpec(
+                            (piece_rows, cols, pair_ch),
+                            lambda g, s: (piece_of(jnp.minimum(g, 1), s, pieces), 0, 0),
+                        ),
+                        vmem,
+                    ],
+                    [jax.ShapeDtypeStruct(stored.shape, bf16), emb_shape, token_shape],
+                )(idx, *fresh, merged_other, merged, w_merge_out)
+        else:
+            for piece, part in ((2 * chunk + 1, merged), (2 * chunk, merged_other)):
+                with jax.named_scope("embed%d" % piece):
+                    emb = call(
+                        embed_kernel,
+                        (1,),
+                        [vmem, vmem, anywhere],
+                        pl.BlockSpec((piece_rows, cols, pair_ch), at_piece(piece)),
+                        emb_shape,
+                        aliases={3: 0},
+                    )(idx, part, w_merge_out, emb)
     return (jnp.swapaxes(out, 1, 2)[None], emb)
 
 
 PIECES = 4
+VMEM_GRANT = 16 << 20
 STEP_ROWS = 8
 
 
@@ -631,6 +743,7 @@
         and col_devs == 2
         and cols == BLOCK
         and BLOCK % rows == 0
+        and row_devs & (row_devs - 1) == 0
         and row_devs % col_devs == 0
         and rows * (row_devs // col_devs) == cols
         and rows % (PIECES * STEP_ROWS) == 0

time: 87.5 us -> 57 us (0.65)
  Pallas kernels: 53.5 us -> 35 us
  local copies, waits for them, and re-layouts: 10.3 us -> 0.1 us
  starting transfers between devices: 17.8 us -> 12.2 us
  waiting for transfers between devices: 4.34 us -> 8.57 us
    pallas_call x12 -> x16, Pallas kernels: 48.7 us -> 31.3 us  [the longest x4 14.1 us: fused_on_device(): plain_call(functools.partial(attend_kernel, heads, side * piece_rows, pie...]
    unnamed x27 -> x6, local copies, waits for them, and re-layouts: 7.62 us -> 0.02 us
    ppermute x8, starting transfers between devices: 15.6 us -> 9.9 us  [the longest x3 4.39 us: fused_on_device(): tiles.append(lax.ppermute(bias_tile, 'row', perm))]
    ppermute x2, waiting for transfers between devices: 0.01 us -> 3.28 us  [fused_on_device(): far_state = lax.ppermute(pair_state, 'tmpl', chips)]
    ppermute x8, waiting for transfers between devices: 0.98 us -> 3.78 us  [the longest x1 3.18 us: fused_on_device(): far_tiles = lax.ppermute(picked, 'col', swap)]
    broadcast_in_dim x2 -> x0, local copies, waits for them, and re-layouts: 2.13 us -> none  [the longest x1 1.33 us: fused_on_device(): tri_gain_wide = jnp.broadcast_to(tri_gain[:, None], (channels, cols))]
    ppermute x2, waiting for transfers between devices: 3.36 us -> 1.51 us  [fused_on_device(): merged_other = lax.ppermute(merged, 'tmpl', cores)]
    pallas_call x1, Pallas kernels: 4.77 us -> 3.66 us  [fused_on_device(): call(functools.partial(norm_kernel, heads), (pieces,), [pl.BlockSpec((pie...]
  transfers between devices with their start and end apart: 12 -> 12, of which waited for: 3 -> 4; matrix products, arithmetic and copies ran while one was open for 2% -> 0% of each run, Pallas kernels for 50% -> 51%
where the time goes in v3:
time: 57 us; the launch traced here: 56.7 us
  Pallas kernels  35 us (61%)
  starting transfers between devices  12.2 us (21%)
  waiting for transfers between devices  8.57 us (15%)
  between operations  0.82 us (1%)
    pallas_call x4, Pallas kernels, fused_on_device(): plain_call(functools.partial(attend_kernel, heads, side * piece_rows, pie...  14.1 us
    ppermute x3, starting transfers between devices, fused_on_device(): tiles.append(lax.ppermute(bias_tile, 'row', perm))  4.39 us
    pallas_call x1, Pallas kernels, fused_on_device(): call(functools.partial(norm_kernel, heads), (pieces,), [pl.BlockSpec((pie...  3.66 us
    pallas_call x1, Pallas kernels, fused_on_device(): call(functools.partial(query_kernel, dim ** (-0.5)), (pieces,), [pl.Block...  3.65 us
    pallas_call x2, Pallas kernels, fused_on_device(): call(embed_kernel, (1,), [vmem, vmem, anywhere], pl.BlockSpec((piece_rows...  3.35 us
    ppermute x2, waiting for transfers between devices, fused_on_device(): far_state = lax.ppermute(pair_state, 'tmpl', chips)  3.28 us
    ppermute x1, waiting for transfers between devices, fused_on_device(): far_tiles = lax.ppermute(picked, 'col', swap)  3.18 us
    ppermute x1, starting transfers between devices, fused_on_device(): fars = [lax.ppermute(norms[0], 'col', swap)]  3.06 us
  transfers between devices with their start and end apart: 12, of which 4 were waited for; matrix products, arithmetic and copies ran while one was open for 0% of the time, Pallas kernels for 51%

profile of v3, /device:TPU:0, one launch (start us, length us, event | category | flops | bytes accessed | tf_op | source)
XLA Modules:
  0.0 56.7 jit_solution(9693445496741009017)
XLA Ops:
  0.7 0.1 stack.23.idx_ref
  0.7 3.7 %shard_map.131 = (bf16[32,64,128]{2,1,0:T(8,128)(2,1)S(1)}, bf16[32,64,128]{2,1,0:T(8,128)(2,1)S(1)}, bf16[32,64,128]{2,1,0:T(8,128)(2,1)S(1)}, bf16[32,64,128]{2,1,0:T(8,128)(2,1)S(1)}, bf16[4,64,128]{2,1,0:T(8,128)(2,1)S(1)}) custom-call(s32[5]{0:T(128)S(1)} %stack.23.idx_ref, bf16[64,64,128]{2,1,0:T(8,128)(2,1)} %bitcast.22, f32[1,64]{1,0:T(1,128)} %bitcast.25, ...), custom_call_target="tpu_custom_call" | custom-call | flops 1000000 | bytes 1048576 | tf_op jit(solution)/shard_map/pallas_call | solution.py:559
  4.4 3.1 %collective-permute-start = (bf16[32,64,128]{2,1,0:T(8,128)(2,1)S(1)}, bf16[32,64,128]{2,1,0:T(8,128)(2,1)S(1)}, u32[]{:S(2)}, u32[]{:S(2)}) collective-permute-start(bf16[32,64,128]{2,1,0:T(8,128)(2,1)S(1)} %get-tuple-element.21.own_ref), channel_id=1, source_target_pairs={{0,1},{1,0},{2,3},{3,2},{4,5},{5,4},{6,7},{7,6},{8,9},{9,8},{10,11... | collective-permute-start | bytes 1572872 | tf_op jit(solution)/shard_map/ppermute | solution.py:593
  7.5 1.6 %collective-permute-start.1 = (bf16[4,64,128]{2,1,0:T(8,128)(2,1)S(1)}, bf16[4,64,128]{2,1,0:T(8,128)(2,1)S(1)}, u32[]{:S(2)}, u32[]{:S(2)}) collective-permute-start(bf16[4,64,128]{2,1,0:T(8,128)(2,1)S(1)} %get-tuple-element.22.refs_0_), channel_id=1, source_target_pairs={{0,2},{2,0},{4,6},{6,4},{1,3},{3,1},{5,7},{7,5},{8,10},{10,8},{12,... | collective-permute-start | bytes 196616 | tf_op jit(solution)/shard_map/ppermute | solution.py:591
  9.0 2.6 %collective-permute-start.2 = (bf16[4,64,128]{2,1,0:T(8,128)(2,1)S(1)}, bf16[4,64,128]{2,1,0:T(8,128)(2,1)S(1)}, u32[]{:S(2)}, u32[]{:S(2)}) collective-permute-start(bf16[4,64,128]{2,1,0:T(8,128)(2,1)S(1)} %get-tuple-element.22.refs_0_), channel_id=1, source_target_pairs={{0,4},{2,6},{4,0},{6,2},{1,5},{3,7},{5,1},{7,3},{8,12},{10,14},{12... | collective-permute-start | bytes 196616 | tf_op jit(solution)/shard_map/ppermute | solution.py:591
  11.6 0.2 collective-permute-start.3
  11.9 3.6 %query.1.refs_5_.main_query = f32[64,64,128]{2,1,0:T(8,128)S(1)} custom-call(s32[5]{0:T(128)S(1)} %stack.23.idx_ref, bf16[64,128,128]{2,1,0:T(8,128)(2,1)} %main_ref.1, bf16[64,128]{1,0:T(8,128)(2,1)} %bitcast.23), custom_call_target="tpu_custom_call" | custom-call | flops 1000000 | bytes 1048576 | tf_op jit(solution)/shard_map/query/pallas_call | solution.py:611
  15.5 0.0 copy-start.1
  15.5 0.0 copy-start.2
  15.5 1.5 %pack.1 = (bf16[576,64]{1,0:T(8,128)(2,1)S(1)}, f32[64,128]{1,0:T(8,128)S(1)}) custom-call(s32[5]{0:T(128)S(1)} %stack.23.idx_ref, bf16[64,256]{1,0:T(8,128)(2,1)} %project_ref.1, bf16[64,64]{1,0:T(8,128)(2,1)} %tri_out_ref.1, bf16[64,128]{1,0:T(8,128)(2,1)} %kv_ref.1, f32[1,64]{1,0:T(1,128)} %bitcast.26), custom_call_target="tpu_custom_call" | custom-call | flops 1000000 | bytes 1048576 | tf_op jit(solution)/shard_map/pack/pallas_call | solution.py:601
  17.1 0.0 collective-permute-done.1.refs_1_
  17.1 0.0 collective-permute-done.2.refs_2_
  17.1 0.6 %collective-permute-done.3.refs_3_ = bf16[4,64,128]{2,1,0:T(8,128)(2,1)S(1)} collective-permute-done((bf16[4,64,128]{2,1,0:T(8,128)(2,1)S(1)}, bf16[4,64,128]{2,1,0:T(8,128)(2,1)S(1)}, u32[]{:S(2)}, u32[]{:S(2)}) %collective-permute-start.3) | collective-permute-done | bytes 65568 | tf_op jit(solution)/shard_map/ppermute | solution.py:591
  17.7 0.6 %shard_map.133 = bf16[2,4,64,128]{3,2,1,0:T(8,128)(2,1)S(1)} custom-call(s32[5]{0:T(128)S(1)} %stack.23.idx_ref, bf16[4,64,128]{2,1,0:T(8,128)(2,1)S(1)} %get-tuple-element.22.refs_0_, bf16[4,64,128]{2,1,0:T(8,128)(2,1)S(1)} %collective-permute-done.1.refs_1_, bf16[4,64,128]{2,1,0:T(8,128)(2,1)S(1)} %collective-permute-done.2.refs_2_, ...), custom_call_target="tpu_custom_call" | custom-call | flops 1000000 | bytes 1048576 | tf_op jit(solution)/shard_map/pallas_call | solution.py:624
  18.3 0.6 %collective-permute-start.4 = (bf16[2,4,64,128]{3,2,1,0:T(8,128)(2,1)S(1)}, bf16[2,4,64,128]{3,2,1,0:T(8,128)(2,1)S(1)}, u32[]{:S(2)}, u32[]{:S(2)}) collective-permute-start(bf16[2,4,64,128]{3,2,1,0:T(8,128)(2,1)S(1)} %shard_map.133), channel_id=1, source_target_pairs={{0,1},{1,0},{2,3},{3,2},{4,5},{5,4},{6,7},{7,6},{8,9},{9,8},{10,11... | collective-permute-start | bytes 393224 | tf_op jit(solution)/shard_map/ppermute | solution.py:629
  18.9 1.5 %collective-permute-start.5 = (bf16[32,64,128]{2,1,0:T(8,128)(2,1)S(1)}, bf16[32,64,128]{2,1,0:T(8,128)(2,1)S(1)}, u32[]{:S(2)}, u32[]{:S(2)}) collective-permute-start(bf16[32,64,128]{2,1,0:T(8,128)(2,1)S(1)} %get-tuple-element.29.own_ref), channel_id=1, source_target_pairs={{0,1},{1,0},{2,3},{3,2},{4,5},{5,4},{6,7},{7,6},{8,9},{9,8},{10,11... | collective-permute-start | bytes 1572872 | tf_op jit(solution)/shard_map/ppermute | solution.py:637
  20.4 0.0 copy-done.1
  20.4 0.0 copy-done.2
  20.4 1.2 %shard_map.132.own_bias_ref = f32[4,128,128]{2,1,0:T(8,128)S(1)} custom-call(s32[5]{0:T(128)S(1)} %stack.23.idx_ref, s32[2,4]{1,0:T(2,128)S(1)} %bitcast.16, s32[2,2]{1,0:T(2,128)S(1)} %copy-done.2, bf16[4,64,128]{2,1,0:T(8,128)(2,1)S(1)} %get-tuple-element.22.refs_0_, bf16[4,64,128]{2,1,0:T(8,128)(2,1)S(1)} %collective-permute-done.1.refs_1_, ...), custom_call_target="tpu_custom_call" | custom-call | flops 1000000 | bytes 1048576 | tf_op jit(solution)/shard_map/pallas_call | solution.py:631
  21.5 3.2 %collective-permute-done.4.tiles_ref = bf16[2,4,64,128]{3,2,1,0:T(8,128)(2,1)S(1)} collective-permute-done((bf16[2,4,64,128]{3,2,1,0:T(8,128)(2,1)S(1)}, bf16[2,4,64,128]{3,2,1,0:T(8,128)(2,1)S(1)}, u32[]{:S(2)}, u32[]{:S(2)}) %collective-permute-start.4) | collective-permute-done | bytes 131104 | tf_op jit(solution)/shard_map/ppermute | solution.py:629
  24.7 0.9 %shard_map.134.far_bias_ref.after_ref = f32[4,128,128]{2,1,0:T(8,128)S(1)} custom-call(s32[5]{0:T(128)S(1)} %stack.23.idx_ref, s32[2,4]{1,0:T(2,128)S(1)} %bitcast.17, s32[2,2]{1,0:T(2,128)S(1)} %copy-done.2, bf16[2,4,64,128]{3,2,1,0:T(8,128)(2,1)S(1)} %collective-permute-done.4.tiles_ref), custom_call_target="tpu_custom_call" | custom-call | flops 1000000 | bytes 1048576 | tf_op jit(solution)/shard_map/pallas_call | solution.py:634
  25.6 0.0 collective-permute-done.far_ref
  25.6 3.5 %attend0.1 = (bf16[16,64,128]{2,1,0:T(8,128)(2,1)S(1)}, bf16[16,72,128]{2,1,0:T(8,128)(2,1)S(1)}) custom-call(bf16[32,64,128]{2,1,0:T(8,128)(2,1)S(1)} %get-tuple-element.20.x_ref, bf16[32,64,128]{2,1,0:T(8,128)(2,1)S(1)} %get-tuple-element.21.own_ref, bf16[32,64,128]{2,1,0:T(8,128)(2,1)S(1)} %collective-permute-done.far_ref, ...), custom_call_target="tpu_custom_call" | custom-call | flops 6000000000 | bytes 1048576 | tf_op jit(solution)/shard_map/attend0/pallas_call | solution.py:647
  29.1 0.1 collective-permute-start.6
  29.1 3.5 %attend1.1 = (bf16[16,64,128]{2,1,0:T(8,128)(2,1)S(1)}, bf16[16,72,128]{2,1,0:T(8,128)(2,1)S(1)}) custom-call(bf16[32,64,128]{2,1,0:T(8,128)(2,1)S(1)} %get-tuple-element.20.x_ref, bf16[32,64,128]{2,1,0:T(8,128)(2,1)S(1)} %get-tuple-element.21.own_ref, bf16[32,64,128]{2,1,0:T(8,128)(2,1)S(1)} %collective-permute-done.far_ref, ...), custom_call_target="tpu_custom_call" | custom-call | flops 6000000000 | bytes 1048576 | tf_op jit(solution)/shard_map/attend1/pallas_call | solution.py:647
  32.6 0.0 collective-permute-done.6.other_ref
  32.6 0.8 %corejoin0.1.after_ref.own_ref = bf16[16,72,128]{2,1,0:T(8,128)(2,1)S(1)} custom-call(s32[5]{0:T(128)S(1)} %stack.23.idx_ref, s32[2,4]{1,0:T(2,128)S(1)} %bitcast.18, s32[2,2]{1,0:T(2,128)S(1)} %copy-done.2, bf16[16,72,128]{2,1,0:T(8,128)(2,1)S(1)} %get-tuple-element.30.own_ref, bf16[16,72,128]{2,1,0:T(8,128)(2,1)S(1)} %collective-permute-done.6.other_ref), custom_call_target="tpu_custom_call" | custom-call | flops 1000000 | bytes 1048576 | tf_op jit(solution)/shard_map/corejoin0/pallas_call | solution.py:670
  33.4 1.6 %collective-permute-start.7 = (bf16[16,72,128]{2,1,0:T(8,128)(2,1)S(1)}, bf16[16,72,128]{2,1,0:T(8,128)(2,1)S(1)}, u32[]{:S(2)}, u32[]{:S(2)}) collective-permute-start(bf16[16,72,128]{2,1,0:T(8,128)(2,1)S(1)} %corejoin0.1.after_ref.own_ref), channel_id=1, source_target_pairs={{0,16},{8,24},{16,0},{24,8},{1,17},{9,25},{17,1},{25,9},{2,18},{10... | collective-permute-start | bytes 884744 | tf_op jit(solution)/shard_map/chipswap0/ppermute | solution.py:687
  35.0 0.0 collective-permute-done.5.far_ref
  35.0 3.5 %attend2.1 = (bf16[16,64,128]{2,1,0:T(8,128)(2,1)S(1)}, bf16[16,72,128]{2,1,0:T(8,128)(2,1)S(1)}) custom-call(bf16[32,64,128]{2,1,0:T(8,128)(2,1)S(1)} %get-tuple-element.28.x_ref, bf16[32,64,128]{2,1,0:T(8,128)(2,1)S(1)} %get-tuple-element.29.own_ref, bf16[32,64,128]{2,1,0:T(8,128)(2,1)S(1)} %collective-permute-done.5.far_ref, ...), custom_call_target="tpu_custom_call" | custom-call | flops 6000000000 | bytes 1048576 | tf_op jit(solution)/shard_map/attend2/pallas_call | solution.py:647
  38.4 0.0 copy-start
  38.5 0.3 collective-permute-start.8
  38.7 3.7 %attend3.1 = (bf16[16,64,128]{2,1,0:T(8,128)(2,1)S(1)}, bf16[16,72,128]{2,1,0:T(8,128)(2,1)S(1)}) custom-call(bf16[32,64,128]{2,1,0:T(8,128)(2,1)S(1)} %get-tuple-element.28.x_ref, bf16[32,64,128]{2,1,0:T(8,128)(2,1)S(1)} %get-tuple-element.29.own_ref, bf16[32,64,128]{2,1,0:T(8,128)(2,1)S(1)} %collective-permute-done.5.far_ref, ...), custom_call_target="tpu_custom_call" | custom-call | flops 6000000000 | bytes 1048576 | tf_op jit(solution)/shard_map/attend3/pallas_call | solution.py:647
  42.4 0.0 collective-permute-done.8.other_ref
  42.4 0.8 %corejoin1.1._.own_ref = bf16[16,72,128]{2,1,0:T(8,128)(2,1)S(1)} custom-call(s32[5]{0:T(128)S(1)} %stack.23.idx_ref, s32[2,4]{1,0:T(2,128)S(1)} %bitcast.19, s32[2,2]{1,0:T(2,128)S(1)} %copy-done.2, bf16[16,72,128]{2,1,0:T(8,128)(2,1)S(1)} %get-tuple-element.34.own_ref, bf16[16,72,128]{2,1,0:T(8,128)(2,1)S(1)} %collective-permute-done.8.other_ref), custom_call_target="tpu_custom_call" | custom-call | flops 1000000 | bytes 1048576 | tf_op jit(solution)/shard_map/corejoin1/pallas_call | solution.py:670
  43.2 0.6 %collective-permute-start.10 = (bf16[16,72,128]{2,1,0:T(8,128)(2,1)S(1)}, bf16[16,72,128]{2,1,0:T(8,128)(2,1)S(1)}, u32[]{:S(2)}, u32[]{:S(2)}) collective-permute-start(bf16[16,72,128]{2,1,0:T(8,128)(2,1)S(1)} %corejoin1.1._.own_ref), channel_id=1, source_target_pairs={{0,16},{8,24},{16,0},{24,8},{1,17},{9,25},{17,1},{25,9},{2,18},{10... | collective-permute-start | bytes 884744 | tf_op jit(solution)/shard_map/chipswap1/ppermute | solution.py:687
  43.8 0.0 collective-permute-done.7.other_ref
  43.8 0.8 %chipjoin0.1.refs_5_ = bf16[16,64,128]{2,1,0:T(8,128)(2,1)S(1)} custom-call(s32[5]{0:T(128)S(1)} %stack.23.idx_ref, s32[2,4]{1,0:T(2,128)S(1)} %bitcast.20, s32[2,2]{1,0:T(2,128)S(1)} %copy-done.2, bf16[16,72,128]{2,1,0:T(8,128)(2,1)S(1)} %corejoin0.1.after_ref.own_ref, bf16[16,72,128]{2,1,0:T(8,128)(2,1)S(1)} %collective-permute-done.7.other_ref, ...), custom_call_target="tpu_custom_call" | custom-call | flops 1000000 | bytes 1048576 | tf_op jit(solution)/shard_map/chipjoin0/pallas_call | solution.py:689
  44.6 0.1 collective-permute-start.9
  44.7 1.5 %collective-permute-done.9.refs_4_ = bf16[16,64,128]{2,1,0:T(8,128)(2,1)S(1)} collective-permute-done((bf16[16,64,128]{2,1,0:T(8,128)(2,1)S(1)}, bf16[16,64,128]{2,1,0:T(8,128)(2,1)S(1)}, u32[]{:S(2)}, u32[]{:S(2)}) %collective-permute-start.9) | collective-permute-done | bytes 262176 | tf_op jit(solution)/shard_map/lastswap0/ppermute | solution.py:695
  46.2 0.0 copy-done
  46.2 3.0 %finish.1 = (bf16[64,64,128]{2,1,0:T(8,128)(2,1)}, bf16[64,128,128]{2,1,0:T(8,128)(2,1)}, f32[8,128]{1,0:T(8,128)S(1)}) custom-call(s32[5]{0:T(128)S(1)} %stack.23.idx_ref, bf16[16,64,128]{2,1,0:T(8,128)(2,1)S(1)} %get-tuple-element.25.refs_0_, bf16[16,64,128]{2,1,0:T(8,128)(2,1)S(1)} %get-tuple-element.27.refs_1_, ...), custom_call_target="tpu_custom_call" | custom-call | flops 1000000 | bytes 1048576 | tf_op jit(solution)/shard_map/finish/pallas_call | solution.py:702
  49.2 3.3 %collective-permute-done.10.other_ref = bf16[16,72,128]{2,1,0:T(8,128)(2,1)S(1)} collective-permute-done((bf16[16,72,128]{2,1,0:T(8,128)(2,1)S(1)}, bf16[16,72,128]{2,1,0:T(8,128)(2,1)S(1)}, u32[]{:S(2)}, u32[]{:S(2)}) %collective-permute-start.10) | collective-permute-done | bytes 294944 | tf_op jit(solution)/shard_map/chipswap1/ppermute | solution.py:687
  52.5 0.8 %chipjoin1.1.merged_ref = bf16[16,64,128]{2,1,0:T(8,128)(2,1)S(1)} custom-call(s32[5]{0:T(128)S(1)} %stack.23.idx_ref, s32[2,4]{1,0:T(2,128)S(1)} %bitcast.21, s32[2,2]{1,0:T(2,128)S(1)} %copy-done.2, bf16[16,72,128]{2,1,0:T(8,128)(2,1)S(1)} %corejoin1.1._.own_ref, bf16[16,72,128]{2,1,0:T(8,128)(2,1)S(1)} %collective-permute-done.10.other_ref, ...), custom_call_target="tpu_custom_call" | custom-call | flops 1000000 | bytes 1048576 | tf_op jit(solution)/shard_map/chipjoin1/pallas_call | solution.py:689
  53.2 0.1 collective-permute-start.11
  53.3 1.7 %embed3.1.prior_ref = bf16[64,128,128]{2,1,0:T(8,128)(2,1)} custom-call(s32[5]{0:T(128)S(1)} %stack.23.idx_ref, bf16[16,64,128]{2,1,0:T(8,128)(2,1)S(1)} %chipjoin1.1.merged_ref, bf16[64,128]{1,0:T(8,128)(2,1)S(1)} %copy-done, bf16[64,128,128]{2,1,0:T(8,128)(2,1)} %get-tuple-element.37.prior_ref), custom_call_target="tpu_custom_call", output_to_operand_aliasing={{}: (3, {})} | custom-call | flops 1000000 | bytes 1048576 | tf_op jit(solution)/shard_map/embed3/pallas_call | solution.py:722
  55.0 0.0 collective-permute-done.11.merged_ref
  55.0 1.7 %embed2.1 = bf16[64,128,128]{2,1,0:T(8,128)(2,1)} custom-call(s32[5]{0:T(128)S(1)} %stack.23.idx_ref, bf16[16,64,128]{2,1,0:T(8,128)(2,1)S(1)} %collective-permute-done.11.merged_ref, bf16[64,128]{1,0:T(8,128)(2,1)S(1)} %copy-done, bf16[64,128,128]{2,1,0:T(8,128)(2,1)} %embed3.1.prior_ref), custom_call_target="tpu_custom_call", output_to_operand_aliasing={{}: (3, {})} | custom-call | flops 1000000 | bytes 1048576 | tf_op jit(solution)/shard_map/embed2/pallas_call | solution.py:722
Async XLA Ops:
  4.4 21.2 %collective-permute-start = (bf16[32,64,128]{2,1,0:T(8,128)(2,1)S(1)}, bf16[32,64,128]{2,1,0:T(8,128)(2,1)S(1)}, u32[]{:S(2)}, u32[]{:S(2)}) collective-permute-start(bf16[32,64,128]{2,1,0:T(8,128)(2,1)S(1)} %get-tuple-element.21.own_ref), channel_id=1, source_target_pairs={{0,1},{1,0},{2,3},{3,2},{4,5},{5,4},{6,7},{7,6},{8,9},{9,8},{10,11... | collective-permute-start | bytes 1572872 | tf_op jit(solution)/shard_map/ppermute | solution.py:593
  7.5 9.6 %collective-permute-start.1 = (bf16[4,64,128]{2,1,0:T(8,128)(2,1)S(1)}, bf16[4,64,128]{2,1,0:T(8,128)(2,1)S(1)}, u32[]{:S(2)}, u32[]{:S(2)}) collective-permute-start(bf16[4,64,128]{2,1,0:T(8,128)(2,1)S(1)} %get-tuple-element.22.refs_0_), channel_id=1, source_target_pairs={{0,2},{2,0},{4,6},{6,4},{1,3},{3,1},{5,7},{7,5},{8,10},{10,8},{12,... | collective-permute-start | bytes 196616 | tf_op jit(solution)/shard_map/ppermute | solution.py:591
  9.0 8.1 %collective-permute-start.2 = (bf16[4,64,128]{2,1,0:T(8,128)(2,1)S(1)}, bf16[4,64,128]{2,1,0:T(8,128)(2,1)S(1)}, u32[]{:S(2)}, u32[]{:S(2)}) collective-permute-start(bf16[4,64,128]{2,1,0:T(8,128)(2,1)S(1)} %get-tuple-element.22.refs_0_), channel_id=1, source_target_pairs={{0,4},{2,6},{4,0},{6,2},{1,5},{3,7},{5,1},{7,3},{8,12},{10,14},{12... | collective-permute-start | bytes 196616 | tf_op jit(solution)/shard_map/ppermute | solution.py:591
  11.6 6.1 %collective-permute-start.3 = (bf16[4,64,128]{2,1,0:T(8,128)(2,1)S(1)}, bf16[4,64,128]{2,1,0:T(8,128)(2,1)S(1)}, u32[]{:S(2)}, u32[]{:S(2)}) collective-permute-start(bf16[4,64,128]{2,1,0:T(8,128)(2,1)S(1)} %get-tuple-element.22.refs_0_), channel_id=1, source_target_pairs={{0,6},{2,4},{4,2},{6,0},{1,7},{3,5},{5,3},{7,1},{8,14},{10,12},{12... | collective-permute-start | bytes 196616 | tf_op jit(solution)/shard_map/ppermute | solution.py:591
  15.5 4.9 %copy-start.1 = (s32[4,2]{0,1:T(2,128)S(1)}, s32[4,2]{0,1:T(2,128)}, u32[]{:S(2)}) copy-start(s32[4,2]{0,1:T(2,128)} %param.14) | copy-start | bytes 100
  15.5 4.9 %copy-start.2 = (s32[2,2]{1,0:T(2,128)S(1)}, s32[2,2]{1,0:T(2,128)}, u32[]{:S(2)}) copy-start(s32[2,2]{1,0:T(2,128)} %mask_ref.11) | copy-start | bytes 52
  18.3 6.4 %collective-permute-start.4 = (bf16[2,4,64,128]{3,2,1,0:T(8,128)(2,1)S(1)}, bf16[2,4,64,128]{3,2,1,0:T(8,128)(2,1)S(1)}, u32[]{:S(2)}, u32[]{:S(2)}) collective-permute-start(bf16[2,4,64,128]{3,2,1,0:T(8,128)(2,1)S(1)} %shard_map.133), channel_id=1, source_target_pairs={{0,1},{1,0},{2,3},{3,2},{4,5},{5,4},{6,7},{7,6},{8,9},{9,8},{10,11... | collective-permute-start | bytes 393224 | tf_op jit(solution)/shard_map/ppermute | solution.py:629
  18.9 16.1 %collective-permute-start.5 = (bf16[32,64,128]{2,1,0:T(8,128)(2,1)S(1)}, bf16[32,64,128]{2,1,0:T(8,128)(2,1)S(1)}, u32[]{:S(2)}, u32[]{:S(2)}) collective-permute-start(bf16[32,64,128]{2,1,0:T(8,128)(2,1)S(1)} %get-tuple-element.29.own_ref), channel_id=1, source_target_pairs={{0,1},{1,0},{2,3},{3,2},{4,5},{5,4},{6,7},{7,6},{8,9},{9,8},{10,11... | collective-permute-start | bytes 1572872 | tf_op jit(solution)/shard_map/ppermute | solution.py:637
  29.1 3.6 %collective-permute-start.6 = (bf16[16,72,128]{2,1,0:T(8,128)(2,1)S(1)}, bf16[16,72,128]{2,1,0:T(8,128)(2,1)S(1)}, u32[]{:S(2)}, u32[]{:S(2)}) collective-permute-start(bf16[16,72,128]{2,1,0:T(8,128)(2,1)S(1)} %get-tuple-element.26.after_ref), channel_id=1, source_target_pairs={{0,8},{8,0},{16,24},{24,16},{1,9},{9,1},{17,25},{25,17},{2,10},{10... | collective-permute-start | bytes 884744 | tf_op jit(solution)/shard_map/coreswap0/ppermute | solution.py:678
  33.4 10.4 %collective-permute-start.7 = (bf16[16,72,128]{2,1,0:T(8,128)(2,1)S(1)}, bf16[16,72,128]{2,1,0:T(8,128)(2,1)S(1)}, u32[]{:S(2)}, u32[]{:S(2)}) collective-permute-start(bf16[16,72,128]{2,1,0:T(8,128)(2,1)S(1)} %corejoin0.1.after_ref.own_ref), channel_id=1, source_target_pairs={{0,16},{8,24},{16,0},{24,8},{1,17},{9,25},{17,1},{25,9},{2,18},{10... | collective-permute-start | bytes 884744 | tf_op jit(solution)/shard_map/chipswap0/ppermute | solution.py:687
  38.4 7.7 %copy-start = (bf16[64,128]{1,0:T(8,128)(2,1)S(1)}, bf16[64,128]{1,0:T(8,128)(2,1)}, u32[]{:S(2)}) copy-start(bf16[64,128]{1,0:T(8,128)(2,1)} %w_ref.3) | copy-start | bytes 49156
  38.5 4.0 %collective-permute-start.8 = (bf16[16,72,128]{2,1,0:T(8,128)(2,1)S(1)}, bf16[16,72,128]{2,1,0:T(8,128)(2,1)S(1)}, u32[]{:S(2)}, u32[]{:S(2)}) collective-permute-start(bf16[16,72,128]{2,1,0:T(8,128)(2,1)S(1)} %get-tuple-element.32.after_ref), channel_id=1, source_target_pairs={{0,8},{8,0},{16,24},{24,16},{1,9},{9,1},{17,25},{25,17},{2,10},{10... | collective-permute-start | bytes 884744 | tf_op jit(solution)/shard_map/coreswap1/ppermute | solution.py:678
  43.2 9.3 %collective-permute-start.10 = (bf16[16,72,128]{2,1,0:T(8,128)(2,1)S(1)}, bf16[16,72,128]{2,1,0:T(8,128)(2,1)S(1)}, u32[]{:S(2)}, u32[]{:S(2)}) collective-permute-start(bf16[16,72,128]{2,1,0:T(8,128)(2,1)S(1)} %corejoin1.1._.own_ref), channel_id=1, source_target_pairs={{0,16},{8,24},{16,0},{24,8},{1,17},{9,25},{17,1},{25,9},{2,18},{10... | collective-permute-start | bytes 884744 | tf_op jit(solution)/shard_map/chipswap1/ppermute | solution.py:687
  44.6 1.6 %collective-permute-start.9 = (bf16[16,64,128]{2,1,0:T(8,128)(2,1)S(1)}, bf16[16,64,128]{2,1,0:T(8,128)(2,1)S(1)}, u32[]{:S(2)}, u32[]{:S(2)}) collective-permute-start(bf16[16,64,128]{2,1,0:T(8,128)(2,1)S(1)} %chipjoin0.1.refs_5_), channel_id=1, source_target_pairs={{0,8},{8,0},{16,24},{24,16},{1,9},{9,1},{17,25},{25,17},{2,10},{10... | collective-permute-start | bytes 786440 | tf_op jit(solution)/shard_map/lastswap0/ppermute | solution.py:695
  53.2 1.8 %collective-permute-start.11 = (bf16[16,64,128]{2,1,0:T(8,128)(2,1)S(1)}, bf16[16,64,128]{2,1,0:T(8,128)(2,1)S(1)}, u32[]{:S(2)}, u32[]{:S(2)}) collective-permute-start(bf16[16,64,128]{2,1,0:T(8,128)(2,1)S(1)} %chipjoin1.1.merged_ref), channel_id=1, source_target_pairs={{0,8},{8,0},{16,24},{24,16},{1,9},{9,1},{17,25},{25,17},{2,10},{10... | collective-permute-start | bytes 786440 | tf_op jit(solution)/shard_map/lastswap1/ppermute | solution.py:695

commit v4 on v3

--- a/solution.py
+++ b/solution.py
@@ -198,6 +198,11 @@
     return (center * lax.rsqrt(spread + EPSILON) * gain).astype(jnp.bfloat16)
 
 
+def places(rows):
+    templ, row_dev, col_dev = (lax.axis_index(axis) for axis in ("tmpl", "row", "col"))
+    return lax.rem(templ, 2), templ, row_dev, col_dev, row_dev * rows // BLOCK
+
+
 def piece_of(piece, idx_ref, pieces):
     half = idx_ref[0]
     odd = lax.rem(piece, 2)
@@ -222,36 +227,50 @@
     return jnp.broadcast_to(row_ref[...], (cols, row_ref.shape[1])).T
 
 
-def norm_kernel(heads, idx_ref, x_ref, gain_ref, bias_w_ref, *refs):
-    piece = pl.program_id(0)
-    *kept_refs, bias_ref, held, wide = refs
+def norm_kernel(heads, x_hbm, gain_hbm, bias_w_hbm, *refs):
+    *kept_refs, bias_ref, held, wide, x_ref, gain_ref, bias_w_ref, done = refs
     norm_refs, raw_refs = kept_refs[::2], kept_refs[1::2]
-
-    @pl.when(piece == 0)
-    def _():
-        wide[...] = widened(gain_ref, wide.shape[1])
-
-    step_rows = x_ref.shape[0]
-    for chunk, (norm_ref, raw_ref) in enumerate(zip(norm_refs, raw_refs)):
-
-        @pl.when(piece // 2 == chunk)
-        def _():
-            base = (piece - 2 * chunk) * step_rows
-            for i in range(step_rows):
-                raw_ref[base + i] = x_ref[i]
-                norm_ref[base + i] = normed_rows(x_ref[i].astype(jnp.float32), wide[...])
-            cols = x_ref.shape[2]
-            wide_norm = jnp.concatenate([norm_ref[base + i] for i in range(step_rows)], axis=1)
-            wide_bias = matmul(bias_w_ref[...], wide_norm)
-            for i in range(step_rows):
-                for head in range(heads):
-                    held[head, i : i + 1, :] = wide_bias[head : head + 1, i * cols : (i + 1) * cols]
-
-    first = pl.multiple_of(piece_of(piece, idx_ref, pl.num_programs(0)) * step_rows, step_rows)
-    bias_ref[:, pl.ds(first, step_rows), :] = held[...].astype(jnp.bfloat16)
-
-
-def weight_kernel(heads, idx_ref, project_ref, tri_out_ref, kv_ref, gain_ref, pack_ref, wide_ref):
+    pieces, step_rows, _, cols = x_ref.shape
+    idx_ref = places(pieces * step_rows)
+    small = [
+        pltpu.make_async_copy(gain_hbm, gain_ref, done.at[pieces]),
+        pltpu.make_async_copy(bias_w_hbm, bias_w_ref, done.at[pieces + 1]),
+    ]
+    firsts = [
+        pl.multiple_of(piece_of(piece, idx_ref, pieces) * step_rows, step_rows)
+        for piece in range(pieces)
+    ]
+    copies = [
+        pltpu.make_async_copy(x_hbm.at[pl.ds(first, step_rows)], x_ref.at[piece], done.at[piece])
+        for piece, first in enumerate(firsts)
+    ]
+    for copy in small + copies:
+        copy.start()
+    for copy in small:
+        copy.wait()
+    wide[...] = widened(gain_ref, cols)
+    for piece in range(pieces):
+        copies[piece].wait()
+        base = piece % 2 * step_rows
+        norm_ref, raw_ref = norm_refs[piece // 2], raw_refs[piece // 2]
+        for i in range(step_rows):
+            raw_ref[base + i] = x_ref[piece, i]
+            norm_ref[base + i] = normed_rows(x_ref[piece, i].astype(jnp.float32), wide[...])
+        wide_norm = jnp.concatenate([norm_ref[base + i] for i in range(step_rows)], axis=1)
+        wide_bias = matmul(bias_w_ref[...], wide_norm)
+        for i in range(step_rows):
+            for head in range(heads):
+                held[piece, head, i : i + 1, :] = wide_bias[
+                    head : head + 1, i * cols : (i + 1) * cols
+                ]
+        bias_ref[:, pl.ds(firsts[piece], step_rows), :] = held[piece].astype(jnp.bfloat16)
+
+
+def weight_kernel(
+    heads, idx_ref, project_ref, tri_out_ref, kv_ref, gain_ref, cover_ref, mask_ref, pack_ref, wide_ref, table_ref
+):
+    for line, shift in enumerate(all_shifts(idx_ref, cover_ref, mask_ref)):
+        table_ref[line : line + 1, :] = jnp.full((1, table_ref.shape[1]), shift, jnp.float32)
     wide_ref[...] = widened(gain_ref, wide_ref.shape[1])
     channels = project_ref.shape[0]
     hidden = tri_out_ref.shape[0]
@@ -286,8 +305,9 @@
             act(tile_ref)
 
 
-def pick_kernel(idx_ref, *refs):
+def pick_kernel(*refs):
     *tile_refs, _, _, out_ref = refs
+    idx_ref = places(tile_refs[0].shape[1])
     for part in range(out_ref.shape[0]):
 
         def act(tile_ref, part=part):
@@ -299,6 +319,18 @@
 def relative_shift(idx_ref, cover_ref, mask_ref, block):
     shifts = [mask_shift(cover_ref, mask_ref, idx_ref[1], idx_ref[4], b) for b in (block, 1 - block)]
     return shifts[0] - jnp.maximum(*shifts)
+
+
+def all_shifts(idx_ref, cover_ref, mask_ref):
+    own, other, best, far_best = pair_shifts(idx_ref, cover_ref, mask_ref)
+    top = jnp.maximum(best, far_best)
+    blocks = (idx_ref[3], 1 - idx_ref[3])
+    return [relative_shift(idx_ref, cover_ref, mask_ref, block) for block in blocks] + [
+        own,
+        other,
+        best - top,
+        far_best - top,
+    ]
 
 
 def place_bias(out_ref, part, tile, shift):
@@ -308,10 +340,11 @@
         out_ref[head, :, part * tile_rows : (part + 1) * tile_rows] = (flipped + shift) * LOG2E
 
 
-def own_bias_kernel(idx_ref, cover_ref, mask_ref, *refs):
+def own_bias_kernel(table_ref, *refs):
     *tile_refs, out_ref = refs
+    idx_ref = places(tile_refs[0].shape[1])
     tiles_per_col = out_ref.shape[2] // tile_refs[0].shape[1]
-    shift = relative_shift(idx_ref, cover_ref, mask_ref, idx_ref[3])
+    shift = table_ref[0:1, : tile_refs[0].shape[1]]
     for part in range(tiles_per_col):
 
         def act(tile_ref, part=part):
@@ -320,8 +353,8 @@
         when_held(idx_ref, idx_ref[3], part, tile_refs, tiles_per_col, act)
 
 
-def far_bias_kernel(idx_ref, cover_ref, mask_ref, tiles_ref, out_ref):
-    shift = relative_shift(idx_ref, cover_ref, mask_ref, 1 - idx_ref[3])
+def far_bias_kernel(table_ref, tiles_ref, _, out_ref):
+    shift = table_ref[1:2, : tiles_ref.shape[2]]
     for part in range(tiles_ref.shape[0]):
         place_bias(out_ref, part, tiles_ref[part], shift)
 
@@ -332,6 +365,110 @@
     wide = matmul(w_ref[...], main_ref[...].reshape(step_rows * cols, pair_ch), 1, 1) * scale
     for i in range(step_rows):
         out_ref[base + i] = wide[:, i * cols : (i + 1) * cols]
+
+
+def split_pack(pack_ref, heads, hidden):
+    channels = pack_ref.shape[1]
+    ends = [heads * channels]
+    for size in (hidden, hidden, channels):
+        ends.append(ends[-1] + size)
+    return ends
+
+
+def near_kernel(
+    heads, skip, own_ref, own_bias_ref, pack_ref, after_ref, probes, gates, own_mix, near, near_tops, turned
+):
+    step_rows, _, channels, cols = probes.shape
+    ends = split_pack(pack_ref, heads, gates.shape[1])
+    for i in range(step_rows):
+        own = own_ref[skip + i]
+        first = matmul(pack_ref[: ends[2], :], own)
+        for h in range(heads):
+            probes[i, h] = first[h * channels : (h + 1) * channels, :].astype(jnp.bfloat16)
+        gates[i] = jax.nn.sigmoid(first[ends[0] : ends[1], :])
+        own_mix[i] = first[ends[1] :, :].astype(jnp.bfloat16)
+        turned[i] = own.T
+    for i in range(step_rows):
+        for h in range(heads):
+            scores = matmul(turned[i], probes[i, h]) + own_bias_ref[h]
+            near[i, h] = scores
+            near_tops[i, h] = jnp.broadcast_to(
+                jnp.max(scores, axis=0, keepdims=True), near_tops.shape[2:]
+            )
+
+
+def late_kernel(
+    heads,
+    skip,
+    query_skip,
+    x_ref,
+    far_ref,
+    main_query,
+    far_bias_ref,
+    pack_ref,
+    gain_ref,
+    probes,
+    gates,
+    own_mix,
+    near,
+    near_tops,
+    after_ref,
+    out_ref,
+    state_ref,
+    turned,
+    mixers,
+    held,
+    tops,
+    gated,
+):
+    step_rows, channels, cols = out_ref.shape
+    hidden = main_query.shape[1]
+    dim = hidden // heads
+    ends = split_pack(pack_ref, heads, hidden)
+    value_w = pack_ref[ends[1] : ends[2], :]
+    for i in range(step_rows):
+        far = far_ref[skip + i]
+        values = matmul(value_w, far).astype(jnp.bfloat16)
+        for h in range(heads):
+            span = slice(h * dim, (h + 1) * dim)
+            mixers[i, h, :dim, :cols] = own_mix[i, span, :]
+            mixers[i, h, :dim, cols:] = values[span, :]
+            mixers[i, h, dim:, :] = jnp.ones((mixers.shape[2] - dim, 2 * cols), jnp.bfloat16)
+        turned[i] = far.T
+
+    slots = held.shape[0]
+
+    def score_row(i):
+        for h in range(heads):
+            scores = matmul(turned[i], probes[i, h]) + far_bias_ref[h]
+            held[i % slots, h] = scores
+            highest = jnp.max(scores, axis=0, keepdims=True)
+            tops[i % slots, h] = jnp.maximum(near_tops[i, h], highest)
+
+    def mix_row(i):
+        for h in range(heads):
+            top = tops[i % slots, h][:1]
+            weights = jnp.concatenate(
+                [
+                    jnp.exp2(part - top).astype(jnp.bfloat16)
+                    for part in (near[i, h], held[i % slots, h])
+                ],
+                axis=0,
+            )
+            mixed = matmul(mixers[i, h], weights)
+            span = slice(h * dim, (h + 1) * dim)
+            gated[i, span, :] = (
+                mixed[:dim] * (1.0 / mixed[dim : dim + 1]) * gates[i, span, :]
+            ).astype(jnp.bfloat16)
+
+    score_row(0)
+    for i in range(step_rows):
+        if i + 1 < step_rows:
+            score_row(i + 1)
+        mix_row(i)
+    write_rows(
+        heads, skip, query_skip, x_ref, main_query, pack_ref, gain_ref, gated, out_ref, state_ref
+    )
 
 
 def attend_kernel(
@@ -363,8 +500,6 @@
     row = heads * channels + hidden
     first_w = pack_ref[:row, :]
     value_w = pack_ref[row : row + hidden, :]
-    tri_w = pack_ref[row + hidden : row + hidden + channels, :]
-    kv_w = pack_ref[row + hidden + channels :, :]
     for i in range(step_rows):
         own = own_ref[skip + i]
         both = jnp.concatenate([own, far_ref[skip + i]], axis=1)
@@ -404,6 +539,20 @@
         if i + 1 < step_rows:
             score_row(i + 1)
         mix_row(i)
+    write_rows(
+        heads, skip, query_skip, x_ref, main_query, pack_ref, gain_ref, gated, out_ref, state_ref
+    )
+
+
+def write_rows(
+    heads, skip, query_skip, x_ref, main_query, pack_ref, gain_ref, gated, out_ref, state_ref
+):
+    step_rows = out_ref.shape[0]
+    hidden = gated.shape[1]
+    dim = hidden // heads
+    ends = split_pack(pack_ref, heads, hidden)
+    tri_w = pack_ref[ends[2] : ends[3], :]
+    kv_w = pack_ref[ends[3] :, :]
     for i in range(step_rows):
         fresh = x_ref[skip + i].astype(jnp.float32) + matmul(tri_w, gated[i])
         out_ref[i] = fresh.astype(jnp.bfloat16)
@@ -470,18 +619,17 @@
     return own - best, other - best, best, far_best
 
 
-def core_join_kernel(heads, idx_ref, cover_ref, mask_ref, own_ref, other_ref, state_ref):
-    own_shift, other_shift, _, _ = pair_shifts(idx_ref, cover_ref, mask_ref)
+def core_join_kernel(heads, table_ref, own_ref, other_ref, state_ref):
+    own_shift, other_shift = table_ref[2:3, :], table_ref[3:4, :]
     for i in range(own_ref.shape[0]):
         values, score = joined(heads, own_ref, other_ref, i, own_shift, other_shift)
         store_state(state_ref, i, values.astype(jnp.bfloat16), score)
 
 
-def chip_join_kernel(heads, idx_ref, cover_ref, mask_ref, own_ref, other_ref, _, merged_ref):
-    _, _, best, far_best = pair_shifts(idx_ref, cover_ref, mask_ref)
-    top = jnp.maximum(best, far_best)
+def chip_join_kernel(heads, table_ref, own_ref, other_ref, _, merged_ref):
+    own_shift, other_shift = table_ref[4:5, :], table_ref[5:6, :]
     for i in range(own_ref.shape[0]):
-        values, _ = joined(heads, own_ref, other_ref, i, best - top, far_best - top)
+        values, _ = joined(heads, own_ref, other_ref, i, own_shift, other_shift)
         merged_ref[i] = values.astype(jnp.bfloat16)
 
 
@@ -556,22 +704,6 @@
 
     chunks = pieces // 2
 
-    *kept_rows, bias_tile = call(
-        functools.partial(norm_kernel, heads),
-        (pieces,),
-        [
-            pl.BlockSpec((piece_rows, channels, cols), lambda p, s: (piece_of(p, s, pieces), 0, 0)),
-            whole(gain_row),
-            pl.BlockSpec((heads, channels), lambda *_: (0, 0)),
-        ],
-        [vmem] * (2 * chunks + 1),
-        [jax.ShapeDtypeStruct((2 * piece_rows, channels, cols), bf16)] * (2 * chunks)
-        + [jax.ShapeDtypeStruct((heads, rows, cols), bf16)],
-        [pltpu.VMEM((heads, piece_rows, cols), f32), pltpu.VMEM((channels, cols), f32)],
-    )(idx, stored, gain_row, in_hbm(w_bias.T))
-    norms, raws = kept_rows[::2], kept_rows[1::2]
-
-
     def plain_call(kernel, in_specs, out_shape, scratch=(), cost=1e6):
         return pl.pallas_call(
             kernel,
@@ -585,6 +717,25 @@
             compiler_params=pltpu.CompilerParams(vmem_limit_bytes=VMEM_GRANT),
         )
 
+    hbm = pl.BlockSpec(memory_space=pltpu.HBM)
+    flat_bias_w = in_hbm(w_bias.T)
+    *kept_rows, bias_tile = plain_call(
+        functools.partial(norm_kernel, heads),
+        [hbm, hbm, hbm],
+        [jax.ShapeDtypeStruct((2 * piece_rows, channels, cols), bf16)] * (2 * chunks)
+        + [jax.ShapeDtypeStruct((heads, rows, cols), bf16)],
+        [
+            pltpu.VMEM((pieces, heads, piece_rows, cols), f32),
+            pltpu.VMEM((channels, cols), f32),
+            pltpu.VMEM((pieces, piece_rows, channels, cols), bf16),
+            pltpu.VMEM((1, channels), f32),
+            pltpu.VMEM(flat_bias_w.shape, bf16),
+            pltpu.SemaphoreType.DMA((pieces + 2,)),
+        ],
+    )(stored, gain_row, flat_bias_w)
+    norms, raws = kept_rows[::2], kept_rows[1::2]
+
+
     tiles = [bias_tile]
     for turn in range(1, row_devs):
         perm = [(z, z ^ turn) for z in range(row_devs)]
@@ -596,15 +747,16 @@
     packed_shapes = [
         jax.ShapeDtypeStruct(pack_shape, bf16),
         jax.ShapeDtypeStruct((channels, cols), f32),
+        jax.ShapeDtypeStruct((8, cols), f32),
     ]
     with jax.named_scope("pack"):
-        pack, merge_gain_wide = call(
+        pack, merge_gain_wide, table = call(
             functools.partial(weight_kernel, heads),
             (1,),
-            [whole(w) for w in raw_weights],
+            [whole(w) for w in raw_weights] + [smem] * 2,
             [vmem] * len(packed_shapes),
             packed_shapes,
-        )(idx, *raw_weights)
+        )(idx, *raw_weights, cover, pair_mask)
     query_w = in_hbm(w_merge_q.T)
     query_w = in_hbm(w_merge_q.T)
     with jax.named_scope("query"):
@@ -623,18 +775,43 @@
         )(idx, main_pair, query_w)
     picked = plain_call(
         pick_kernel,
-        [smem] + [vmem] * row_devs + [anywhere] * 2,
+        [vmem] * row_devs + [anywhere] * 2,
         jax.ShapeDtypeStruct((tiles_per_col,) + bias_tile.shape, bf16),
-    )(idx, *tiles, pack, main_query)
+    )(*tiles, pack, main_query)
     far_tiles = lax.ppermute(picked, "col", swap)
     half_shape = jax.ShapeDtypeStruct((heads, cols, cols), f32)
-    own_bias = plain_call(own_bias_kernel, [smem] * 3 + [vmem] * row_devs, half_shape)(
-        idx, cover, pair_mask, *tiles
-    )
-    far_bias = plain_call(far_bias_kernel, [smem] * 3 + [vmem], half_shape)(
-        idx, cover, pair_mask, far_tiles
-    )
-    fars += [lax.ppermute(norm, "col", swap) for norm in norms[1:]]
+    own_bias = plain_call(own_bias_kernel, [vmem] * (row_devs + 1), half_shape)(
+        table, *tiles
+    )
+    after = own_bias
+    nears = []
+    near_shapes = [
+        jax.ShapeDtypeStruct((piece_rows,) + shape, dtype)
+        for shape, dtype in (
+            ((heads, channels, cols), bf16),
+            ((hidden, cols), f32),
+            ((hidden, cols), bf16),
+            ((heads, cols, cols), f32),
+            ((heads, 8, cols), f32),
+        )
+    ]
+    for side in range(2):
+        with jax.named_scope("near%d" % side):
+            nears.append(
+                plain_call(
+                    functools.partial(near_kernel, heads, side * piece_rows),
+                    [vmem] * 3 + [anywhere],
+                    near_shapes,
+                    [pltpu.VMEM((piece_rows, cols, channels), bf16)],
+                    2e9,
+                )(norms[0], own_bias, pack, after)
+            )
+        after = nears[-1][-1]
+    far_bias = plain_call(far_bias_kernel, [vmem, vmem, anywhere], half_shape)(
+        table, far_tiles, after
+    )
+    held_back = lax.optimization_barrier((norms[1:], picked))[0]
+    fars += [lax.ppermute(norm, "col", swap) for norm in held_back]
 
     fresh, states, pair_states = [], [], []
     after = far_bias
@@ -643,25 +820,45 @@
     state_shape = jax.ShapeDtypeStruct((piece_rows, hidden + 2 * heads, cols), bf16)
     for piece in range(pieces):
         chunk, side = piece // 2, piece % 2
-        with jax.named_scope("attend%d" % piece):
-            rows_out, state = plain_call(
-                functools.partial(attend_kernel, heads, side * piece_rows, piece * piece_rows),
-                [vmem] * 8 + [anywhere],
-                [jax.ShapeDtypeStruct((piece_rows, channels, cols), bf16), state_shape],
-                [
-                    pltpu.VMEM((piece_rows, col_devs * cols, channels), bf16),
-                    pltpu.VMEM((piece_rows, heads, channels, cols), bf16),
-                    pltpu.VMEM((piece_rows, hidden, cols), f32),
-                    pltpu.VMEM((piece_rows, heads, 2 * dim, col_devs * cols), bf16),
-                    pltpu.VMEM((2, heads, col_devs * cols, cols), f32),
-                    pltpu.VMEM((2, heads, 8, cols), f32),
-                    pltpu.VMEM((piece_rows, hidden, cols), bf16),
-                ],
-                6e9,
-            )(
-                raws[chunk], norms[chunk], fars[chunk], main_query, own_bias, far_bias, pack,
-                merge_gain_wide, after,
-            )
+        row_shapes = [jax.ShapeDtypeStruct((piece_rows, channels, cols), bf16), state_shape]
+        if chunk == 0:
+            with jax.named_scope("attend%d" % piece):
+                rows_out, state = plain_call(
+                    functools.partial(late_kernel, heads, side * piece_rows, piece * piece_rows),
+                    [vmem] * 11 + [anywhere],
+                    row_shapes,
+                    [
+                        pltpu.VMEM((piece_rows, cols, channels), bf16),
+                        pltpu.VMEM((piece_rows, heads, 2 * dim, col_devs * cols), bf16),
+                        pltpu.VMEM((2, heads, cols, cols), f32),
+                        pltpu.VMEM((2, heads, 8, cols), f32),
+                        pltpu.VMEM((piece_rows, hidden, cols), bf16),
+                    ],
+                    6e9,
+                )(
+                    raws[chunk], fars[chunk], main_query, far_bias, pack, merge_gain_wide,
+                    *nears[side], after,
+                )
+        else:
+            with jax.named_scope("attend%d" % piece):
+                rows_out, state = plain_call(
+                    functools.partial(attend_kernel, heads, side * piece_rows, piece * piece_rows),
+                    [vmem] * 8 + [anywhere],
+                    [jax.ShapeDtypeStruct((piece_rows, channels, cols), bf16), state_shape],
+                    [
+                        pltpu.VMEM((piece_rows, col_devs * cols, channels), bf16),
+                        pltpu.VMEM((piece_rows, heads, channels, cols), bf16),
+                        pltpu.VMEM((piece_rows, hidden, cols), f32),
+                        pltpu.VMEM((piece_rows, heads, 2 * dim, col_devs * cols), bf16),
+                        pltpu.VMEM((2, heads, col_devs * cols, cols), f32),
+                        pltpu.VMEM((2, heads, 8, cols), f32),
+                        pltpu.VMEM((piece_rows, hidden, cols), bf16),
+                    ],
+                    6e9,
+                )(
+                    raws[chunk], norms[chunk], fars[chunk], main_query, own_bias, far_bias, pack,
+                    merge_gain_wide, after,
+                )
         fresh.append(rows_out)
         states.append(state)
         after = state
@@ -669,9 +866,9 @@
             with jax.named_scope("corejoin%d" % chunk):
                 after = plain_call(
                     functools.partial(core_join_kernel, heads),
-                    [smem] * 3 + [vmem] * 2,
+                    [vmem] * 3,
                     state_shape,
-                )(idx, cover, pair_mask, state, swapped)
+                )(table, state, swapped)
             pair_states.append(after)
         else:
             with jax.named_scope("coreswap%d" % chunk):
@@ -688,9 +885,9 @@
         with jax.named_scope("chipjoin%d" % chunk):
             merged = plain_call(
                 functools.partial(chip_join_kernel, heads),
-                [smem] * 3 + [vmem] * 2 + [anywhere],
+                [vmem] * 3 + [anywhere],
                 merged_shape,
-            )(idx, cover, pair_mask, pair_state, far_state, token)
+            )(table, pair_state, far_state, token)
         with jax.named_scope("lastswap%d" % chunk):
             merged_other = lax.ppermute(merged, "tmpl", cores)
 

time: 57 us -> 52.9 us (0.928)
  Pallas kernels: 35 us -> 31 us
  waiting for transfers between devices: 8.57 us -> 7.28 us
  starting transfers between devices: 12.2 us -> 13.4 us
    pallas_call x4 -> x2, Pallas kernels: 14.1 us -> 7.08 us  [fused_on_device(): plain_call(functools.partial(attend_kernel, heads, side * piece_rows, pie...]
    pallas_call x8 -> x12, Pallas kernels: 9.31 us -> 12.4 us  [the longest x2 6.09 us: fused_on_device(): plain_call(functools.partial(late_kernel, heads, side * piece_rows, piece...]
    ppermute x1, waiting for transfers between devices: 3.18 us -> 1.53 us  [fused_on_device(): far_tiles = lax.ppermute(picked, 'col', swap)]
    ppermute x2, starting transfers between devices: 2.16 us -> 3.34 us  [fused_on_device(): far_state = lax.ppermute(pair_state, 'tmpl', chips)]
    ppermute x1, waiting for transfers between devices: 0.01 us -> 1.03 us  [fused_on_device(): fars += [lax.ppermute(norm, 'col', swap) for norm in held_back]]
  transfers between devices with their start and end apart: 12 -> 12, of which waited for: 4 -> 5; matrix products, arithmetic and copies ran while one was open for 0% -> 0% of each run, Pallas kernels for 51% -> 51%
where the time goes in v4:
time: 52.9 us; the launch traced here: 52.6 us
  Pallas kernels  31 us (59%)
  starting transfers between devices  13.4 us (25%)
  waiting for transfers between devices  7.28 us (14%)
  between operations  0.81 us (2%)
    pallas_call x2, Pallas kernels, fused_on_device(): plain_call(functools.partial(attend_kernel, heads, side * piece_rows, pie...  7.08 us
    pallas_call x2, Pallas kernels, fused_on_device(): plain_call(functools.partial(late_kernel, heads, side * piece_rows, piece...  6.09 us
    ppermute x3, starting transfers between devices, fused_on_device(): tiles.append(lax.ppermute(bias_tile, 'row', perm))  4.39 us
    pallas_call x1, Pallas kernels, fused_on_device(): call(functools.partial(query_kernel, dim ** (-0.5)), (pieces,), [pl.Block...  3.65 us
    pallas_call x2, Pallas kernels, fused_on_device(): call(embed_kernel, (1,), [vmem, vmem, anywhere], pl.BlockSpec((piece_rows...  3.35 us
    ppermute x2, starting transfers between devices, fused_on_device(): far_state = lax.ppermute(pair_state, 'tmpl', chips)  3.34 us
    ppermute x1, starting transfers between devices, fused_on_device(): fars = [lax.ppermute(norms[0], 'col', swap)]  3.06 us
    pallas_call x1, Pallas kernels, fused_on_device(): call(finish_kernel, (pieces,), [vmem] * (pieces + 3), [pl.BlockSpec((piec...  3.01 us
  transfers between devices with their start and end apart: 12, of which 5 were waited for; matrix products, arithmetic and copies ran while one was open for 0% of the time, Pallas kernels for 51%

profile of v4, /device:TPU:0, one launch (start us, length us, event | category | flops | bytes accessed | tf_op | source)
XLA Modules:
  0.0 52.6 jit_solution(4250825365701869833)
XLA Ops:
  0.6 2.5 %shard_map.131 = (bf16[32,64,128]{2,1,0:T(8,128)(2,1)S(1)}, bf16[32,64,128]{2,1,0:T(8,128)(2,1)S(1)}, bf16[32,64,128]{2,1,0:T(8,128)(2,1)S(1)}, bf16[32,64,128]{2,1,0:T(8,128)(2,1)S(1)}, bf16[4,64,128]{2,1,0:T(8,128)(2,1)S(1)}) custom-call(bf16[64,64,128]{2,1,0:T(8,128)(2,1)} %bitcast.17, f32[1,64]{1,0:T(1,128)} %bitcast.20, bf16[4,64]{1,0:T(4,128)(2,1)} %bitcast.19), custom_call_target="tpu_custom_call" | custom-call | flops 1000000 | bytes 1048576 | tf_op jit(solution)/shard_map/pallas_call | solution.py:722
  3.1 3.1 %collective-permute-start = (bf16[32,64,128]{2,1,0:T(8,128)(2,1)S(1)}, bf16[32,64,128]{2,1,0:T(8,128)(2,1)S(1)}, u32[]{:S(2)}, u32[]{:S(2)}) collective-permute-start(bf16[32,64,128]{2,1,0:T(8,128)(2,1)S(1)} %get-tuple-element.33.own_ref), channel_id=1, source_target_pairs={{0,1},{1,0},{2,3},{3,2},{4,5},{5,4},{6,7},{7,6},{8,9},{9,8},{10,11... | collective-permute-start | bytes 1572872 | tf_op jit(solution)/shard_map/ppermute | solution.py:744
  6.2 1.6 %collective-permute-start.1 = (bf16[4,64,128]{2,1,0:T(8,128)(2,1)S(1)}, bf16[4,64,128]{2,1,0:T(8,128)(2,1)S(1)}, u32[]{:S(2)}, u32[]{:S(2)}) collective-permute-start(bf16[4,64,128]{2,1,0:T(8,128)(2,1)S(1)} %get-tuple-element.35.refs_0_), channel_id=1, source_target_pairs={{0,2},{2,0},{4,6},{6,4},{1,3},{3,1},{5,7},{7,5},{8,10},{10,8},{12,... | collective-permute-start | bytes 196616 | tf_op jit(solution)/shard_map/ppermute | solution.py:742
  7.7 2.6 %collective-permute-start.2 = (bf16[4,64,128]{2,1,0:T(8,128)(2,1)S(1)}, bf16[4,64,128]{2,1,0:T(8,128)(2,1)S(1)}, u32[]{:S(2)}, u32[]{:S(2)}) collective-permute-start(bf16[4,64,128]{2,1,0:T(8,128)(2,1)S(1)} %get-tuple-element.35.refs_0_), channel_id=1, source_target_pairs={{0,4},{2,6},{4,0},{6,2},{1,5},{3,7},{5,1},{7,3},{8,12},{10,14},{12... | collective-permute-start | bytes 196616 | tf_op jit(solution)/shard_map/ppermute | solution.py:742
  10.3 0.2 collective-permute-start.3
  10.5 0.1 stack.23.idx_ref
  10.6 0.0 copy-start.1
  10.6 0.0 copy-start.2
  10.6 3.7 %query.1.refs_5_.main_query = f32[64,64,128]{2,1,0:T(8,128)S(1)} custom-call(s32[5]{0:T(128)S(1)} %stack.23.idx_ref, bf16[64,128,128]{2,1,0:T(8,128)(2,1)} %main_ref.1, bf16[64,128]{1,0:T(8,128)(2,1)} %bitcast.18), custom_call_target="tpu_custom_call" | custom-call | flops 1000000 | bytes 1048576 | tf_op jit(solution)/shard_map/query/pallas_call | solution.py:763
  14.3 0.0 copy-done.1
  14.3 0.0 copy-done.2
  14.3 1.6 %pack.1 = (bf16[576,64]{1,0:T(8,128)(2,1)S(1)}, f32[64,128]{1,0:T(8,128)S(1)}, f32[8,128]{1,0:T(8,128)S(1)}) custom-call(s32[5]{0:T(128)S(1)} %stack.23.idx_ref, bf16[64,256]{1,0:T(8,128)(2,1)} %project_ref.1, bf16[64,64]{1,0:T(8,128)(2,1)} %tri_out_ref.1, bf16[64,128]{1,0:T(8,128)(2,1)} %kv_ref.1, f32[1,64]{1,0:T(1,128)} %bitcast.21, s32[2,4]{1,0:T(2,128)S(1)} %bitcast.16, ...), custom_call_target="tpu_custom_call" | custom-call | flops 1000000 | bytes 1048576 | tf_op jit(solution)/shard_map/pack/pallas_call | solution.py:753
  15.9 0.0 collective-permute-done.1.refs_1_
  15.9 0.0 collective-permute-done.2.refs_2_
  15.9 0.5 collective-permute-done.3.refs_3_
  16.4 0.6 %collective-permute-start.4 = (bf16[2,4,64,128]{3,2,1,0:T(8,128)(2,1)S(1)}, bf16[2,4,64,128]{3,2,1,0:T(8,128)(2,1)S(1)}, u32[]{:S(2)}, u32[]{:S(2)}) collective-permute-start(bf16[2,4,64,128]{3,2,1,0:T(8,128)(2,1)S(1)} %shard_map.132), channel_id=1, source_target_pairs={{0,1},{1,0},{2,3},{3,2},{4,5},{5,4},{6,7},{7,6},{8,9},{9,8},{10,11... | collective-permute-start | bytes 393224 | tf_op jit(solution)/shard_map/ppermute | solution.py:781
  17.0 1.5 %collective-permute-start.5 = (bf16[32,64,128]{2,1,0:T(8,128)(2,1)S(1)}, bf16[32,64,128]{2,1,0:T(8,128)(2,1)S(1)}, u32[]{:S(2)}, u32[]{:S(2)}) collective-permute-start(bf16[32,64,128]{2,1,0:T(8,128)(2,1)S(1)} %get-tuple-element.53.own_ref), channel_id=1, source_target_pairs={{0,1},{1,0},{2,3},{3,2},{4,5},{5,4},{6,7},{7,6},{8,9},{9,8},{10,11... | collective-permute-start | bytes 1572872 | tf_op jit(solution)/shard_map/ppermute | solution.py:814
  18.5 0.6 %shard_map.133.own_bias_ref.after_ref = f32[4,128,128]{2,1,0:T(8,128)S(1)} custom-call(f32[8,128]{1,0:T(8,128)S(1)} %get-tuple-element.34.table_ref, bf16[4,64,128]{2,1,0:T(8,128)(2,1)S(1)} %get-tuple-element.35.refs_0_, bf16[4,64,128]{2,1,0:T(8,128)(2,1)S(1)} %collective-permute-done.1.refs_1_, bf16[4,64,128]{2,1,0:T(8,128)(2,1)S(1)} %collective-permute-done.2.refs_2_, ...), custom_call_target="tpu_custom_call" | custom-call | flops 1000000 | bytes 1048576 | tf_op jit(solution)/shard_map/pallas_call | solution.py:783
  19.1 1.1 %near0.1 = (bf16[16,4,64,128]{3,2,1,0:T(8,128)(2,1)S(1)}, f32[16,64,128]{2,1,0:T(8,128)S(1)}, bf16[16,64,128]{2,1,0:T(8,128)(2,1)S(1)}, f32[16,4,128,128]{3,2,1,0:T(8,128)S(1)}, f32[16,4,8,128]{3,2,1,0:T(8,128)S(1)}) custom-call(bf16[32,64,128]{2,1,0:T(8,128)(2,1)S(1)} %get-tuple-element.33.own_ref, f32[4,128,128]{2,1,0:T(8,128)S(1)} %shard_map.133.own_bias_ref.after_ref, ...), custom_call_target="tpu_custom_call" | custom-call | flops 2000000000 | bytes 1048576 | tf_op jit(solution)/shard_map/near0/pallas_call | solution.py:801
  20.2 1.1 %near1.1 = (bf16[16,4,64,128]{3,2,1,0:T(8,128)(2,1)S(1)}, f32[16,64,128]{2,1,0:T(8,128)S(1)}, bf16[16,64,128]{2,1,0:T(8,128)(2,1)S(1)}, f32[16,4,128,128]{3,2,1,0:T(8,128)S(1)}, f32[16,4,8,128]{3,2,1,0:T(8,128)S(1)}) custom-call(bf16[32,64,128]{2,1,0:T(8,128)(2,1)S(1)} %get-tuple-element.33.own_ref, f32[4,128,128]{2,1,0:T(8,128)S(1)} %shard_map.133.own_bias_ref.after_ref, ...), custom_call_target="tpu_custom_call" | custom-call | flops 2000000000 | bytes 1048576 | tf_op jit(solution)/shard_map/near1/pallas_call | solution.py:801
  21.3 1.5 %collective-permute-done.4.tiles_ref = bf16[2,4,64,128]{3,2,1,0:T(8,128)(2,1)S(1)} collective-permute-done((bf16[2,4,64,128]{3,2,1,0:T(8,128)(2,1)S(1)}, bf16[2,4,64,128]{3,2,1,0:T(8,128)(2,1)S(1)}, u32[]{:S(2)}, u32[]{:S(2)}) %collective-permute-start.4) | collective-permute-done | bytes 131104 | tf_op jit(solution)/shard_map/ppermute | solution.py:781
  22.8 0.3 shard_map.134.far_bias_ref.after_ref
  23.1 0.0 collective-permute-done.far_ref
  23.1 3.0 %attend0.1 = (bf16[16,64,128]{2,1,0:T(8,128)(2,1)S(1)}, bf16[16,72,128]{2,1,0:T(8,128)(2,1)S(1)}) custom-call(bf16[32,64,128]{2,1,0:T(8,128)(2,1)S(1)} %get-tuple-element.32.x_ref, bf16[32,64,128]{2,1,0:T(8,128)(2,1)S(1)} %collective-permute-done.far_ref, f32[64,64,128]{2,1,0:T(8,128)S(1)} %query.1.refs_5_.main_query, ...), custom_call_target="tpu_custom_call" | custom-call | flops 6000000000 | bytes 1048576 | tf_op jit(solution)/shard_map/attend0/pallas_call | solution.py:826
  26.2 0.1 collective-permute-start.6
  26.3 3.1 %attend1.1 = (bf16[16,64,128]{2,1,0:T(8,128)(2,1)S(1)}, bf16[16,72,128]{2,1,0:T(8,128)(2,1)S(1)}) custom-call(bf16[32,64,128]{2,1,0:T(8,128)(2,1)S(1)} %get-tuple-element.32.x_ref, bf16[32,64,128]{2,1,0:T(8,128)(2,1)S(1)} %collective-permute-done.far_ref, f32[64,64,128]{2,1,0:T(8,128)S(1)} %query.1.refs_5_.main_query, ...), custom_call_target="tpu_custom_call" | custom-call | flops 6000000000 | bytes 1048576 | tf_op jit(solution)/shard_map/attend1/pallas_call | solution.py:826
  29.3 0.0 collective-permute-done.6.other_ref
  29.3 0.2 corejoin0.1.after_ref.own_ref
  29.5 1.6 %collective-permute-start.7 = (bf16[16,72,128]{2,1,0:T(8,128)(2,1)S(1)}, bf16[16,72,128]{2,1,0:T(8,128)(2,1)S(1)}, u32[]{:S(2)}, u32[]{:S(2)}) collective-permute-start(bf16[16,72,128]{2,1,0:T(8,128)(2,1)S(1)} %corejoin0.1.after_ref.own_ref), channel_id=1, source_target_pairs={{0,16},{8,24},{16,0},{24,8},{1,17},{9,25},{17,1},{25,9},{2,18},{10... | collective-permute-start | bytes 884744 | tf_op jit(solution)/shard_map/chipswap0/ppermute | solution.py:884
  31.1 1.0 %collective-permute-done.5.far_ref = bf16[32,64,128]{2,1,0:T(8,128)(2,1)S(1)} collective-permute-done((bf16[32,64,128]{2,1,0:T(8,128)(2,1)S(1)}, bf16[32,64,128]{2,1,0:T(8,128)(2,1)S(1)}, u32[]{:S(2)}, u32[]{:S(2)}) %collective-permute-start.5) | collective-permute-done | bytes 524320 | tf_op jit(solution)/shard_map/ppermute | solution.py:814
  32.1 3.4 %attend2.1 = (bf16[16,64,128]{2,1,0:T(8,128)(2,1)S(1)}, bf16[16,72,128]{2,1,0:T(8,128)(2,1)S(1)}) custom-call(bf16[32,64,128]{2,1,0:T(8,128)(2,1)S(1)} %get-tuple-element.51.x_ref, bf16[32,64,128]{2,1,0:T(8,128)(2,1)S(1)} %get-tuple-element.53.own_ref, bf16[32,64,128]{2,1,0:T(8,128)(2,1)S(1)} %collective-permute-done.5.far_ref, ...), custom_call_target="tpu_custom_call" | custom-call | flops 6000000000 | bytes 1048576 | tf_op jit(solution)/shard_map/attend2/pallas_call | solution.py:844
  35.6 0.0 copy-start
  35.6 0.1 collective-permute-start.8
  35.7 3.7 %attend3.1 = (bf16[16,64,128]{2,1,0:T(8,128)(2,1)S(1)}, bf16[16,72,128]{2,1,0:T(8,128)(2,1)S(1)}) custom-call(bf16[32,64,128]{2,1,0:T(8,128)(2,1)S(1)} %get-tuple-element.51.x_ref, bf16[32,64,128]{2,1,0:T(8,128)(2,1)S(1)} %get-tuple-element.53.own_ref, bf16[32,64,128]{2,1,0:T(8,128)(2,1)S(1)} %collective-permute-done.5.far_ref, ...), custom_call_target="tpu_custom_call" | custom-call | flops 6000000000 | bytes 1048576 | tf_op jit(solution)/shard_map/attend3/pallas_call | solution.py:844
  39.3 0.0 collective-permute-done.8.other_ref
  39.3 0.2 corejoin1.1._.own_ref
  39.5 1.8 %collective-permute-start.10 = (bf16[16,72,128]{2,1,0:T(8,128)(2,1)S(1)}, bf16[16,72,128]{2,1,0:T(8,128)(2,1)S(1)}, u32[]{:S(2)}, u32[]{:S(2)}) collective-permute-start(bf16[16,72,128]{2,1,0:T(8,128)(2,1)S(1)} %corejoin1.1._.own_ref), channel_id=1, source_target_pairs={{0,16},{8,24},{16,0},{24,8},{1,17},{9,25},{17,1},{25,9},{2,18},{10... | collective-permute-start | bytes 884744 | tf_op jit(solution)/shard_map/chipswap1/ppermute | solution.py:884
  41.3 0.0 collective-permute-done.7.other_ref
  41.3 0.2 chipjoin0.1.refs_5_
  41.5 0.3 collective-permute-start.9
  41.8 1.3 %collective-permute-done.9.refs_4_ = bf16[16,64,128]{2,1,0:T(8,128)(2,1)S(1)} collective-permute-done((bf16[16,64,128]{2,1,0:T(8,128)(2,1)S(1)}, bf16[16,64,128]{2,1,0:T(8,128)(2,1)S(1)}, u32[]{:S(2)}, u32[]{:S(2)}) %collective-permute-start.9) | collective-permute-done | bytes 262176 | tf_op jit(solution)/shard_map/lastswap0/ppermute | solution.py:892
  43.1 0.0 copy-done
  43.1 3.0 %finish.1 = (bf16[64,64,128]{2,1,0:T(8,128)(2,1)}, bf16[64,128,128]{2,1,0:T(8,128)(2,1)}, f32[8,128]{1,0:T(8,128)S(1)}) custom-call(s32[5]{0:T(128)S(1)} %stack.23.idx_ref, bf16[16,64,128]{2,1,0:T(8,128)(2,1)S(1)} %get-tuple-element.44.refs_0_, bf16[16,64,128]{2,1,0:T(8,128)(2,1)S(1)} %get-tuple-element.50.refs_1_, ...), custom_call_target="tpu_custom_call" | custom-call | flops 1000000 | bytes 1048576 | tf_op jit(solution)/shard_map/finish/pallas_call | solution.py:899
  46.1 2.9 %collective-permute-done.10.other_ref = bf16[16,72,128]{2,1,0:T(8,128)(2,1)S(1)} collective-permute-done((bf16[16,72,128]{2,1,0:T(8,128)(2,1)S(1)}, bf16[16,72,128]{2,1,0:T(8,128)(2,1)S(1)}, u32[]{:S(2)}, u32[]{:S(2)}) %collective-permute-start.10) | collective-permute-done | bytes 294944 | tf_op jit(solution)/shard_map/chipswap1/ppermute | solution.py:884
  49.0 0.2 chipjoin1.1.merged_ref
  49.2 0.1 collective-permute-start.11
  49.3 1.7 %embed3.1.prior_ref = bf16[64,128,128]{2,1,0:T(8,128)(2,1)} custom-call(s32[5]{0:T(128)S(1)} %stack.23.idx_ref, bf16[16,64,128]{2,1,0:T(8,128)(2,1)S(1)} %chipjoin1.1.merged_ref, bf16[64,128]{1,0:T(8,128)(2,1)S(1)} %copy-done, bf16[64,128,128]{2,1,0:T(8,128)(2,1)} %get-tuple-element.61.prior_ref), custom_call_target="tpu_custom_call", output_to_operand_aliasing={{}: (3, {})} | custom-call | flops 1000000 | bytes 1048576 | tf_op jit(solution)/shard_map/embed3/pallas_call | solution.py:919
  50.9 0.0 collective-permute-done.11.merged_ref
  50.9 1.7 %embed2.1 = bf16[64,128,128]{2,1,0:T(8,128)(2,1)} custom-call(s32[5]{0:T(128)S(1)} %stack.23.idx_ref, bf16[16,64,128]{2,1,0:T(8,128)(2,1)S(1)} %collective-permute-done.11.merged_ref, bf16[64,128]{1,0:T(8,128)(2,1)S(1)} %copy-done, bf16[64,128,128]{2,1,0:T(8,128)(2,1)} %embed3.1.prior_ref), custom_call_target="tpu_custom_call", output_to_operand_aliasing={{}: (3, {})} | custom-call | flops 1000000 | bytes 1048576 | tf_op jit(solution)/shard_map/embed2/pallas_call | solution.py:919
  (1 shorter events, 0.0 us)
Async XLA Ops:
  3.1 20.0 %collective-permute-start = (bf16[32,64,128]{2,1,0:T(8,128)(2,1)S(1)}, bf16[32,64,128]{2,1,0:T(8,128)(2,1)S(1)}, u32[]{:S(2)}, u32[]{:S(2)}) collective-permute-start(bf16[32,64,128]{2,1,0:T(8,128)(2,1)S(1)} %get-tuple-element.33.own_ref), channel_id=1, source_target_pairs={{0,1},{1,0},{2,3},{3,2},{4,5},{5,4},{6,7},{7,6},{8,9},{9,8},{10,11... | collective-permute-start | bytes 1572872 | tf_op jit(solution)/shard_map/ppermute | solution.py:744
  6.2 9.7 %collective-permute-start.1 = (bf16[4,64,128]{2,1,0:T(8,128)(2,1)S(1)}, bf16[4,64,128]{2,1,0:T(8,128)(2,1)S(1)}, u32[]{:S(2)}, u32[]{:S(2)}) collective-permute-start(bf16[4,64,128]{2,1,0:T(8,128)(2,1)S(1)} %get-tuple-element.35.refs_0_), channel_id=1, source_target_pairs={{0,2},{2,0},{4,6},{6,4},{1,3},{3,1},{5,7},{7,5},{8,10},{10,8},{12,... | collective-permute-start | bytes 196616 | tf_op jit(solution)/shard_map/ppermute | solution.py:742
  7.7 8.2 %collective-permute-start.2 = (bf16[4,64,128]{2,1,0:T(8,128)(2,1)S(1)}, bf16[4,64,128]{2,1,0:T(8,128)(2,1)S(1)}, u32[]{:S(2)}, u32[]{:S(2)}) collective-permute-start(bf16[4,64,128]{2,1,0:T(8,128)(2,1)S(1)} %get-tuple-element.35.refs_0_), channel_id=1, source_target_pairs={{0,4},{2,6},{4,0},{6,2},{1,5},{3,7},{5,1},{7,3},{8,12},{10,14},{12... | collective-permute-start | bytes 196616 | tf_op jit(solution)/shard_map/ppermute | solution.py:742
  10.3 6.1 %collective-permute-start.3 = (bf16[4,64,128]{2,1,0:T(8,128)(2,1)S(1)}, bf16[4,64,128]{2,1,0:T(8,128)(2,1)S(1)}, u32[]{:S(2)}, u32[]{:S(2)}) collective-permute-start(bf16[4,64,128]{2,1,0:T(8,128)(2,1)S(1)} %get-tuple-element.35.refs_0_), channel_id=1, source_target_pairs={{0,6},{2,4},{4,2},{6,0},{1,7},{3,5},{5,3},{7,1},{8,14},{10,12},{12... | collective-permute-start | bytes 196616 | tf_op jit(solution)/shard_map/ppermute | solution.py:742
  10.6 3.7 %copy-start.1 = (s32[4,2]{0,1:T(2,128)S(1)}, s32[4,2]{0,1:T(2,128)}, u32[]{:S(2)}) copy-start(s32[4,2]{0,1:T(2,128)} %param.14) | copy-start | bytes 100
  10.6 3.7 %copy-start.2 = (s32[2,2]{1,0:T(2,128)S(1)}, s32[2,2]{1,0:T(2,128)}, u32[]{:S(2)}) copy-start(s32[2,2]{1,0:T(2,128)} %mask_ref.1) | copy-start | bytes 52
  16.4 6.4 %collective-permute-start.4 = (bf16[2,4,64,128]{3,2,1,0:T(8,128)(2,1)S(1)}, bf16[2,4,64,128]{3,2,1,0:T(8,128)(2,1)S(1)}, u32[]{:S(2)}, u32[]{:S(2)}) collective-permute-start(bf16[2,4,64,128]{3,2,1,0:T(8,128)(2,1)S(1)} %shard_map.132), channel_id=1, source_target_pairs={{0,1},{1,0},{2,3},{3,2},{4,5},{5,4},{6,7},{7,6},{8,9},{9,8},{10,11... | collective-permute-start | bytes 393224 | tf_op jit(solution)/shard_map/ppermute | solution.py:781
  17.0 15.1 %collective-permute-start.5 = (bf16[32,64,128]{2,1,0:T(8,128)(2,1)S(1)}, bf16[32,64,128]{2,1,0:T(8,128)(2,1)S(1)}, u32[]{:S(2)}, u32[]{:S(2)}) collective-permute-start(bf16[32,64,128]{2,1,0:T(8,128)(2,1)S(1)} %get-tuple-element.53.own_ref), channel_id=1, source_target_pairs={{0,1},{1,0},{2,3},{3,2},{4,5},{5,4},{6,7},{7,6},{8,9},{9,8},{10,11... | collective-permute-start | bytes 1572872 | tf_op jit(solution)/shard_map/ppermute | solution.py:814
  26.2 3.1 %collective-permute-start.6 = (bf16[16,72,128]{2,1,0:T(8,128)(2,1)S(1)}, bf16[16,72,128]{2,1,0:T(8,128)(2,1)S(1)}, u32[]{:S(2)}, u32[]{:S(2)}) collective-permute-start(bf16[16,72,128]{2,1,0:T(8,128)(2,1)S(1)} %get-tuple-element.49.after_ref), channel_id=1, source_target_pairs={{0,8},{8,0},{16,24},{24,16},{1,9},{9,1},{17,25},{25,17},{2,10},{10... | collective-permute-start | bytes 884744 | tf_op jit(solution)/shard_map/coreswap0/ppermute | solution.py:875
  29.5 11.8 %collective-permute-start.7 = (bf16[16,72,128]{2,1,0:T(8,128)(2,1)S(1)}, bf16[16,72,128]{2,1,0:T(8,128)(2,1)S(1)}, u32[]{:S(2)}, u32[]{:S(2)}) collective-permute-start(bf16[16,72,128]{2,1,0:T(8,128)(2,1)S(1)} %corejoin0.1.after_ref.own_ref), channel_id=1, source_target_pairs={{0,16},{8,24},{16,0},{24,8},{1,17},{9,25},{17,1},{25,9},{2,18},{10... | collective-permute-start | bytes 884744 | tf_op jit(solution)/shard_map/chipswap0/ppermute | solution.py:884
  35.6 7.5 %copy-start = (bf16[64,128]{1,0:T(8,128)(2,1)S(1)}, bf16[64,128]{1,0:T(8,128)(2,1)}, u32[]{:S(2)}) copy-start(bf16[64,128]{1,0:T(8,128)(2,1)} %w_ref.3) | copy-start | bytes 49156
  35.6 3.7 %collective-permute-start.8 = (bf16[16,72,128]{2,1,0:T(8,128)(2,1)S(1)}, bf16[16,72,128]{2,1,0:T(8,128)(2,1)S(1)}, u32[]{:S(2)}, u32[]{:S(2)}) collective-permute-start(bf16[16,72,128]{2,1,0:T(8,128)(2,1)S(1)} %get-tuple-element.56.after_ref), channel_id=1, source_target_pairs={{0,8},{8,0},{16,24},{24,16},{1,9},{9,1},{17,25},{25,17},{2,10},{10... | collective-permute-start | bytes 884744 | tf_op jit(solution)/shard_map/coreswap1/ppermute | solution.py:875
  39.5 9.5 %collective-permute-start.10 = (bf16[16,72,128]{2,1,0:T(8,128)(2,1)S(1)}, bf16[16,72,128]{2,1,0:T(8,128)(2,1)S(1)}, u32[]{:S(2)}, u32[]{:S(2)}) collective-permute-start(bf16[16,72,128]{2,1,0:T(8,128)(2,1)S(1)} %corejoin1.1._.own_ref), channel_id=1, source_target_pairs={{0,16},{8,24},{16,0},{24,8},{1,17},{9,25},{17,1},{25,9},{2,18},{10... | collective-permute-start | bytes 884744 | tf_op jit(solution)/shard_map/chipswap1/ppermute | solution.py:884
  41.5 1.6 %collective-permute-start.9 = (bf16[16,64,128]{2,1,0:T(8,128)(2,1)S(1)}, bf16[16,64,128]{2,1,0:T(8,128)(2,1)S(1)}, u32[]{:S(2)}, u32[]{:S(2)}) collective-permute-start(bf16[16,64,128]{2,1,0:T(8,128)(2,1)S(1)} %chipjoin0.1.refs_5_), channel_id=1, source_target_pairs={{0,8},{8,0},{16,24},{24,16},{1,9},{9,1},{17,25},{25,17},{2,10},{10... | collective-permute-start | bytes 786440 | tf_op jit(solution)/shard_map/lastswap0/ppermute | solution.py:892
  49.2 1.8 %collective-permute-start.11 = (bf16[16,64,128]{2,1,0:T(8,128)(2,1)S(1)}, bf16[16,64,128]{2,1,0:T(8,128)(2,1)S(1)}, u32[]{:S(2)}, u32[]{:S(2)}) collective-permute-start(bf16[16,64,128]{2,1,0:T(8,128)(2,1)S(1)} %chipjoin1.1.merged_ref), channel_id=1, source_target_pairs={{0,8},{8,0},{16,24},{24,16},{1,9},{9,1},{17,25},{25,17},{2,10},{10... | collective-permute-start | bytes 786440 | tf_op jit(solution)/shard_map/lastswap1/ppermute | solution.py:892

commit v5 on v4

--- a/solution.py
+++ b/solution.py
@@ -341,7 +341,7 @@
 
 
 def own_bias_kernel(table_ref, *refs):
-    *tile_refs, out_ref = refs
+    *tile_refs, _, out_ref = refs
     idx_ref = places(tile_refs[0].shape[1])
     tiles_per_col = out_ref.shape[2] // tile_refs[0].shape[1]
     shift = table_ref[0:1, : tile_refs[0].shape[1]]
@@ -378,7 +378,7 @@
 def near_kernel(
     heads, skip, own_ref, own_bias_ref, pack_ref, after_ref, probes, gates, own_mix, near, near_tops, turned
 ):
-    step_rows, _, channels, cols = probes.shape
+    step_rows, _, channels, _ = probes.shape
     ends = split_pack(pack_ref, heads, gates.shape[1])
     for i in range(step_rows):
         own = own_ref[skip + i]
@@ -421,7 +421,7 @@
     tops,
     gated,
 ):
-    step_rows, channels, cols = out_ref.shape
+    step_rows, _, cols = out_ref.shape
     hidden = main_query.shape[1]
     dim = hidden // heads
     ends = split_pack(pack_ref, heads, hidden)
@@ -438,107 +438,32 @@
 
     slots = held.shape[0]
 
-    def score_row(i):
-        for h in range(heads):
-            scores = matmul(turned[i], probes[i, h]) + far_bias_ref[h]
-            held[i % slots, h] = scores
-            highest = jnp.max(scores, axis=0, keepdims=True)
-            tops[i % slots, h] = jnp.maximum(near_tops[i, h], highest)
-
-    def mix_row(i):
-        for h in range(heads):
-            top = tops[i % slots, h][:1]
-            weights = jnp.concatenate(
-                [
-                    jnp.exp2(part - top).astype(jnp.bfloat16)
-                    for part in (near[i, h], held[i % slots, h])
-                ],
-                axis=0,
-            )
-            mixed = matmul(mixers[i, h], weights)
-            span = slice(h * dim, (h + 1) * dim)
-            gated[i, span, :] = (
-                mixed[:dim] * (1.0 / mixed[dim : dim + 1]) * gates[i, span, :]
-            ).astype(jnp.bfloat16)
-
-    score_row(0)
-    for i in range(step_rows):
-        if i + 1 < step_rows:
-            score_row(i + 1)
-        mix_row(i)
-    write_rows(
-        heads, skip, query_skip, x_ref, main_query, pack_ref, gain_ref, gated, out_ref, state_ref
-    )
-
-
-def attend_kernel(
-    heads,
-    skip,
-    query_skip,
-    x_ref,
-    own_ref,
-    far_ref,
-    main_query,
-    own_bias_ref,
-    far_bias_ref,
-    pack_ref,
-    gain_ref,
-    after_ref,
-    out_ref,
-    state_ref,
-    turned,
-    probes,
-    gates,
-    mixers,
-    held,
-    tops,
-    gated,
-):
-    step_rows, channels, cols = out_ref.shape
-    hidden = main_query.shape[1]
-    dim = hidden // heads
-    row = heads * channels + hidden
-    first_w = pack_ref[:row, :]
-    value_w = pack_ref[row : row + hidden, :]
-    for i in range(step_rows):
-        own = own_ref[skip + i]
-        both = jnp.concatenate([own, far_ref[skip + i]], axis=1)
-        first = matmul(first_w, own)
-        for h in range(heads):
-            probes[i, h] = first[h * channels : (h + 1) * channels, :].astype(jnp.bfloat16)
-        gates[i] = jax.nn.sigmoid(first[heads * channels :, :])
-        values = matmul(value_w, both).astype(jnp.bfloat16)
-        for h in range(heads):
-            mixers[i, h, :dim, :] = values[h * dim : (h + 1) * dim, :]
-            mixers[i, h, dim:, :] = jnp.ones((mixers.shape[2] - dim, both.shape[1]), jnp.bfloat16)
-        turned[i] = both.T
-
-    slots = held.shape[0]
-
-    def score_row(i):
-        for h in range(heads):
-            scores = matmul(turned[i], probes[i, h])
-            near = scores[:cols] + own_bias_ref[h]
-            other = scores[cols:] + far_bias_ref[h]
-            held[i % slots, h, :cols] = near
-            held[i % slots, h, cols:] = other
-            highest = jnp.max(jnp.maximum(near, other), axis=0, keepdims=True)
-            tops[i % slots, h] = jnp.broadcast_to(highest, tops.shape[2:])
-
-    def mix_row(i):
-        for h in range(heads):
-            weights = jnp.exp2(held[i % slots, h] - tops[i % slots, h][:1])
-            mixed = matmul(mixers[i, h], weights.astype(jnp.bfloat16))
-            span = slice(h * dim, (h + 1) * dim)
-            gated[i, span, :] = (
-                mixed[:dim] * (1.0 / mixed[dim : dim + 1]) * gates[i, span, :]
-            ).astype(jnp.bfloat16)
-
-    score_row(0)
-    for i in range(step_rows):
-        if i + 1 < step_rows:
-            score_row(i + 1)
-        mix_row(i)
+    def score_row(i, h):
+        scores = matmul(turned[i], probes[i, h]) + far_bias_ref[h]
+        held[i % slots, h] = scores
+        highest = jnp.max(scores, axis=0, keepdims=True)
+        tops[i % slots, h] = jnp.maximum(near_tops[i, h], highest)
+
+    def mix_row(i, h):
+        top = tops[i % slots, h][:1]
+        weights = jnp.concatenate(
+            [
+                jnp.exp2(part - top).astype(jnp.bfloat16)
+                for part in (near[i, h], held[i % slots, h])
+            ],
+            axis=0,
+        )
+        mixed = matmul(mixers[i, h], weights)
+        span = slice(h * dim, (h + 1) * dim)
+        gated[i, span, :] = (
+            mixed[:dim] * (1.0 / mixed[dim : dim + 1]) * gates[i, span, :]
+        ).astype(jnp.bfloat16)
+
+    for unit in range(heads * step_rows + LEAD):
+        if unit < heads * step_rows:
+            score_row(*divmod(unit, heads))
+        if unit >= LEAD:
+            mix_row(*divmod(unit - LEAD, heads))
     write_rows(
         heads, skip, query_skip, x_ref, main_query, pack_ref, gain_ref, gated, out_ref, state_ref
     )
@@ -669,10 +594,9 @@
     idx = jnp.stack([templ % 2, templ, row_dev, col_dev, (row_dev * rows) // BLOCK]).astype(jnp.int32)
     pieces = PIECES
     piece_rows = rows // pieces
-    step_rows = STEP_ROWS
-    steps = piece_rows // step_rows
     stored = jnp.swapaxes(templ_pair[0], 1, 2)
     bf16, f32 = jnp.bfloat16, jnp.float32
+
     def in_hbm(array):
         return pltpu.with_memory_space_constraint(array, pltpu.HBM)
 
@@ -749,30 +673,25 @@
         jax.ShapeDtypeStruct((channels, cols), f32),
         jax.ShapeDtypeStruct((8, cols), f32),
     ]
-    with jax.named_scope("pack"):
-        pack, merge_gain_wide, table = call(
-            functools.partial(weight_kernel, heads),
-            (1,),
-            [whole(w) for w in raw_weights] + [smem] * 2,
-            [vmem] * len(packed_shapes),
-            packed_shapes,
-        )(idx, *raw_weights, cover, pair_mask)
+    pack, merge_gain_wide, table = call(
+        functools.partial(weight_kernel, heads),
+        (1,),
+        [whole(w) for w in raw_weights] + [smem] * 2,
+        [vmem] * len(packed_shapes),
+        packed_shapes,
+    )(idx, *raw_weights, cover, pair_mask)
     query_w = in_hbm(w_merge_q.T)
     query_w = in_hbm(w_merge_q.T)
-    with jax.named_scope("query"):
-        main_query = call(
-            functools.partial(query_kernel, dim ** (-0.5)),
-            (pieces,),
-            [
-                pl.BlockSpec(
-                    (piece_rows, cols, pair_ch),
-                    lambda g, s: (piece_of(g, s, pieces), 0, 0),
-                ),
-                whole(query_w),
-            ],
-            vmem,
-            jax.ShapeDtypeStruct((rows, hidden, cols), f32),
-        )(idx, main_pair, query_w)
+    main_query = call(
+        functools.partial(query_kernel, dim ** (-0.5)),
+        (pieces,),
+        [
+            pl.BlockSpec((piece_rows, cols, pair_ch), lambda g, s: (piece_of(g, s, pieces), 0, 0)),
+            whole(query_w),
+        ],
+        vmem,
+        jax.ShapeDtypeStruct((rows, hidden, cols), f32),
+    )(idx, main_pair, query_w)
     picked = plain_call(
         pick_kernel,
         [vmem] * row_devs + [anywhere] * 2,
@@ -780,8 +699,8 @@
     )(*tiles, pack, main_query)
     far_tiles = lax.ppermute(picked, "col", swap)
     half_shape = jax.ShapeDtypeStruct((heads, cols, cols), f32)
-    own_bias = plain_call(own_bias_kernel, [vmem] * (row_devs + 1), half_shape)(
-        table, *tiles
+    own_bias = plain_call(own_bias_kernel, [vmem] * (row_devs + 1) + [anywhere], half_shape)(
+        table, *tiles, picked
     )
     after = own_bias
     nears = []
@@ -795,18 +714,22 @@
             ((heads, 8, cols), f32),
         )
     ]
-    for side in range(2):
-        with jax.named_scope("near%d" % side):
-            nears.append(
-                plain_call(
-                    functools.partial(near_kernel, heads, side * piece_rows),
-                    [vmem] * 3 + [anywhere],
-                    near_shapes,
-                    [pltpu.VMEM((piece_rows, cols, channels), bf16)],
-                    2e9,
-                )(norms[0], own_bias, pack, after)
-            )
-        after = nears[-1][-1]
+
+    def near_part(after):
+        piece = len(nears)
+        nears.append(
+            plain_call(
+                functools.partial(near_kernel, heads, piece % 2 * piece_rows),
+                [vmem] * 3 + [anywhere],
+                near_shapes,
+                [pltpu.VMEM((piece_rows, cols, channels), bf16)],
+                2e9,
+            )(norms[piece // 2], own_bias, pack, after)
+        )
+        return nears[-1][-1]
+
+    while len(nears) < EARLY:
+        after = near_part(after)
     far_bias = plain_call(far_bias_kernel, [vmem, vmem, anywhere], half_shape)(
         table, far_tiles, after
     )
@@ -820,59 +743,38 @@
     state_shape = jax.ShapeDtypeStruct((piece_rows, hidden + 2 * heads, cols), bf16)
     for piece in range(pieces):
         chunk, side = piece // 2, piece % 2
-        row_shapes = [jax.ShapeDtypeStruct((piece_rows, channels, cols), bf16), state_shape]
-        if chunk == 0:
-            with jax.named_scope("attend%d" % piece):
-                rows_out, state = plain_call(
-                    functools.partial(late_kernel, heads, side * piece_rows, piece * piece_rows),
-                    [vmem] * 11 + [anywhere],
-                    row_shapes,
-                    [
-                        pltpu.VMEM((piece_rows, cols, channels), bf16),
-                        pltpu.VMEM((piece_rows, heads, 2 * dim, col_devs * cols), bf16),
-                        pltpu.VMEM((2, heads, cols, cols), f32),
-                        pltpu.VMEM((2, heads, 8, cols), f32),
-                        pltpu.VMEM((piece_rows, hidden, cols), bf16),
-                    ],
-                    6e9,
-                )(
-                    raws[chunk], fars[chunk], main_query, far_bias, pack, merge_gain_wide,
-                    *nears[side], after,
-                )
-        else:
-            with jax.named_scope("attend%d" % piece):
-                rows_out, state = plain_call(
-                    functools.partial(attend_kernel, heads, side * piece_rows, piece * piece_rows),
-                    [vmem] * 8 + [anywhere],
-                    [jax.ShapeDtypeStruct((piece_rows, channels, cols), bf16), state_shape],
-                    [
-                        pltpu.VMEM((piece_rows, col_devs * cols, channels), bf16),
-                        pltpu.VMEM((piece_rows, heads, channels, cols), bf16),
-                        pltpu.VMEM((piece_rows, hidden, cols), f32),
-                        pltpu.VMEM((piece_rows, heads, 2 * dim, col_devs * cols), bf16),
-                        pltpu.VMEM((2, heads, col_devs * cols, cols), f32),
-                        pltpu.VMEM((2, heads, 8, cols), f32),
-                        pltpu.VMEM((piece_rows, hidden, cols), bf16),
-                    ],
-                    6e9,
-                )(
-                    raws[chunk], norms[chunk], fars[chunk], main_query, own_bias, far_bias, pack,
-                    merge_gain_wide, after,
-                )
+        if len(nears) == piece:
+            after = near_part(after)
+        rows_out, state = plain_call(
+            functools.partial(late_kernel, heads, side * piece_rows, piece * piece_rows),
+            [vmem] * 11 + [anywhere],
+            [jax.ShapeDtypeStruct((piece_rows, channels, cols), bf16), state_shape],
+            [
+                pltpu.VMEM((piece_rows, cols, channels), bf16),
+                pltpu.VMEM((piece_rows, heads, 2 * dim, col_devs * cols), bf16),
+                pltpu.VMEM((2, heads, cols, cols), f32),
+                pltpu.VMEM((2, heads, 8, cols), f32),
+                pltpu.VMEM((piece_rows, hidden, cols), bf16),
+            ],
+            6e9,
+        )(
+            raws[chunk], fars[chunk], main_query, far_bias, pack, merge_gain_wide,
+            *nears[piece], after,
+        )
         fresh.append(rows_out)
         states.append(state)
         after = state
         if side:
-            with jax.named_scope("corejoin%d" % chunk):
-                after = plain_call(
-                    functools.partial(core_join_kernel, heads),
-                    [vmem] * 3,
-                    state_shape,
-                )(table, state, swapped)
+            after = plain_call(
+                functools.partial(core_join_kernel, heads),
+                [vmem] * 3,
+                state_shape,
+            )(table, state, swapped)
             pair_states.append(after)
+            if len(nears) < pieces:
+                after = near_part(after)
         else:
-            with jax.named_scope("coreswap%d" % chunk):
-                swapped = lax.ppermute(state, "tmpl", cores)
+            swapped = lax.ppermute(state, "tmpl", cores)
 
     emb_shape = jax.ShapeDtypeStruct(main_pair.shape, bf16)
     token = pair_states[-1]
@@ -880,54 +782,51 @@
     merged_shape = jax.ShapeDtypeStruct((piece_rows, hidden, cols), bf16)
     for chunk in range(chunks):
         pair_state = pair_states[chunk]
-        with jax.named_scope("chipswap%d" % chunk):
-            far_state = lax.ppermute(pair_state, "tmpl", chips)
-        with jax.named_scope("chipjoin%d" % chunk):
-            merged = plain_call(
-                functools.partial(chip_join_kernel, heads),
-                [vmem] * 3 + [anywhere],
-                merged_shape,
-            )(table, pair_state, far_state, token)
-        with jax.named_scope("lastswap%d" % chunk):
-            merged_other = lax.ppermute(merged, "tmpl", cores)
+        far_state = lax.ppermute(pair_state, "tmpl", chips)
+        merged = plain_call(
+            functools.partial(chip_join_kernel, heads),
+            [vmem] * 3 + [anywhere],
+            merged_shape,
+        )(table, pair_state, far_state, token)
+        merged_other = lax.ppermute(merged, "tmpl", cores)
 
         def at_piece(piece):
             return lambda g, s: (piece_of(piece, s, pieces), 0, 0)
 
         if chunk == 0:
-            with jax.named_scope("finish"):
-                out, emb, token = call(
-                    finish_kernel,
-                    (pieces,),
-                    [vmem] * (pieces + 3),
-                    [
-                        pl.BlockSpec(
-                            (piece_rows, channels, cols),
-                            lambda g, s: (piece_of(g, s, pieces), 0, 0),
-                        ),
-                        pl.BlockSpec(
-                            (piece_rows, cols, pair_ch),
-                            lambda g, s: (piece_of(jnp.minimum(g, 1), s, pieces), 0, 0),
-                        ),
-                        vmem,
-                    ],
-                    [jax.ShapeDtypeStruct(stored.shape, bf16), emb_shape, token_shape],
-                )(idx, *fresh, merged_other, merged, w_merge_out)
+            out, emb, token = call(
+                finish_kernel,
+                (pieces,),
+                [vmem] * (pieces + 3),
+                [
+                    pl.BlockSpec(
+                        (piece_rows, channels, cols),
+                        lambda g, s: (piece_of(g, s, pieces), 0, 0),
+                    ),
+                    pl.BlockSpec(
+                        (piece_rows, cols, pair_ch),
+                        lambda g, s: (piece_of(jnp.minimum(g, 1), s, pieces), 0, 0),
+                    ),
+                    vmem,
+                ],
+                [jax.ShapeDtypeStruct(stored.shape, bf16), emb_shape, token_shape],
+            )(idx, *fresh, merged_other, merged, w_merge_out)
         else:
             for piece, part in ((2 * chunk + 1, merged), (2 * chunk, merged_other)):
-                with jax.named_scope("embed%d" % piece):
-                    emb = call(
-                        embed_kernel,
-                        (1,),
-                        [vmem, vmem, anywhere],
-                        pl.BlockSpec((piece_rows, cols, pair_ch), at_piece(piece)),
-                        emb_shape,
-                        aliases={3: 0},
-                    )(idx, part, w_merge_out, emb)
+                emb = call(
+                    embed_kernel,
+                    (1,),
+                    [vmem, vmem, anywhere],
+                    pl.BlockSpec((piece_rows, cols, pair_ch), at_piece(piece)),
+                    emb_shape,
+                    aliases={3: 0},
+                )(idx, part, w_merge_out, emb)
     return (jnp.swapaxes(out, 1, 2)[None], emb)
 
 
 PIECES = 4
+EARLY = 3
+LEAD = 1
 VMEM_GRANT = 16 << 20
 STEP_ROWS = 8
 

time: 52.9 us -> 54.4 us (1.028)
  waiting for transfers between devices: 7.28 us -> 10.3 us
  Pallas kernels: 31 us -> 29.5 us
    pallas_call x5, Pallas kernels: 9.87 us -> 5.02 us  [the longest x4 4.46 us: near_part(): plain_call(functools.partial(near_kernel, heads, piece % 2 * piece_rows),...]
    pallas_call x2 -> x4, Pallas kernels: 6.09 us -> 9.37 us  [fused_on_device(): plain_call(functools.partial(late_kernel, heads, side * piece_rows, piece...]
    ppermute x1, waiting for transfers between devices: 1.53 us -> 4.41 us  [fused_on_device(): far_tiles = lax.ppermute(picked, 'col', swap)]
    ppermute x3, starting transfers between devices: 4.39 us -> 5.71 us  [fused_on_device(): tiles.append(lax.ppermute(bias_tile, 'row', perm))]
    ppermute x1, starting transfers between devices: 3.06 us -> 1.74 us  [fused_on_device(): fars = [lax.ppermute(norms[0], 'col', swap)]]
  transfers between devices with their start and end apart: 12 -> 12, of which waited for: 5 -> 4; matrix products, arithmetic and copies ran while one was open for 0% -> 0% of each run, Pallas kernels for 51% -> 47%
where the time goes in v5:
time: 54.4 us; the launch traced here: 54.1 us
  Pallas kernels  29.5 us (54%)
  starting transfers between devices  13.4 us (25%)
  waiting for transfers between devices  10.3 us (19%)
  between operations  0.84 us (2%)
    pallas_call x4, Pallas kernels, fused_on_device(): plain_call(functools.partial(late_kernel, heads, side * piece_rows, piece...  9.37 us
    ppermute x3, starting transfers between devices, fused_on_device(): tiles.append(lax.ppermute(bias_tile, 'row', perm))  5.71 us
    pallas_call x4, Pallas kernels, near_part(): plain_call(functools.partial(near_kernel, heads, piece % 2 * piece_rows),...  4.46 us
    ppermute x1, waiting for transfers between devices, fused_on_device(): far_tiles = lax.ppermute(picked, 'col', swap)  4.41 us
    pallas_call x1, Pallas kernels, fused_on_device(): call(functools.partial(query_kernel, dim ** (-0.5)), (pieces,), [pl.Block...  3.65 us
    pallas_call x2, Pallas kernels, fused_on_device(): call(embed_kernel, (1,), [vmem, vmem, anywhere], pl.BlockSpec((piece_rows...  3.35 us
    ppermute x2, starting transfers between devices, fused_on_device(): far_state = lax.ppermute(pair_state, 'tmpl', chips)  3.33 us
    ppermute x2, waiting for transfers between devices, fused_on_device(): far_state = lax.ppermute(pair_state, 'tmpl', chips)  3.11 us
  transfers between devices with their start and end apart: 12, of which 4 were waited for; matrix products, arithmetic and copies ran while one was open for 0% of the time, Pallas kernels for 47%

profile of v5, /device:TPU:0, one launch (start us, length us, event | category | flops | bytes accessed | tf_op | source)
XLA Modules:
  0.0 54.1 jit_solution(947358875208444121)
XLA Ops:
  0.6 2.5 %shard_map.131 = (bf16[32,64,128]{2,1,0:T(8,128)(2,1)S(1)}, bf16[32,64,128]{2,1,0:T(8,128)(2,1)S(1)}, bf16[32,64,128]{2,1,0:T(8,128)(2,1)S(1)}, bf16[32,64,128]{2,1,0:T(8,128)(2,1)S(1)}, bf16[4,64,128]{2,1,0:T(8,128)(2,1)S(1)}) custom-call(bf16[64,64,128]{2,1,0:T(8,128)(2,1)} %bitcast.17, f32[1,64]{1,0:T(1,128)} %bitcast.20, bf16[4,64]{1,0:T(4,128)(2,1)} %bitcast.19), custom_call_target="tpu_custom_call" | custom-call | flops 1000000 | bytes 1048576 | tf_op jit(solution)/shard_map/pallas_call | solution.py:646
  3.1 3.1 %collective-permute-start.1 = (bf16[4,64,128]{2,1,0:T(8,128)(2,1)S(1)}, bf16[4,64,128]{2,1,0:T(8,128)(2,1)S(1)}, u32[]{:S(2)}, u32[]{:S(2)}) collective-permute-start(bf16[4,64,128]{2,1,0:T(8,128)(2,1)S(1)} %get-tuple-element.45.refs_0_), channel_id=1, source_target_pairs={{0,2},{2,0},{4,6},{6,4},{1,3},{3,1},{5,7},{7,5},{8,10},{10,8},{12,... | collective-permute-start | bytes 196616 | tf_op jit(solution)/shard_map/ppermute | solution.py:666
  6.2 2.6 %collective-permute-start.2 = (bf16[4,64,128]{2,1,0:T(8,128)(2,1)S(1)}, bf16[4,64,128]{2,1,0:T(8,128)(2,1)S(1)}, u32[]{:S(2)}, u32[]{:S(2)}) collective-permute-start(bf16[4,64,128]{2,1,0:T(8,128)(2,1)S(1)} %get-tuple-element.45.refs_0_), channel_id=1, source_target_pairs={{0,4},{2,6},{4,0},{6,2},{1,5},{3,7},{5,1},{7,3},{8,12},{10,14},{12... | collective-permute-start | bytes 196616 | tf_op jit(solution)/shard_map/ppermute | solution.py:666
  8.8 0.0 collective-permute-start.3
  8.8 1.7 %collective-permute-start = (bf16[32,64,128]{2,1,0:T(8,128)(2,1)S(1)}, bf16[32,64,128]{2,1,0:T(8,128)(2,1)S(1)}, u32[]{:S(2)}, u32[]{:S(2)}) collective-permute-start(bf16[32,64,128]{2,1,0:T(8,128)(2,1)S(1)} %get-tuple-element.43.own_ref), channel_id=1, source_target_pairs={{0,1},{1,0},{2,3},{3,2},{4,5},{5,4},{6,7},{7,6},{8,9},{9,8},{10,11... | collective-permute-start | bytes 1572872 | tf_op jit(solution)/shard_map/ppermute | solution.py:668
  10.5 0.1 stack.23.idx_ref
  10.6 0.0 copy-start.1
  10.6 0.0 copy-start.2
  10.6 3.7 %shard_map.132.refs_5_.main_query = f32[64,64,128]{2,1,0:T(8,128)S(1)} custom-call(s32[5]{0:T(128)S(1)} %stack.23.idx_ref, bf16[64,128,128]{2,1,0:T(8,128)(2,1)} %main_ref.1, bf16[64,128]{1,0:T(8,128)(2,1)} %bitcast.18), custom_call_target="tpu_custom_call" | custom-call | flops 1000000 | bytes 1048576 | tf_op jit(solution)/shard_map/pallas_call | solution.py:685
  14.3 0.0 copy-done.1
  14.3 0.0 copy-done.2
  14.3 1.6 %shard_map.133 = (bf16[576,64]{1,0:T(8,128)(2,1)S(1)}, f32[64,128]{1,0:T(8,128)S(1)}, f32[8,128]{1,0:T(8,128)S(1)}) custom-call(s32[5]{0:T(128)S(1)} %stack.23.idx_ref, bf16[64,256]{1,0:T(8,128)(2,1)} %project_ref.1, bf16[64,64]{1,0:T(8,128)(2,1)} %tri_out_ref.1, bf16[64,128]{1,0:T(8,128)(2,1)} %kv_ref.1, f32[1,64]{1,0:T(1,128)} %bitcast.21, ...), custom_call_target="tpu_custom_call" | custom-call | flops 1000000 | bytes 1048576 | tf_op jit(solution)/shard_map/pallas_call | solution.py:676
  15.9 0.0 collective-permute-done.1.refs_1_
  15.9 0.0 collective-permute-done.2.refs_2_
  15.9 0.0 collective-permute-done.3.refs_3_
  15.9 0.1 shard_map.134.refs_4_
  16.0 0.5 collective-permute-start.4
  16.5 1.6 %collective-permute-start.5 = (bf16[32,64,128]{2,1,0:T(8,128)(2,1)S(1)}, bf16[32,64,128]{2,1,0:T(8,128)(2,1)S(1)}, u32[]{:S(2)}, u32[]{:S(2)}) collective-permute-start(bf16[32,64,128]{2,1,0:T(8,128)(2,1)S(1)} %get-tuple-element.64.own_ref), channel_id=1, source_target_pairs={{0,1},{1,0},{2,3},{3,2},{4,5},{5,4},{6,7},{7,6},{8,9},{9,8},{10,11... | collective-permute-start | bytes 1572872 | tf_op jit(solution)/shard_map/ppermute | solution.py:737
  18.1 0.6 %shard_map.135.own_bias_ref.after_ref = f32[4,128,128]{2,1,0:T(8,128)S(1)} custom-call(f32[8,128]{1,0:T(8,128)S(1)} %get-tuple-element.44.table_ref, bf16[4,64,128]{2,1,0:T(8,128)(2,1)S(1)} %get-tuple-element.45.refs_0_, bf16[4,64,128]{2,1,0:T(8,128)(2,1)S(1)} %collective-permute-done.1.refs_1_, bf16[4,64,128]{2,1,0:T(8,128)(2,1)S(1)} %collective-permute-done.2.refs_2_, ...), custom_call_target="tpu_custom_call" | custom-call | flops 1000000 | bytes 1048576 | tf_op jit(solution)/shard_map/pallas_call | solution.py:702
  18.6 1.1 %shard_map.136 = (bf16[16,4,64,128]{3,2,1,0:T(8,128)(2,1)S(1)}, f32[16,64,128]{2,1,0:T(8,128)S(1)}, bf16[16,64,128]{2,1,0:T(8,128)(2,1)S(1)}, f32[16,4,128,128]{3,2,1,0:T(8,128)S(1)}, f32[16,4,8,128]{3,2,1,0:T(8,128)S(1)}) custom-call(bf16[32,64,128]{2,1,0:T(8,128)(2,1)S(1)} %get-tuple-element.43.own_ref, ...), custom_call_target="tpu_custom_call" | custom-call | flops 2000000000 | bytes 1048576 | tf_op jit(solution)/shard_map/pallas_call | solution.py:721
  19.8 1.1 %shard_map.137 = (bf16[16,4,64,128]{3,2,1,0:T(8,128)(2,1)S(1)}, f32[16,64,128]{2,1,0:T(8,128)S(1)}, bf16[16,64,128]{2,1,0:T(8,128)(2,1)S(1)}, f32[16,4,128,128]{3,2,1,0:T(8,128)S(1)}, f32[16,4,8,128]{3,2,1,0:T(8,128)S(1)}) custom-call(bf16[32,64,128]{2,1,0:T(8,128)(2,1)S(1)} %get-tuple-element.43.own_ref, ...), custom_call_target="tpu_custom_call" | custom-call | flops 2000000000 | bytes 1048576 | tf_op jit(solution)/shard_map/pallas_call | solution.py:721
  20.9 1.1 %shard_map.138 = (bf16[16,4,64,128]{3,2,1,0:T(8,128)(2,1)S(1)}, f32[16,64,128]{2,1,0:T(8,128)S(1)}, bf16[16,64,128]{2,1,0:T(8,128)(2,1)S(1)}, f32[16,4,128,128]{3,2,1,0:T(8,128)S(1)}, f32[16,4,8,128]{3,2,1,0:T(8,128)S(1)}) custom-call(bf16[32,64,128]{2,1,0:T(8,128)(2,1)S(1)} %get-tuple-element.64.own_ref, ...), custom_call_target="tpu_custom_call" | custom-call | flops 2000000000 | bytes 1048576 | tf_op jit(solution)/shard_map/pallas_call | solution.py:721
  22.0 4.4 %collective-permute-done.4.tiles_ref = bf16[2,4,64,128]{3,2,1,0:T(8,128)(2,1)S(1)} collective-permute-done((bf16[2,4,64,128]{3,2,1,0:T(8,128)(2,1)S(1)}, bf16[2,4,64,128]{3,2,1,0:T(8,128)(2,1)S(1)}, u32[]{:S(2)}, u32[]{:S(2)}) %collective-permute-start.4) | collective-permute-done | bytes 131104 | tf_op jit(solution)/shard_map/ppermute | solution.py:700
  26.4 0.3 shard_map.139.far_bias_ref.after_ref
  26.7 0.0 collective-permute-done.far_ref
  26.7 2.3 %shard_map.140 = (bf16[16,64,128]{2,1,0:T(8,128)(2,1)S(1)}, bf16[16,72,128]{2,1,0:T(8,128)(2,1)S(1)}) custom-call(bf16[32,64,128]{2,1,0:T(8,128)(2,1)S(1)} %get-tuple-element.42.x_ref, bf16[32,64,128]{2,1,0:T(8,128)(2,1)S(1)} %collective-permute-done.far_ref, f32[64,64,128]{2,1,0:T(8,128)S(1)} %shard_map.132.refs_5_.main_query, ...), custom_call_target="tpu_custom_call" | custom-call | flops 6000000000 | bytes 1048576 | tf_op jit(solution)/shard_map/pallas_call | solution.py:748
  29.0 0.1 collective-permute-start.6
  29.1 2.3 %shard_map.141 = (bf16[16,64,128]{2,1,0:T(8,128)(2,1)S(1)}, bf16[16,72,128]{2,1,0:T(8,128)(2,1)S(1)}) custom-call(bf16[32,64,128]{2,1,0:T(8,128)(2,1)S(1)} %get-tuple-element.42.x_ref, bf16[32,64,128]{2,1,0:T(8,128)(2,1)S(1)} %collective-permute-done.far_ref, f32[64,64,128]{2,1,0:T(8,128)S(1)} %shard_map.132.refs_5_.main_query, ...), custom_call_target="tpu_custom_call" | custom-call | flops 6000000000 | bytes 1048576 | tf_op jit(solution)/shard_map/pallas_call | solution.py:748
  31.4 0.0 collective-permute-done.6.other_ref
  31.4 0.2 shard_map.142.after_ref.own_ref
  31.6 1.8 %collective-permute-start.7 = (bf16[16,72,128]{2,1,0:T(8,128)(2,1)S(1)}, bf16[16,72,128]{2,1,0:T(8,128)(2,1)S(1)}, u32[]{:S(2)}, u32[]{:S(2)}) collective-permute-start(bf16[16,72,128]{2,1,0:T(8,128)(2,1)S(1)} %shard_map.142.after_ref.own_ref), channel_id=1, source_target_pairs={{0,16},{8,24},{16,0},{24,8},{1,17},{9,25},{17,1},{25,9},{2,18},{10... | collective-permute-start | bytes 884744 | tf_op jit(solution)/shard_map/ppermute | solution.py:785
  33.4 1.1 %shard_map.143 = (bf16[16,4,64,128]{3,2,1,0:T(8,128)(2,1)S(1)}, f32[16,64,128]{2,1,0:T(8,128)S(1)}, bf16[16,64,128]{2,1,0:T(8,128)(2,1)S(1)}, f32[16,4,128,128]{3,2,1,0:T(8,128)S(1)}, f32[16,4,8,128]{3,2,1,0:T(8,128)S(1)}) custom-call(bf16[32,64,128]{2,1,0:T(8,128)(2,1)S(1)} %get-tuple-element.64.own_ref, ...), custom_call_target="tpu_custom_call" | custom-call | flops 2000000000 | bytes 1048576 | tf_op jit(solution)/shard_map/pallas_call | solution.py:721
  34.5 1.4 %collective-permute-done.5.far_ref = bf16[32,64,128]{2,1,0:T(8,128)(2,1)S(1)} collective-permute-done((bf16[32,64,128]{2,1,0:T(8,128)(2,1)S(1)}, bf16[32,64,128]{2,1,0:T(8,128)(2,1)S(1)}, u32[]{:S(2)}, u32[]{:S(2)}) %collective-permute-start.5) | collective-permute-done | bytes 524320 | tf_op jit(solution)/shard_map/ppermute | solution.py:737
  36.0 2.3 %shard_map.144 = (bf16[16,64,128]{2,1,0:T(8,128)(2,1)S(1)}, bf16[16,72,128]{2,1,0:T(8,128)(2,1)S(1)}) custom-call(bf16[32,64,128]{2,1,0:T(8,128)(2,1)S(1)} %get-tuple-element.63.x_ref, bf16[32,64,128]{2,1,0:T(8,128)(2,1)S(1)} %collective-permute-done.5.far_ref, f32[64,64,128]{2,1,0:T(8,128)S(1)} %shard_map.132.refs_5_.main_query, ...), custom_call_target="tpu_custom_call" | custom-call | flops 6000000000 | bytes 1048576 | tf_op jit(solution)/shard_map/pallas_call | solution.py:748
  38.2 0.1 collective-permute-start.8
  38.3 0.0 copy-start
  38.3 2.5 %shard_map.145 = (bf16[16,64,128]{2,1,0:T(8,128)(2,1)S(1)}, bf16[16,72,128]{2,1,0:T(8,128)(2,1)S(1)}) custom-call(bf16[32,64,128]{2,1,0:T(8,128)(2,1)S(1)} %get-tuple-element.63.x_ref, bf16[32,64,128]{2,1,0:T(8,128)(2,1)S(1)} %collective-permute-done.5.far_ref, f32[64,64,128]{2,1,0:T(8,128)S(1)} %shard_map.132.refs_5_.main_query, ...), custom_call_target="tpu_custom_call" | custom-call | flops 6000000000 | bytes 1048576 | tf_op jit(solution)/shard_map/pallas_call | solution.py:748
  40.8 0.0 collective-permute-done.8.other_ref
  40.9 0.2 shard_map.146._.own_ref
  41.1 1.6 %collective-permute-start.10 = (bf16[16,72,128]{2,1,0:T(8,128)(2,1)S(1)}, bf16[16,72,128]{2,1,0:T(8,128)(2,1)S(1)}, u32[]{:S(2)}, u32[]{:S(2)}) collective-permute-start(bf16[16,72,128]{2,1,0:T(8,128)(2,1)S(1)} %shard_map.146._.own_ref), channel_id=1, source_target_pairs={{0,16},{8,24},{16,0},{24,8},{1,17},{9,25},{17,1},{25,9},{2,18},{10... | collective-permute-start | bytes 884744 | tf_op jit(solution)/shard_map/ppermute | solution.py:785
  42.6 0.0 collective-permute-done.7.other_ref
  42.6 0.2 shard_map.147.refs_5_
  42.8 0.3 collective-permute-start.9
  43.1 1.3 %collective-permute-done.9.refs_4_ = bf16[16,64,128]{2,1,0:T(8,128)(2,1)S(1)} collective-permute-done((bf16[16,64,128]{2,1,0:T(8,128)(2,1)S(1)}, bf16[16,64,128]{2,1,0:T(8,128)(2,1)S(1)}, u32[]{:S(2)}, u32[]{:S(2)}) %collective-permute-start.9) | collective-permute-done | bytes 262176 | tf_op jit(solution)/shard_map/ppermute | solution.py:791
  44.4 0.0 copy-done
  44.4 3.0 %shard_map.148 = (bf16[64,64,128]{2,1,0:T(8,128)(2,1)}, bf16[64,128,128]{2,1,0:T(8,128)(2,1)}, f32[8,128]{1,0:T(8,128)S(1)}) custom-call(s32[5]{0:T(128)S(1)} %stack.23.idx_ref, bf16[16,64,128]{2,1,0:T(8,128)(2,1)S(1)} %get-tuple-element.56.refs_0_, bf16[16,64,128]{2,1,0:T(8,128)(2,1)S(1)} %get-tuple-element.62.refs_1_, ...), custom_call_target="tpu_custom_call" | custom-call | flops 1000000 | bytes 1048576 | tf_op jit(solution)/shard_map/pallas_call | solution.py:797
  47.4 3.1 %collective-permute-done.10.other_ref = bf16[16,72,128]{2,1,0:T(8,128)(2,1)S(1)} collective-permute-done((bf16[16,72,128]{2,1,0:T(8,128)(2,1)S(1)}, bf16[16,72,128]{2,1,0:T(8,128)(2,1)S(1)}, u32[]{:S(2)}, u32[]{:S(2)}) %collective-permute-start.10) | collective-permute-done | bytes 294944 | tf_op jit(solution)/shard_map/ppermute | solution.py:785
  50.5 0.2 shard_map.149.merged_ref
  50.7 0.1 collective-permute-start.11
  50.8 1.7 %shard_map.150.prior_ref = bf16[64,128,128]{2,1,0:T(8,128)(2,1)} custom-call(s32[5]{0:T(128)S(1)} %stack.23.idx_ref, bf16[16,64,128]{2,1,0:T(8,128)(2,1)S(1)} %shard_map.149.merged_ref, bf16[64,128]{1,0:T(8,128)(2,1)S(1)} %copy-done, bf16[64,128,128]{2,1,0:T(8,128)(2,1)} %get-tuple-element.81.prior_ref), custom_call_target="tpu_custom_call", output_to_operand_aliasing={{}: (3, {})} | custom-call | flops 1000000 | bytes 1048576 | tf_op jit(solution)/shard_map/pallas_call | solution.py:816
  52.5 0.0 collective-permute-done.11.merged_ref
  52.5 1.7 %shard_map.151 = bf16[64,128,128]{2,1,0:T(8,128)(2,1)} custom-call(s32[5]{0:T(128)S(1)} %stack.23.idx_ref, bf16[16,64,128]{2,1,0:T(8,128)(2,1)S(1)} %collective-permute-done.11.merged_ref, bf16[64,128]{1,0:T(8,128)(2,1)S(1)} %copy-done, bf16[64,128,128]{2,1,0:T(8,128)(2,1)} %shard_map.150.prior_ref), custom_call_target="tpu_custom_call", output_to_operand_aliasing={{}: (3, {})} | custom-call | flops 1000000 | bytes 1048576 | tf_op jit(solution)/shard_map/pallas_call | solution.py:816
Async XLA Ops:
  3.1 12.8 %collective-permute-start.1 = (bf16[4,64,128]{2,1,0:T(8,128)(2,1)S(1)}, bf16[4,64,128]{2,1,0:T(8,128)(2,1)S(1)}, u32[]{:S(2)}, u32[]{:S(2)}) collective-permute-start(bf16[4,64,128]{2,1,0:T(8,128)(2,1)S(1)} %get-tuple-element.45.refs_0_), channel_id=1, source_target_pairs={{0,2},{2,0},{4,6},{6,4},{1,3},{3,1},{5,7},{7,5},{8,10},{10,8},{12,... | collective-permute-start | bytes 196616 | tf_op jit(solution)/shard_map/ppermute | solution.py:666
  6.2 9.7 %collective-permute-start.2 = (bf16[4,64,128]{2,1,0:T(8,128)(2,1)S(1)}, bf16[4,64,128]{2,1,0:T(8,128)(2,1)S(1)}, u32[]{:S(2)}, u32[]{:S(2)}) collective-permute-start(bf16[4,64,128]{2,1,0:T(8,128)(2,1)S(1)} %get-tuple-element.45.refs_0_), channel_id=1, source_target_pairs={{0,4},{2,6},{4,0},{6,2},{1,5},{3,7},{5,1},{7,3},{8,12},{10,14},{12... | collective-permute-start | bytes 196616 | tf_op jit(solution)/shard_map/ppermute | solution.py:666
  8.8 7.1 %collective-permute-start.3 = (bf16[4,64,128]{2,1,0:T(8,128)(2,1)S(1)}, bf16[4,64,128]{2,1,0:T(8,128)(2,1)S(1)}, u32[]{:S(2)}, u32[]{:S(2)}) collective-permute-start(bf16[4,64,128]{2,1,0:T(8,128)(2,1)S(1)} %get-tuple-element.45.refs_0_), channel_id=1, source_target_pairs={{0,6},{2,4},{4,2},{6,0},{1,7},{3,5},{5,3},{7,1},{8,14},{10,12},{12... | collective-permute-start | bytes 196616 | tf_op jit(solution)/shard_map/ppermute | solution.py:666
  8.8 17.9 %collective-permute-start = (bf16[32,64,128]{2,1,0:T(8,128)(2,1)S(1)}, bf16[32,64,128]{2,1,0:T(8,128)(2,1)S(1)}, u32[]{:S(2)}, u32[]{:S(2)}) collective-permute-start(bf16[32,64,128]{2,1,0:T(8,128)(2,1)S(1)} %get-tuple-element.43.own_ref), channel_id=1, source_target_pairs={{0,1},{1,0},{2,3},{3,2},{4,5},{5,4},{6,7},{7,6},{8,9},{9,8},{10,11... | collective-permute-start | bytes 1572872 | tf_op jit(solution)/shard_map/ppermute | solution.py:668
  10.6 3.7 %copy-start.1 = (s32[4,2]{0,1:T(2,128)S(1)}, s32[4,2]{0,1:T(2,128)}, u32[]{:S(2)}) copy-start(s32[4,2]{0,1:T(2,128)} %param.14) | copy-start | bytes 100
  10.6 3.7 %copy-start.2 = (s32[2,2]{1,0:T(2,128)S(1)}, s32[2,2]{1,0:T(2,128)}, u32[]{:S(2)}) copy-start(s32[2,2]{1,0:T(2,128)} %mask_ref.1) | copy-start | bytes 52
  16.0 10.4 %collective-permute-start.4 = (bf16[2,4,64,128]{3,2,1,0:T(8,128)(2,1)S(1)}, bf16[2,4,64,128]{3,2,1,0:T(8,128)(2,1)S(1)}, u32[]{:S(2)}, u32[]{:S(2)}) collective-permute-start(bf16[2,4,64,128]{3,2,1,0:T(8,128)(2,1)S(1)} %shard_map.134.refs_4_), channel_id=1, source_target_pairs={{0,1},{1,0},{2,3},{3,2},{4,5},{5,4},{6,7},{7,6},{8,9},{9,8},{10,11... | collective-permute-start | bytes 393224 | tf_op jit(solution)/shard_map/ppermute | solution.py:700
  16.5 19.5 %collective-permute-start.5 = (bf16[32,64,128]{2,1,0:T(8,128)(2,1)S(1)}, bf16[32,64,128]{2,1,0:T(8,128)(2,1)S(1)}, u32[]{:S(2)}, u32[]{:S(2)}) collective-permute-start(bf16[32,64,128]{2,1,0:T(8,128)(2,1)S(1)} %get-tuple-element.64.own_ref), channel_id=1, source_target_pairs={{0,1},{1,0},{2,3},{3,2},{4,5},{5,4},{6,7},{7,6},{8,9},{9,8},{10,11... | collective-permute-start | bytes 1572872 | tf_op jit(solution)/shard_map/ppermute | solution.py:737
  29.0 2.4 %collective-permute-start.6 = (bf16[16,72,128]{2,1,0:T(8,128)(2,1)S(1)}, bf16[16,72,128]{2,1,0:T(8,128)(2,1)S(1)}, u32[]{:S(2)}, u32[]{:S(2)}) collective-permute-start(bf16[16,72,128]{2,1,0:T(8,128)(2,1)S(1)} %get-tuple-element.61.after_ref), channel_id=1, source_target_pairs={{0,8},{8,0},{16,24},{24,16},{1,9},{9,1},{17,25},{25,17},{2,10},{10... | collective-permute-start | bytes 884744 | tf_op jit(solution)/shard_map/ppermute | solution.py:777
  31.6 11.0 %collective-permute-start.7 = (bf16[16,72,128]{2,1,0:T(8,128)(2,1)S(1)}, bf16[16,72,128]{2,1,0:T(8,128)(2,1)S(1)}, u32[]{:S(2)}, u32[]{:S(2)}) collective-permute-start(bf16[16,72,128]{2,1,0:T(8,128)(2,1)S(1)} %shard_map.142.after_ref.own_ref), channel_id=1, source_target_pairs={{0,16},{8,24},{16,0},{24,8},{1,17},{9,25},{17,1},{25,9},{2,18},{10... | collective-permute-start | bytes 884744 | tf_op jit(solution)/shard_map/ppermute | solution.py:785
  38.2 2.6 %collective-permute-start.8 = (bf16[16,72,128]{2,1,0:T(8,128)(2,1)S(1)}, bf16[16,72,128]{2,1,0:T(8,128)(2,1)S(1)}, u32[]{:S(2)}, u32[]{:S(2)}) collective-permute-start(bf16[16,72,128]{2,1,0:T(8,128)(2,1)S(1)} %get-tuple-element.76.after_ref), channel_id=1, source_target_pairs={{0,8},{8,0},{16,24},{24,16},{1,9},{9,1},{17,25},{25,17},{2,10},{10... | collective-permute-start | bytes 884744 | tf_op jit(solution)/shard_map/ppermute | solution.py:777
  38.3 6.1 %copy-start = (bf16[64,128]{1,0:T(8,128)(2,1)S(1)}, bf16[64,128]{1,0:T(8,128)(2,1)}, u32[]{:S(2)}) copy-start(bf16[64,128]{1,0:T(8,128)(2,1)} %w_ref.3) | copy-start | bytes 49156
  41.1 9.5 %collective-permute-start.10 = (bf16[16,72,128]{2,1,0:T(8,128)(2,1)S(1)}, bf16[16,72,128]{2,1,0:T(8,128)(2,1)S(1)}, u32[]{:S(2)}, u32[]{:S(2)}) collective-permute-start(bf16[16,72,128]{2,1,0:T(8,128)(2,1)S(1)} %shard_map.146._.own_ref), channel_id=1, source_target_pairs={{0,16},{8,24},{16,0},{24,8},{1,17},{9,25},{17,1},{25,9},{2,18},{10... | collective-permute-start | bytes 884744 | tf_op jit(solution)/shard_map/ppermute | solution.py:785
  42.8 1.6 %collective-permute-start.9 = (bf16[16,64,128]{2,1,0:T(8,128)(2,1)S(1)}, bf16[16,64,128]{2,1,0:T(8,128)(2,1)S(1)}, u32[]{:S(2)}, u32[]{:S(2)}) collective-permute-start(bf16[16,64,128]{2,1,0:T(8,128)(2,1)S(1)} %shard_map.147.refs_5_), channel_id=1, source_target_pairs={{0,8},{8,0},{16,24},{24,16},{1,9},{9,1},{17,25},{25,17},{2,10},{10... | collective-permute-start | bytes 786440 | tf_op jit(solution)/shard_map/ppermute | solution.py:791
  50.7 1.8 %collective-permute-start.11 = (bf16[16,64,128]{2,1,0:T(8,128)(2,1)S(1)}, bf16[16,64,128]{2,1,0:T(8,128)(2,1)S(1)}, u32[]{:S(2)}, u32[]{:S(2)}) collective-permute-start(bf16[16,64,128]{2,1,0:T(8,128)(2,1)S(1)} %shard_map.149.merged_ref), channel_id=1, source_target_pairs={{0,8},{8,0},{16,24},{24,16},{1,9},{9,1},{17,25},{25,17},{2,10},{10... | collective-permute-start | bytes 786440 | tf_op jit(solution)/shard_map/ppermute | solution.py:791

commit v6 on v5

--- a/solution.py
+++ b/solution.py
@@ -563,8 +563,20 @@
         out_ref[i] = matmul(merged_ref[i], w_ref[...], 0, 0).astype(jnp.bfloat16)
 
 
-def embed_kernel(idx_ref, merged_ref, w_ref, prior_ref, out_ref):
-    embed_rows(merged_ref, w_ref, out_ref)
+def embed_kernel(piece, pieces, merged_ref, w_ref, prior_ref, out_hbm, rows_ref, done):
+    step_rows = merged_ref.shape[0]
+    groups = done.shape[0]
+    size = step_rows // groups
+    first = piece_of(piece, places(step_rows * pieces), pieces) * step_rows
+    copies = []
+    for group in range(groups):
+        span = pl.ds(group * size, size)
+        embed_rows(merged_ref.at[span], w_ref, rows_ref.at[span])
+        target = out_hbm.at[pl.ds(pl.multiple_of(first + group * size, size), size)]
+        copies.append(pltpu.make_async_copy(rows_ref.at[span], target, done.at[group]))
+        copies[-1].start()
+    for copy in copies:
+        copy.wait()
 
 
 def finish_kernel(idx_ref, *refs):
@@ -790,9 +802,6 @@
         )(table, pair_state, far_state, token)
         merged_other = lax.ppermute(merged, "tmpl", cores)
 
-        def at_piece(piece):
-            return lambda g, s: (piece_of(piece, s, pieces), 0, 0)
-
         if chunk == 0:
             out, emb, token = call(
                 finish_kernel,
@@ -813,14 +822,18 @@
             )(idx, *fresh, merged_other, merged, w_merge_out)
         else:
             for piece, part in ((2 * chunk + 1, merged), (2 * chunk, merged_other)):
-                emb = call(
-                    embed_kernel,
-                    (1,),
-                    [vmem, vmem, anywhere],
-                    pl.BlockSpec((piece_rows, cols, pair_ch), at_piece(piece)),
-                    emb_shape,
-                    aliases={3: 0},
-                )(idx, part, w_merge_out, emb)
+                emb = pl.pallas_call(
+                    functools.partial(embed_kernel, piece, pieces),
+                    in_specs=[vmem, vmem, hbm],
+                    out_specs=hbm,
+                    out_shape=emb_shape,
+                    scratch_shapes=[
+                        pltpu.VMEM((piece_rows, cols, pair_ch), bf16),
+                        pltpu.SemaphoreType.DMA((2,)),
+                    ],
+                    input_output_aliases={2: 0},
+                    compiler_params=pltpu.CompilerParams(vmem_limit_bytes=VMEM_GRANT),
+                )(part, w_merge_out, emb)
     return (jnp.swapaxes(out, 1, 2)[None], emb)
 
 

time: 54.4 us -> 53.8 us (0.989)
  Pallas kernels: 29.5 us -> 28.3 us
    pallas_call x2, Pallas kernels: 3.35 us -> 2.16 us  [fused_on_device(): pl.pallas_call(functools.partial(embed_kernel, piece, pieces), in_specs=[...]
  transfers between devices with their start and end apart: 12 -> 12, of which waited for: 4 -> 5; matrix products, arithmetic and copies ran while one was open for 0% -> 0% of each run, Pallas kernels for 47% -> 46%
where the time goes in v6:
time: 53.8 us; the launch traced here: 53.6 us
  Pallas kernels  28.3 us (53%)
  starting transfers between devices  13.4 us (25%)
  waiting for transfers between devices  10.7 us (20%)
  between operations  1.03 us (2%)
    pallas_call x4, Pallas kernels, fused_on_device(): plain_call(functools.partial(late_kernel, heads, side * piece_rows, piece...  9.37 us
    ppermute x3, starting transfers between devices, fused_on_device(): tiles.append(lax.ppermute(bias_tile, 'row', perm))  5.71 us
    pallas_call x4, Pallas kernels, near_part(): plain_call(functools.partial(near_kernel, heads, piece % 2 * piece_rows),...  4.46 us
    ppermute x1, waiting for transfers between devices, fused_on_device(): far_tiles = lax.ppermute(picked, 'col', swap)  4.41 us
    pallas_call x1, Pallas kernels, fused_on_device(): call(functools.partial(query_kernel, dim ** (-0.5)), (pieces,), [pl.Block...  3.65 us
    ppermute x2, starting transfers between devices, fused_on_device(): far_state = lax.ppermute(pair_state, 'tmpl', chips)  3.33 us
    ppermute x2, waiting for transfers between devices, fused_on_device(): far_state = lax.ppermute(pair_state, 'tmpl', chips)  3.11 us
    pallas_call x1, Pallas kernels, fused_on_device(): call(finish_kernel, (pieces,), [vmem] * (pieces + 3), [pl.BlockSpec((piec...  3.02 us
  transfers between devices with their start and end apart: 12, of which 5 were waited for; matrix products, arithmetic and copies ran while one was open for 0% of the time, Pallas kernels for 46%

profile of v6, /device:TPU:0, one launch (start us, length us, event | category | flops | bytes accessed | tf_op | source)
XLA Modules:
  0.0 53.6 jit_solution(18095868845308221224)
XLA Ops:
  0.6 2.5 %shard_map.131 = (bf16[32,64,128]{2,1,0:T(8,128)(2,1)S(1)}, bf16[32,64,128]{2,1,0:T(8,128)(2,1)S(1)}, bf16[32,64,128]{2,1,0:T(8,128)(2,1)S(1)}, bf16[32,64,128]{2,1,0:T(8,128)(2,1)S(1)}, bf16[4,64,128]{2,1,0:T(8,128)(2,1)S(1)}) custom-call(bf16[64,64,128]{2,1,0:T(8,128)(2,1)} %bitcast.17, f32[1,64]{1,0:T(1,128)} %bitcast.20, bf16[4,64]{1,0:T(4,128)(2,1)} %bitcast.19), custom_call_target="tpu_custom_call" | custom-call | flops 1000000 | bytes 1048576 | tf_op jit(solution)/shard_map/pallas_call | solution.py:658
  3.1 3.1 %collective-permute-start.1 = (bf16[4,64,128]{2,1,0:T(8,128)(2,1)S(1)}, bf16[4,64,128]{2,1,0:T(8,128)(2,1)S(1)}, u32[]{:S(2)}, u32[]{:S(2)}) collective-permute-start(bf16[4,64,128]{2,1,0:T(8,128)(2,1)S(1)} %get-tuple-element.45.refs_0_), channel_id=1, source_target_pairs={{0,2},{2,0},{4,6},{6,4},{1,3},{3,1},{5,7},{7,5},{8,10},{10,8},{12,... | collective-permute-start | bytes 196616 | tf_op jit(solution)/shard_map/ppermute | solution.py:678
  6.2 2.6 %collective-permute-start.2 = (bf16[4,64,128]{2,1,0:T(8,128)(2,1)S(1)}, bf16[4,64,128]{2,1,0:T(8,128)(2,1)S(1)}, u32[]{:S(2)}, u32[]{:S(2)}) collective-permute-start(bf16[4,64,128]{2,1,0:T(8,128)(2,1)S(1)} %get-tuple-element.45.refs_0_), channel_id=1, source_target_pairs={{0,4},{2,6},{4,0},{6,2},{1,5},{3,7},{5,1},{7,3},{8,12},{10,14},{12... | collective-permute-start | bytes 196616 | tf_op jit(solution)/shard_map/ppermute | solution.py:678
  8.8 0.0 collective-permute-start.3
  8.8 1.7 %collective-permute-start = (bf16[32,64,128]{2,1,0:T(8,128)(2,1)S(1)}, bf16[32,64,128]{2,1,0:T(8,128)(2,1)S(1)}, u32[]{:S(2)}, u32[]{:S(2)}) collective-permute-start(bf16[32,64,128]{2,1,0:T(8,128)(2,1)S(1)} %get-tuple-element.43.own_ref), channel_id=1, source_target_pairs={{0,1},{1,0},{2,3},{3,2},{4,5},{5,4},{6,7},{7,6},{8,9},{9,8},{10,11... | collective-permute-start | bytes 1572872 | tf_op jit(solution)/shard_map/ppermute | solution.py:680
  10.5 0.1 stack.23.idx_ref
  10.6 0.0 copy-start.1
  10.6 0.0 copy-start.2
  10.6 3.7 %shard_map.132.refs_5_.main_query = f32[64,64,128]{2,1,0:T(8,128)S(1)} custom-call(s32[5]{0:T(128)S(1)} %stack.23.idx_ref, bf16[64,128,128]{2,1,0:T(8,128)(2,1)} %main_ref.1, bf16[64,128]{1,0:T(8,128)(2,1)} %bitcast.18), custom_call_target="tpu_custom_call" | custom-call | flops 1000000 | bytes 1048576 | tf_op jit(solution)/shard_map/pallas_call | solution.py:697
  14.3 0.0 copy-done.1
  14.3 0.0 copy-done.2
  14.3 1.6 %shard_map.133 = (bf16[576,64]{1,0:T(8,128)(2,1)S(1)}, f32[64,128]{1,0:T(8,128)S(1)}, f32[8,128]{1,0:T(8,128)S(1)}) custom-call(s32[5]{0:T(128)S(1)} %stack.23.idx_ref, bf16[64,256]{1,0:T(8,128)(2,1)} %project_ref.1, bf16[64,64]{1,0:T(8,128)(2,1)} %tri_out_ref.1, bf16[64,128]{1,0:T(8,128)(2,1)} %kv_ref.1, f32[1,64]{1,0:T(1,128)} %bitcast.21, ...), custom_call_target="tpu_custom_call" | custom-call | flops 1000000 | bytes 1048576 | tf_op jit(solution)/shard_map/pallas_call | solution.py:688
  15.9 0.0 collective-permute-done.1.refs_1_
  15.9 0.0 collective-permute-done.2.refs_2_
  15.9 0.0 collective-permute-done.3.refs_3_
  15.9 0.1 shard_map.134.refs_4_
  16.0 0.5 collective-permute-start.4
  16.5 1.6 %collective-permute-start.5 = (bf16[32,64,128]{2,1,0:T(8,128)(2,1)S(1)}, bf16[32,64,128]{2,1,0:T(8,128)(2,1)S(1)}, u32[]{:S(2)}, u32[]{:S(2)}) collective-permute-start(bf16[32,64,128]{2,1,0:T(8,128)(2,1)S(1)} %get-tuple-element.64.own_ref), channel_id=1, source_target_pairs={{0,1},{1,0},{2,3},{3,2},{4,5},{5,4},{6,7},{7,6},{8,9},{9,8},{10,11... | collective-permute-start | bytes 1572872 | tf_op jit(solution)/shard_map/ppermute | solution.py:749
  18.1 0.6 %shard_map.135.own_bias_ref.after_ref = f32[4,128,128]{2,1,0:T(8,128)S(1)} custom-call(f32[8,128]{1,0:T(8,128)S(1)} %get-tuple-element.44.table_ref, bf16[4,64,128]{2,1,0:T(8,128)(2,1)S(1)} %get-tuple-element.45.refs_0_, bf16[4,64,128]{2,1,0:T(8,128)(2,1)S(1)} %collective-permute-done.1.refs_1_, bf16[4,64,128]{2,1,0:T(8,128)(2,1)S(1)} %collective-permute-done.2.refs_2_, ...), custom_call_target="tpu_custom_call" | custom-call | flops 1000000 | bytes 1048576 | tf_op jit(solution)/shard_map/pallas_call | solution.py:714
  18.6 1.1 %shard_map.136 = (bf16[16,4,64,128]{3,2,1,0:T(8,128)(2,1)S(1)}, f32[16,64,128]{2,1,0:T(8,128)S(1)}, bf16[16,64,128]{2,1,0:T(8,128)(2,1)S(1)}, f32[16,4,128,128]{3,2,1,0:T(8,128)S(1)}, f32[16,4,8,128]{3,2,1,0:T(8,128)S(1)}) custom-call(bf16[32,64,128]{2,1,0:T(8,128)(2,1)S(1)} %get-tuple-element.43.own_ref, ...), custom_call_target="tpu_custom_call" | custom-call | flops 2000000000 | bytes 1048576 | tf_op jit(solution)/shard_map/pallas_call | solution.py:733
  19.8 1.1 %shard_map.137 = (bf16[16,4,64,128]{3,2,1,0:T(8,128)(2,1)S(1)}, f32[16,64,128]{2,1,0:T(8,128)S(1)}, bf16[16,64,128]{2,1,0:T(8,128)(2,1)S(1)}, f32[16,4,128,128]{3,2,1,0:T(8,128)S(1)}, f32[16,4,8,128]{3,2,1,0:T(8,128)S(1)}) custom-call(bf16[32,64,128]{2,1,0:T(8,128)(2,1)S(1)} %get-tuple-element.43.own_ref, ...), custom_call_target="tpu_custom_call" | custom-call | flops 2000000000 | bytes 1048576 | tf_op jit(solution)/shard_map/pallas_call | solution.py:733
  20.9 1.1 %shard_map.138 = (bf16[16,4,64,128]{3,2,1,0:T(8,128)(2,1)S(1)}, f32[16,64,128]{2,1,0:T(8,128)S(1)}, bf16[16,64,128]{2,1,0:T(8,128)(2,1)S(1)}, f32[16,4,128,128]{3,2,1,0:T(8,128)S(1)}, f32[16,4,8,128]{3,2,1,0:T(8,128)S(1)}) custom-call(bf16[32,64,128]{2,1,0:T(8,128)(2,1)S(1)} %get-tuple-element.64.own_ref, ...), custom_call_target="tpu_custom_call" | custom-call | flops 2000000000 | bytes 1048576 | tf_op jit(solution)/shard_map/pallas_call | solution.py:733
  22.0 4.4 %collective-permute-done.4.tiles_ref = bf16[2,4,64,128]{3,2,1,0:T(8,128)(2,1)S(1)} collective-permute-done((bf16[2,4,64,128]{3,2,1,0:T(8,128)(2,1)S(1)}, bf16[2,4,64,128]{3,2,1,0:T(8,128)(2,1)S(1)}, u32[]{:S(2)}, u32[]{:S(2)}) %collective-permute-start.4) | collective-permute-done | bytes 131104 | tf_op jit(solution)/shard_map/ppermute | solution.py:712
  26.4 0.3 shard_map.139.far_bias_ref.after_ref
  26.7 0.0 collective-permute-done.far_ref
  26.7 2.3 %shard_map.140 = (bf16[16,64,128]{2,1,0:T(8,128)(2,1)S(1)}, bf16[16,72,128]{2,1,0:T(8,128)(2,1)S(1)}) custom-call(bf16[32,64,128]{2,1,0:T(8,128)(2,1)S(1)} %get-tuple-element.42.x_ref, bf16[32,64,128]{2,1,0:T(8,128)(2,1)S(1)} %collective-permute-done.far_ref, f32[64,64,128]{2,1,0:T(8,128)S(1)} %shard_map.132.refs_5_.main_query, ...), custom_call_target="tpu_custom_call" | custom-call | flops 6000000000 | bytes 1048576 | tf_op jit(solution)/shard_map/pallas_call | solution.py:760
  29.0 0.1 collective-permute-start.6
  29.1 2.3 %shard_map.141 = (bf16[16,64,128]{2,1,0:T(8,128)(2,1)S(1)}, bf16[16,72,128]{2,1,0:T(8,128)(2,1)S(1)}) custom-call(bf16[32,64,128]{2,1,0:T(8,128)(2,1)S(1)} %get-tuple-element.42.x_ref, bf16[32,64,128]{2,1,0:T(8,128)(2,1)S(1)} %collective-permute-done.far_ref, f32[64,64,128]{2,1,0:T(8,128)S(1)} %shard_map.132.refs_5_.main_query, ...), custom_call_target="tpu_custom_call" | custom-call | flops 6000000000 | bytes 1048576 | tf_op jit(solution)/shard_map/pallas_call | solution.py:760
  31.4 0.0 collective-permute-done.6.other_ref
  31.4 0.2 shard_map.142.after_ref.own_ref
  31.6 1.8 %collective-permute-start.7 = (bf16[16,72,128]{2,1,0:T(8,128)(2,1)S(1)}, bf16[16,72,128]{2,1,0:T(8,128)(2,1)S(1)}, u32[]{:S(2)}, u32[]{:S(2)}) collective-permute-start(bf16[16,72,128]{2,1,0:T(8,128)(2,1)S(1)} %shard_map.142.after_ref.own_ref), channel_id=1, source_target_pairs={{0,16},{8,24},{16,0},{24,8},{1,17},{9,25},{17,1},{25,9},{2,18},{10... | collective-permute-start | bytes 884744 | tf_op jit(solution)/shard_map/ppermute | solution.py:797
  33.4 1.1 %shard_map.143 = (bf16[16,4,64,128]{3,2,1,0:T(8,128)(2,1)S(1)}, f32[16,64,128]{2,1,0:T(8,128)S(1)}, bf16[16,64,128]{2,1,0:T(8,128)(2,1)S(1)}, f32[16,4,128,128]{3,2,1,0:T(8,128)S(1)}, f32[16,4,8,128]{3,2,1,0:T(8,128)S(1)}) custom-call(bf16[32,64,128]{2,1,0:T(8,128)(2,1)S(1)} %get-tuple-element.64.own_ref, ...), custom_call_target="tpu_custom_call" | custom-call | flops 2000000000 | bytes 1048576 | tf_op jit(solution)/shard_map/pallas_call | solution.py:733
  34.5 1.4 %collective-permute-done.5.far_ref = bf16[32,64,128]{2,1,0:T(8,128)(2,1)S(1)} collective-permute-done((bf16[32,64,128]{2,1,0:T(8,128)(2,1)S(1)}, bf16[32,64,128]{2,1,0:T(8,128)(2,1)S(1)}, u32[]{:S(2)}, u32[]{:S(2)}) %collective-permute-start.5) | collective-permute-done | bytes 524320 | tf_op jit(solution)/shard_map/ppermute | solution.py:749
  36.0 2.3 %shard_map.144 = (bf16[16,64,128]{2,1,0:T(8,128)(2,1)S(1)}, bf16[16,72,128]{2,1,0:T(8,128)(2,1)S(1)}) custom-call(bf16[32,64,128]{2,1,0:T(8,128)(2,1)S(1)} %get-tuple-element.63.x_ref, bf16[32,64,128]{2,1,0:T(8,128)(2,1)S(1)} %collective-permute-done.5.far_ref, f32[64,64,128]{2,1,0:T(8,128)S(1)} %shard_map.132.refs_5_.main_query, ...), custom_call_target="tpu_custom_call" | custom-call | flops 6000000000 | bytes 1048576 | tf_op jit(solution)/shard_map/pallas_call | solution.py:760
  38.2 0.1 collective-permute-start.8
  38.3 0.0 copy-start
  38.3 2.5 %shard_map.145 = (bf16[16,64,128]{2,1,0:T(8,128)(2,1)S(1)}, bf16[16,72,128]{2,1,0:T(8,128)(2,1)S(1)}) custom-call(bf16[32,64,128]{2,1,0:T(8,128)(2,1)S(1)} %get-tuple-element.63.x_ref, bf16[32,64,128]{2,1,0:T(8,128)(2,1)S(1)} %collective-permute-done.5.far_ref, f32[64,64,128]{2,1,0:T(8,128)S(1)} %shard_map.132.refs_5_.main_query, ...), custom_call_target="tpu_custom_call" | custom-call | flops 6000000000 | bytes 1048576 | tf_op jit(solution)/shard_map/pallas_call | solution.py:760
  40.8 0.0 collective-permute-done.8.other_ref
  40.9 0.2 shard_map.146._.own_ref
  41.1 1.6 %collective-permute-start.10 = (bf16[16,72,128]{2,1,0:T(8,128)(2,1)S(1)}, bf16[16,72,128]{2,1,0:T(8,128)(2,1)S(1)}, u32[]{:S(2)}, u32[]{:S(2)}) collective-permute-start(bf16[16,72,128]{2,1,0:T(8,128)(2,1)S(1)} %shard_map.146._.own_ref), channel_id=1, source_target_pairs={{0,16},{8,24},{16,0},{24,8},{1,17},{9,25},{17,1},{25,9},{2,18},{10... | collective-permute-start | bytes 884744 | tf_op jit(solution)/shard_map/ppermute | solution.py:797
  42.6 0.0 collective-permute-done.7.other_ref
  42.6 0.2 shard_map.147.refs_5_
  42.8 0.3 collective-permute-start.9
  43.1 1.3 %collective-permute-done.9.refs_4_ = bf16[16,64,128]{2,1,0:T(8,128)(2,1)S(1)} collective-permute-done((bf16[16,64,128]{2,1,0:T(8,128)(2,1)S(1)}, bf16[16,64,128]{2,1,0:T(8,128)(2,1)S(1)}, u32[]{:S(2)}, u32[]{:S(2)}) %collective-permute-start.9) | collective-permute-done | bytes 262176 | tf_op jit(solution)/shard_map/ppermute | solution.py:803
  44.4 0.0 copy-done
  44.4 3.0 %shard_map.148 = (bf16[64,64,128]{2,1,0:T(8,128)(2,1)}, bf16[64,128,128]{2,1,0:T(8,128)(2,1)}, f32[8,128]{1,0:T(8,128)S(1)}) custom-call(s32[5]{0:T(128)S(1)} %stack.23.idx_ref, bf16[16,64,128]{2,1,0:T(8,128)(2,1)S(1)} %get-tuple-element.56.refs_0_, bf16[16,64,128]{2,1,0:T(8,128)(2,1)S(1)} %get-tuple-element.62.refs_1_, ...), custom_call_target="tpu_custom_call" | custom-call | flops 1000000 | bytes 1048576 | tf_op jit(solution)/shard_map/pallas_call | solution.py:806
  47.4 3.1 %collective-permute-done.10.other_ref = bf16[16,72,128]{2,1,0:T(8,128)(2,1)S(1)} collective-permute-done((bf16[16,72,128]{2,1,0:T(8,128)(2,1)S(1)}, bf16[16,72,128]{2,1,0:T(8,128)(2,1)S(1)}, u32[]{:S(2)}, u32[]{:S(2)}) %collective-permute-start.10) | collective-permute-done | bytes 294944 | tf_op jit(solution)/shard_map/ppermute | solution.py:797
  50.5 0.2 shard_map.149.merged_ref
  50.7 0.1 collective-permute-start.11
  50.8 1.1 %shard_map.150.prior_ref = bf16[64,128,128]{2,1,0:T(8,128)(2,1)} custom-call(bf16[16,64,128]{2,1,0:T(8,128)(2,1)S(1)} %shard_map.149.merged_ref, bf16[64,128]{1,0:T(8,128)(2,1)S(1)} %copy-done, bf16[64,128,128]{2,1,0:T(8,128)(2,1)} %get-tuple-element.81.prior_ref), custom_call_target="tpu_custom_call", output_to_operand_aliasing={{}: (2, {})} | custom-call | tf_op jit(solution)/shard_map/pallas_call | solution.py:825
  51.9 0.4 collective-permute-done.11.merged_ref
  52.3 1.1 %shard_map.151 = bf16[64,128,128]{2,1,0:T(8,128)(2,1)} custom-call(bf16[16,64,128]{2,1,0:T(8,128)(2,1)S(1)} %collective-permute-done.11.merged_ref, bf16[64,128]{1,0:T(8,128)(2,1)S(1)} %copy-done, bf16[64,128,128]{2,1,0:T(8,128)(2,1)} %shard_map.150.prior_ref), custom_call_target="tpu_custom_call", output_to_operand_aliasing={{}: (2, {})} | custom-call | tf_op jit(solution)/shard_map/pallas_call | solution.py:825
Async XLA Ops:
  3.1 12.8 %collective-permute-start.1 = (bf16[4,64,128]{2,1,0:T(8,128)(2,1)S(1)}, bf16[4,64,128]{2,1,0:T(8,128)(2,1)S(1)}, u32[]{:S(2)}, u32[]{:S(2)}) collective-permute-start(bf16[4,64,128]{2,1,0:T(8,128)(2,1)S(1)} %get-tuple-element.45.refs_0_), channel_id=1, source_target_pairs={{0,2},{2,0},{4,6},{6,4},{1,3},{3,1},{5,7},{7,5},{8,10},{10,8},{12,... | collective-permute-start | bytes 196616 | tf_op jit(solution)/shard_map/ppermute | solution.py:678
  6.2 9.7 %collective-permute-start.2 = (bf16[4,64,128]{2,1,0:T(8,128)(2,1)S(1)}, bf16[4,64,128]{2,1,0:T(8,128)(2,1)S(1)}, u32[]{:S(2)}, u32[]{:S(2)}) collective-permute-start(bf16[4,64,128]{2,1,0:T(8,128)(2,1)S(1)} %get-tuple-element.45.refs_0_), channel_id=1, source_target_pairs={{0,4},{2,6},{4,0},{6,2},{1,5},{3,7},{5,1},{7,3},{8,12},{10,14},{12... | collective-permute-start | bytes 196616 | tf_op jit(solution)/shard_map/ppermute | solution.py:678
  8.8 7.1 %collective-permute-start.3 = (bf16[4,64,128]{2,1,0:T(8,128)(2,1)S(1)}, bf16[4,64,128]{2,1,0:T(8,128)(2,1)S(1)}, u32[]{:S(2)}, u32[]{:S(2)}) collective-permute-start(bf16[4,64,128]{2,1,0:T(8,128)(2,1)S(1)} %get-tuple-element.45.refs_0_), channel_id=1, source_target_pairs={{0,6},{2,4},{4,2},{6,0},{1,7},{3,5},{5,3},{7,1},{8,14},{10,12},{12... | collective-permute-start | bytes 196616 | tf_op jit(solution)/shard_map/ppermute | solution.py:678
  8.8 17.9 %collective-permute-start = (bf16[32,64,128]{2,1,0:T(8,128)(2,1)S(1)}, bf16[32,64,128]{2,1,0:T(8,128)(2,1)S(1)}, u32[]{:S(2)}, u32[]{:S(2)}) collective-permute-start(bf16[32,64,128]{2,1,0:T(8,128)(2,1)S(1)} %get-tuple-element.43.own_ref), channel_id=1, source_target_pairs={{0,1},{1,0},{2,3},{3,2},{4,5},{5,4},{6,7},{7,6},{8,9},{9,8},{10,11... | collective-permute-start | bytes 1572872 | tf_op jit(solution)/shard_map/ppermute | solution.py:680
  10.6 3.7 %copy-start.1 = (s32[4,2]{0,1:T(2,128)S(1)}, s32[4,2]{0,1:T(2,128)}, u32[]{:S(2)}) copy-start(s32[4,2]{0,1:T(2,128)} %param.14) | copy-start | bytes 100
  10.6 3.7 %copy-start.2 = (s32[2,2]{1,0:T(2,128)S(1)}, s32[2,2]{1,0:T(2,128)}, u32[]{:S(2)}) copy-start(s32[2,2]{1,0:T(2,128)} %mask_ref.1) | copy-start | bytes 52
  16.0 10.4 %collective-permute-start.4 = (bf16[2,4,64,128]{3,2,1,0:T(8,128)(2,1)S(1)}, bf16[2,4,64,128]{3,2,1,0:T(8,128)(2,1)S(1)}, u32[]{:S(2)}, u32[]{:S(2)}) collective-permute-start(bf16[2,4,64,128]{3,2,1,0:T(8,128)(2,1)S(1)} %shard_map.134.refs_4_), channel_id=1, source_target_pairs={{0,1},{1,0},{2,3},{3,2},{4,5},{5,4},{6,7},{7,6},{8,9},{9,8},{10,11... | collective-permute-start | bytes 393224 | tf_op jit(solution)/shard_map/ppermute | solution.py:712
  16.5 19.5 %collective-permute-start.5 = (bf16[32,64,128]{2,1,0:T(8,128)(2,1)S(1)}, bf16[32,64,128]{2,1,0:T(8,128)(2,1)S(1)}, u32[]{:S(2)}, u32[]{:S(2)}) collective-permute-start(bf16[32,64,128]{2,1,0:T(8,128)(2,1)S(1)} %get-tuple-element.64.own_ref), channel_id=1, source_target_pairs={{0,1},{1,0},{2,3},{3,2},{4,5},{5,4},{6,7},{7,6},{8,9},{9,8},{10,11... | collective-permute-start | bytes 1572872 | tf_op jit(solution)/shard_map/ppermute | solution.py:749
  29.0 2.4 %collective-permute-start.6 = (bf16[16,72,128]{2,1,0:T(8,128)(2,1)S(1)}, bf16[16,72,128]{2,1,0:T(8,128)(2,1)S(1)}, u32[]{:S(2)}, u32[]{:S(2)}) collective-permute-start(bf16[16,72,128]{2,1,0:T(8,128)(2,1)S(1)} %get-tuple-element.61.after_ref), channel_id=1, source_target_pairs={{0,8},{8,0},{16,24},{24,16},{1,9},{9,1},{17,25},{25,17},{2,10},{10... | collective-permute-start | bytes 884744 | tf_op jit(solution)/shard_map/ppermute | solution.py:789
  31.6 11.0 %collective-permute-start.7 = (bf16[16,72,128]{2,1,0:T(8,128)(2,1)S(1)}, bf16[16,72,128]{2,1,0:T(8,128)(2,1)S(1)}, u32[]{:S(2)}, u32[]{:S(2)}) collective-permute-start(bf16[16,72,128]{2,1,0:T(8,128)(2,1)S(1)} %shard_map.142.after_ref.own_ref), channel_id=1, source_target_pairs={{0,16},{8,24},{16,0},{24,8},{1,17},{9,25},{17,1},{25,9},{2,18},{10... | collective-permute-start | bytes 884744 | tf_op jit(solution)/shard_map/ppermute | solution.py:797
  38.2 2.6 %collective-permute-start.8 = (bf16[16,72,128]{2,1,0:T(8,128)(2,1)S(1)}, bf16[16,72,128]{2,1,0:T(8,128)(2,1)S(1)}, u32[]{:S(2)}, u32[]{:S(2)}) collective-permute-start(bf16[16,72,128]{2,1,0:T(8,128)(2,1)S(1)} %get-tuple-element.76.after_ref), channel_id=1, source_target_pairs={{0,8},{8,0},{16,24},{24,16},{1,9},{9,1},{17,25},{25,17},{2,10},{10... | collective-permute-start | bytes 884744 | tf_op jit(solution)/shard_map/ppermute | solution.py:789
  38.3 6.1 %copy-start = (bf16[64,128]{1,0:T(8,128)(2,1)S(1)}, bf16[64,128]{1,0:T(8,128)(2,1)}, u32[]{:S(2)}) copy-start(bf16[64,128]{1,0:T(8,128)(2,1)} %w_ref.3) | copy-start | bytes 49156
  41.1 9.5 %collective-permute-start.10 = (bf16[16,72,128]{2,1,0:T(8,128)(2,1)S(1)}, bf16[16,72,128]{2,1,0:T(8,128)(2,1)S(1)}, u32[]{:S(2)}, u32[]{:S(2)}) collective-permute-start(bf16[16,72,128]{2,1,0:T(8,128)(2,1)S(1)} %shard_map.146._.own_ref), channel_id=1, source_target_pairs={{0,16},{8,24},{16,0},{24,8},{1,17},{9,25},{17,1},{25,9},{2,18},{10... | collective-permute-start | bytes 884744 | tf_op jit(solution)/shard_map/ppermute | solution.py:797
  42.8 1.6 %collective-permute-start.9 = (bf16[16,64,128]{2,1,0:T(8,128)(2,1)S(1)}, bf16[16,64,128]{2,1,0:T(8,128)(2,1)S(1)}, u32[]{:S(2)}, u32[]{:S(2)}) collective-permute-start(bf16[16,64,128]{2,1,0:T(8,128)(2,1)S(1)} %shard_map.147.refs_5_), channel_id=1, source_target_pairs={{0,8},{8,0},{16,24},{24,16},{1,9},{9,1},{17,25},{25,17},{2,10},{10... | collective-permute-start | bytes 786440 | tf_op jit(solution)/shard_map/ppermute | solution.py:803
  50.7 1.6 %collective-permute-start.11 = (bf16[16,64,128]{2,1,0:T(8,128)(2,1)S(1)}, bf16[16,64,128]{2,1,0:T(8,128)(2,1)S(1)}, u32[]{:S(2)}, u32[]{:S(2)}) collective-permute-start(bf16[16,64,128]{2,1,0:T(8,128)(2,1)S(1)} %shard_map.149.merged_ref), channel_id=1, source_target_pairs={{0,8},{8,0},{16,24},{24,16},{1,9},{9,1},{17,25},{25,17},{2,10},{10... | collective-permute-start | bytes 786440 | tf_op jit(solution)/shard_map/ppermute | solution.py:803
